TPU v7x, 32 devices: a whole 2x2x4 slice. The times are simulated.
32 devices in a mesh: replica: 4 (over x, core), shard: 8 (over z, y).
Axes of the slice: x: 2, y: 2, z: 4, core: 2. Of those that a mesh axis runs over, the one named last changes fastest.
Arguments:
- tokens: bfloat16 [4, 2048, 2048], P('replica', 'shard'), may hold values from -6 to 6
- cotangent: bfloat16 [4, 2048, 2048], P('replica', 'shard'), may hold values from -6 to 6
- lengths: int32 [4], replicated, may hold values from 1024 to 2048, as said below
- attn_gain: bfloat16 [2048], P('shard'), may hold values from 0.5 to 1.5
- query_down: bfloat16 [2048, 1024], P('shard'), may hold values from -0.125 to 0.125
- key_value: bfloat16 [2048, 512], P('shard'), may hold values from -0.125 to 0.125
- query_gain: bfloat16 [1024], P('shard'), may hold values from 0.5 to 1.5
- query_up: bfloat16 [1024, 4096], P('shard'), may hold values from -0.1875 to 0.1875
- out_proj: bfloat16 [4096, 2048], P('shard'), may hold values from -0.75 to 0.75
- mlp_gain: bfloat16 [2048], P('shard'), may hold values from 0.5 to 1.5
- gate_up: bfloat16 [2048, 11264], P('shard'), may hold values from -0.125 to 0.125
- down_proj: bfloat16 [5632, 2048], P('shard'), may hold values from -0.078125 to 0.078125
Outputs:
- layer_out: bfloat16 [4, 2048, 2048], P('replica', 'shard')
- input_grad: bfloat16 [4, 2048, 2048], P('replica', 'shard')
- grad_attn_gain: float32 [2048], P('shard')
- grad_query_down: float32 [2048, 1024], P('shard')
- grad_key_value: float32 [2048, 512], P('shard')
- grad_query_gain: float32 [1024], P('shard')
- grad_query_up: float32 [1024, 4096], P('shard')
- grad_out_proj: float32 [4096, 2048], P('shard')
- grad_mlp_gain: float32 [2048], P('shard')
- grad_gate_up: float32 [2048, 11264], P('shard')
- grad_down_proj: float32 [5632, 2048], P('shard')
Inputs may be any that keep to these rules, and one draw needn't show every extreme that they name: `lengths`: real tokens of each sequence, the rest of its slot is padding; some sequence has exactly 2048.
All inputs are finite; a program needn't handle non-finite values.
Results may differ from a plain program's by a relative error of at most 0.022.
Values may be sent and summed in bfloat16 or wider, within the bound.
No kernel may reach another device: no remote copies, remote signals or barrier semaphores. Data moves between devices by JAX's collectives and lax.ppermute only.
A program may use at most 448 MiB of HBM per device.

v0:
```python
import math

import jax
import jax.numpy as jnp
from jax import lax
from jax.sharding import PartitionSpec as P

HEADS = 16
HD = 256
FF = 5632


EPSILON = 1e-06


def inv_rms(values):
    return lax.rsqrt(jnp.mean(values * values, axis=-1, keepdims=True) + EPSILON)


def rope_tables(positions, head_dim):
    half_dim = head_dim // 2
    frequency = jnp.exp(-math.log(10000.0) * jnp.arange(half_dim).astype(jnp.float32) / half_dim)
    angles = positions.astype(jnp.float32)[:, None] * frequency[None, :]
    return (jnp.cos(angles), jnp.sin(angles))


def rotate(values, cosine, sine):
    half_dim = values.shape[-1] // 2
    first_half = values[..., :half_dim]
    second_half = values[..., half_dim:]
    return jnp.concatenate(
        [first_half * cosine - second_half * sine, second_half * cosine + first_half * sine],
        axis=-1,
    )


def rotate_back(grads, cosine, sine):
    half_dim = grads.shape[-1] // 2
    first_half = grads[..., :half_dim]
    second_half = grads[..., half_dim:]
    return jnp.concatenate(
        [first_half * cosine + second_half * sine, second_half * cosine - first_half * sine],
        axis=-1,
    )


def deal_slots(lengths, groups, per_group):
    order = jnp.argsort(-lengths, stable=True)
    ranking = jnp.argsort(order, stable=True)
    turn_id = ranking // groups
    column = ranking % groups
    group_id = jnp.where(turn_id % 2 == 0, column, groups - 1 - column)
    return group_id * per_group + turn_id


def contract_rows(left, right):
    return lax.dot_general(
        left, right, (((0,), (0,)), ((), ())), preferred_element_type=jnp.float32
    )


def contract_cols(left, right):
    return lax.dot_general(
        left, right, (((1,), (1,)), ((), ())), preferred_element_type=jnp.float32
    )


def masked_scores(query_block, key_block, allowed, scale):
    rows_here = allowed.shape[0]
    heads_here = query_block.shape[0] // rows_here
    raw_scores = contract_cols(query_block, key_block) * scale
    raw_scores = raw_scores.reshape(rows_here, heads_here, key_block.shape[0])
    return jnp.where(allowed[:, None, :], raw_scores, -1e30)


def attend(query_block, key_block, value_block, allowed, scale):
    scores = masked_scores(query_block, key_block, allowed, scale)
    peak = jnp.max(scores, axis=-1, keepdims=True)
    expo = jnp.exp(scores - peak)
    total = jnp.sum(expo, axis=-1, keepdims=True)
    probs_low = (
        (expo / total).astype(jnp.bfloat16).reshape(query_block.shape[0], key_block.shape[0])
    )
    attn_val = jnp.dot(probs_low, value_block, preferred_element_type=jnp.float32)
    return (attn_val, peak + jnp.log(total))


def attend_back(query_block, key_block, value_block, allowed, logsum, out_grad, scale):
    scores = masked_scores(query_block, key_block, allowed, scale)
    probs = jnp.exp(scores - logsum)
    key_count = key_block.shape[0]
    probs_low = probs.astype(jnp.bfloat16).reshape(query_block.shape[0], key_count)
    prob_grad = contract_cols(out_grad, value_block).reshape(probs.shape)
    delta = jnp.sum(probs * prob_grad, axis=-1, keepdims=True)
    score_grad = (
        (probs * (prob_grad - delta)).astype(jnp.bfloat16).reshape(query_block.shape[0], key_count)
    )
    query_grad = jnp.dot(score_grad, key_block, preferred_element_type=jnp.float32) * scale
    key_term = contract_rows(score_grad, query_block) * scale
    value_term = contract_rows(probs_low, out_grad)
    return (query_grad, jnp.concatenate([key_term, value_term], axis=1))


def on_device(
    tokens,
    cotangent,
    lengths,
    attn_gain,
    query_down,
    key_value,
    query_gain,
    query_up,
    out_proj,
    mlp_gain,
    gate_up,
    down_proj,
):
    n_replica = lax.axis_size("replica")
    n_shard = lax.axis_size("shard")
    per_group, piece_rows, width = tokens.shape
    slot_len = piece_rows * n_shard
    row_count = per_group * piece_rows
    scale = 1.0 / math.sqrt(HD)
    target = deal_slots(lengths, n_replica, per_group)
    source = jnp.argsort(target)
    replica_id = lax.axis_index("replica")
    shard_id = lax.axis_index("shard")
    my_source = lax.dynamic_slice_in_dim(source, replica_id * per_group, per_group)
    my_target = lax.dynamic_slice_in_dim(target, replica_id * per_group, per_group)
    all_tokens, all_cotangent = (
        lax.all_gather(tokens, "replica", axis=0, tiled=True),
        lax.all_gather(cotangent, "replica", axis=0, tiled=True),
    )
    local_tokens = jnp.take(all_tokens, my_source, axis=0)
    local_cot = jnp.take(all_cotangent, my_source, axis=0)
    my_lengths = jnp.take(lengths, my_source)
    positions = shard_id * piece_rows + jnp.arange(piece_rows, dtype=jnp.int32)
    valid = (positions[None, :] < my_lengths[:, None]).astype(jnp.float32).reshape(row_count, 1)
    cosine, sine = rope_tables(jnp.tile(positions, per_group), HD)
    key_pos = jnp.arange(slot_len, dtype=jnp.int32)
    x_rows = local_tokens.reshape(row_count, width).astype(jnp.float32)
    rms_first = inv_rms(x_rows)
    normed_first = x_rows * rms_first
    cot_rows = local_cot.reshape(row_count, width).astype(jnp.float32) * valid
    cot_low = cot_rows.astype(jnp.bfloat16)
    first_gain, qdown_mat, kv_mat, query_norm, qup_mat, out_mat = (
        lax.all_gather(attn_gain, "shard", axis=0, tiled=True),
        lax.all_gather(query_down, "shard", axis=0, tiled=True),
        lax.all_gather(key_value, "shard", axis=0, tiled=True),
        lax.all_gather(query_gain, "shard", axis=0, tiled=True),
        lax.all_gather(query_up, "shard", axis=0, tiled=True),
        lax.all_gather(out_proj, "shard", axis=0, tiled=True),
    )
    second_gain, gateup_mat, down_mat = (
        lax.all_gather(mlp_gain, "shard", axis=0, tiled=True),
        lax.all_gather(gate_up, "shard", axis=0, tiled=True),
        lax.all_gather(down_proj, "shard", axis=0, tiled=True),
    )
    cos_heads = cosine[:, None, :]
    sin_heads = sine[:, None, :]
    attn_input = (normed_first * first_gain.astype(jnp.float32)).astype(jnp.bfloat16)
    qdown_out = jnp.dot(attn_input, qdown_mat, preferred_element_type=jnp.float32)
    kv_out = jnp.dot(attn_input, kv_mat, preferred_element_type=jnp.float32)
    rms_query = inv_rms(qdown_out)
    normed_query = qdown_out * rms_query
    query_input = (normed_query * query_norm.astype(jnp.float32)).astype(jnp.bfloat16)
    query_raw = jnp.dot(query_input, qup_mat, preferred_element_type=jnp.float32)
    query_rot = rotate(query_raw.reshape(row_count, HEADS, HD), cos_heads, sin_heads).astype(
        jnp.bfloat16
    )
    key_rot = rotate(kv_out[:, :HD], cosine, sine).astype(jnp.bfloat16)
    value_part = kv_out[:, HD:].astype(jnp.bfloat16)
    kv_local = jnp.concatenate([key_rot, value_part], axis=1).reshape(per_group, piece_rows, 2 * HD)
    kv_whole = lax.all_gather(kv_local, "shard", axis=1, tiled=True)
    query_slots = query_rot.reshape(per_group, piece_rows * HEADS, HD)
    slot_id = 0
    allowed = (key_pos[None, :] <= positions[:, None]) & (key_pos[None, :] < my_lengths[slot_id])
    mask_blocks = [allowed]
    attn_val, logsum = attend(
        query_slots[slot_id], kv_whole[slot_id, :, :HD], kv_whole[slot_id, :, HD:], allowed, scale
    )
    logsum_blocks = [logsum]
    attn_blocks = attn_val.reshape(piece_rows, HEADS * HD)
    attn_low = attn_blocks.astype(jnp.bfloat16)
    middle = x_rows + jnp.dot(attn_low, out_mat, preferred_element_type=jnp.float32)
    rms_second = inv_rms(middle)
    normed_second = middle * rms_second
    mlp_input = (normed_second * second_gain.astype(jnp.float32)).astype(jnp.bfloat16)
    gateup_out = jnp.dot(mlp_input, gateup_mat, preferred_element_type=jnp.float32)
    gate_part = gateup_out[:, :FF]
    up_part = gateup_out[:, FF:]
    sigmoid_gate = jax.nn.sigmoid(gate_part)
    activated = gate_part * sigmoid_gate
    hidden_low = (activated * up_part).astype(jnp.bfloat16)
    layer = (middle + jnp.dot(hidden_low, down_mat, preferred_element_type=jnp.float32)) * valid
    down_grad = lax.psum_scatter(
        contract_rows(hidden_low, cot_low).astype(jnp.bfloat16),
        "shard",
        scatter_dimension=0,
        tiled=True,
    ).astype(jnp.float32)
    hidden_grad = contract_cols(cot_low, down_mat)
    gate_grad = hidden_grad * up_part * (sigmoid_gate * (1.0 + gate_part * (1.0 - sigmoid_gate)))
    up_grad = hidden_grad * activated
    gateup_grad_low = jnp.concatenate([gate_grad, up_grad], axis=1).astype(jnp.bfloat16)
    gateup_grad = lax.psum_scatter(
        contract_rows(mlp_input, gateup_grad_low).astype(jnp.bfloat16),
        "shard",
        scatter_dimension=0,
        tiled=True,
    ).astype(jnp.float32)
    mlp_in_grad = contract_cols(gateup_grad_low, gateup_mat)
    second_gain_term = jnp.sum(mlp_in_grad * normed_second, axis=0)
    second_normed_grad = mlp_in_grad * second_gain.astype(jnp.float32)
    middle_grad = cot_rows + rms_second * (
        second_normed_grad
        - normed_second * jnp.mean(second_normed_grad * normed_second, axis=-1, keepdims=True)
    )
    middle_low = middle_grad.astype(jnp.bfloat16)
    out_term = contract_rows(attn_low, middle_low)
    attn_val_grad = contract_cols(middle_low, out_mat).astype(jnp.bfloat16)
    grad_slots = attn_val_grad.reshape(per_group, piece_rows * HEADS, HD)
    slot_id = 0
    query_grad, kv_term = attend_back(
        query_slots[slot_id],
        kv_whole[slot_id, :, :HD],
        kv_whole[slot_id, :, HD:],
        mask_blocks[slot_id],
        logsum_blocks[slot_id],
        grad_slots[slot_id],
        scale,
    )
    kv_terms = [kv_term]
    kv_grad = (
        lax.psum_scatter(
            jnp.stack(kv_terms, axis=0).astype(jnp.bfloat16),
            "shard",
            scatter_dimension=1,
            tiled=True,
        )
        .astype(jnp.float32)
        .reshape(row_count, 2 * HD)
    )
    key_raw_grad = rotate_back(kv_grad[:, :HD], cosine, sine)
    kv_grad_low = jnp.concatenate([key_raw_grad, kv_grad[:, HD:]], axis=1).astype(jnp.bfloat16)
    query_rot_grad = query_grad.reshape(row_count, HEADS, HD)
    query_raw_grad = (
        rotate_back(query_rot_grad, cos_heads, sin_heads)
        .reshape(row_count, HEADS * HD)
        .astype(jnp.bfloat16)
    )
    qup_term = contract_rows(query_input, query_raw_grad)
    query_in_grad = contract_cols(query_raw_grad, qup_mat)
    query_gain_term = jnp.sum(query_in_grad * normed_query, axis=0)
    query_normed_grad = query_in_grad * query_norm.astype(jnp.float32)
    qdown_grad_low = (
        rms_query
        * (
            query_normed_grad
            - normed_query * jnp.mean(query_normed_grad * normed_query, axis=-1, keepdims=True)
        )
    ).astype(jnp.bfloat16)
    qdown_term = contract_rows(attn_input, qdown_grad_low)
    kv_mat_term = contract_rows(attn_input, kv_grad_low)
    first_in_grad = contract_cols(qdown_grad_low, qdown_mat) + contract_cols(kv_grad_low, kv_mat)
    first_gain_term = jnp.sum(first_in_grad * normed_first, axis=0)
    first_normed_grad = first_in_grad * first_gain.astype(jnp.float32)
    input_rows_grad = middle_grad + rms_first * (
        first_normed_grad
        - normed_first * jnp.mean(first_normed_grad * normed_first, axis=-1, keepdims=True)
    )
    shard_grads = (
        lax.psum_scatter(
            first_gain_term.astype(jnp.bfloat16), "shard", scatter_dimension=0, tiled=True
        ).astype(jnp.float32),
        lax.psum_scatter(
            qdown_term.astype(jnp.bfloat16), "shard", scatter_dimension=0, tiled=True
        ).astype(jnp.float32),
        lax.psum_scatter(
            kv_mat_term.astype(jnp.bfloat16), "shard", scatter_dimension=0, tiled=True
        ).astype(jnp.float32),
        lax.psum_scatter(
            query_gain_term.astype(jnp.bfloat16), "shard", scatter_dimension=0, tiled=True
        ).astype(jnp.float32),
        lax.psum_scatter(
            qup_term.astype(jnp.bfloat16), "shard", scatter_dimension=0, tiled=True
        ).astype(jnp.float32),
        lax.psum_scatter(
            out_term.astype(jnp.bfloat16), "shard", scatter_dimension=0, tiled=True
        ).astype(jnp.float32),
        lax.psum_scatter(
            second_gain_term.astype(jnp.bfloat16), "shard", scatter_dimension=0, tiled=True
        ).astype(jnp.float32),
    )
    grads = (
        shard_grads[0],
        shard_grads[1],
        shard_grads[2],
        shard_grads[3],
        shard_grads[4],
        shard_grads[5],
        shard_grads[6],
        gateup_grad,
        down_grad,
    )
    summed = (
        lax.psum(grads[0].astype(jnp.bfloat16), "replica").astype(jnp.float32),
        lax.psum(grads[1].astype(jnp.bfloat16), "replica").astype(jnp.float32),
        lax.psum(grads[2].astype(jnp.bfloat16), "replica").astype(jnp.float32),
        lax.psum(grads[3].astype(jnp.bfloat16), "replica").astype(jnp.float32),
        lax.psum(grads[4].astype(jnp.bfloat16), "replica").astype(jnp.float32),
        lax.psum(grads[5].astype(jnp.bfloat16), "replica").astype(jnp.float32),
        lax.psum(grads[6].astype(jnp.bfloat16), "replica").astype(jnp.float32),
        lax.psum(grads[7].astype(jnp.bfloat16), "replica").astype(jnp.float32),
        lax.psum(grads[8].astype(jnp.bfloat16), "replica").astype(jnp.float32),
    )
    layer_low = layer.astype(jnp.bfloat16).reshape(per_group, piece_rows, width)
    input_low = input_rows_grad.astype(jnp.bfloat16).reshape(per_group, piece_rows, width)
    all_layer, all_input = (
        lax.all_gather(layer_low, "replica", axis=0, tiled=True),
        lax.all_gather(input_low, "replica", axis=0, tiled=True),
    )
    out_layer = jnp.take(all_layer, my_target, axis=0)
    out_input = jnp.take(all_input, my_target, axis=0)
    return (
        out_layer,
        out_input,
        summed[0],
        summed[1],
        summed[2],
        summed[3],
        summed[4],
        summed[5],
        summed[6],
        summed[7],
        summed[8],
    )


def solution(mesh):
    in_specs = (
        P("replica", "shard", None),
        P("replica", "shard", None),
        P(),
        P("shard"),
        P("shard", None),
        P("shard", None),
        P("shard"),
        P("shard", None),
        P("shard", None),
        P("shard"),
        P("shard", None),
        P("shard", None),
    )
    out_specs = (
        P("replica", "shard", None),
        P("replica", "shard", None),
        P("shard"),
        P("shard", None),
        P("shard", None),
        P("shard"),
        P("shard", None),
        P("shard", None),
        P("shard"),
        P("shard", None),
        P("shard", None),
    )
    return jax.shard_map(
        on_device, mesh=mesh, in_specs=in_specs, out_specs=out_specs, check_vma=False
    )
```

profile of v0, /device:TPU:13, one launch (start us, length us, event | category | flops | bytes accessed | tf_op | source)
XLA Modules:
  0.0 4192.5 jit_solution(9672613117891592169)
XLA Ops:
  14.9 11.4 all-gather.3
  26.3 19.3 all-gather.18.cloned.1.call-done
  47.2 47.7 %all-gather.24.cloned.1.call-done = bf16[2048,512]{1,0:T(8,128)(2,1)} async-done(((bf16[256,512]{1,0:T(8,128)(2,1)}), bf16[2048,512]{1,0:T(8,128)(2,1)}) %all-gather.24.cloned.1.call-update) | async-done | bytes 2097168 | tf_op jit(solution)/shard_map/all_gather | solution.py:149
  102.4 12.1 all-gather.4
  114.6 14.7 all-gather.5
  130.6 37.6 all-gather.20.cloned.1.call-done
  172.1 120.8 %all-gather.22.cloned.1.call-done = bf16[1024,4096]{1,0:T(8,128)(2,1)} async-done(((bf16[128,4096]{1,0:T(8,128)(2,1)}), bf16[1024,4096]{1,0:T(8,128)(2,1)}) %all-gather.22.cloned.1.call-update) | async-done | bytes 8388624 | tf_op jit(solution)/shard_map/all_gather | solution.py:151
  292.9 6.8 fusion.74
  304.5 39.7 all-gather.34.cloned.1.call-done
  344.3 17.4 fusion.2
  361.7 15.3 fusion.3
  377.0 27.3 exponential_convert_fusion
  404.4 9.7 convolution_convert_fusion.4
  417.0 154.1 %all-gather.26.cloned.1.call-done = bf16[4096,2048]{1,0:T(8,128)(2,1)} async-done(((bf16[512,2048]{1,0:T(8,128)(2,1)}), bf16[4096,2048]{1,0:T(8,128)(2,1)}) %all-gather.26.cloned.1.call-update) | async-done | bytes 16777232 | tf_op jit(solution)/shard_map/all_gather | solution.py:152
  571.1 10.3 multiply_reduce_fusion.3
  581.4 865.3 %all-gather.28.cloned.1.call-done = bf16[2048,11264]{1,0:T(8,128)(2,1)} async-done(((bf16[256,11264]{1,0:T(8,128)(2,1)}), bf16[2048,11264]{1,0:T(8,128)(2,1)}) %all-gather.28.cloned.1.call-update) | async-done | bytes 46137360 | tf_op jit(solution)/shard_map/all_gather | solution.py:156
  1446.7 24.9 fusion.75
  1471.6 12.4 all-gather.32.cloned.1.call-done
  1484.0 441.4 %all-gather.30.cloned.1.call-done = bf16[5632,2048]{1,0:T(8,128)(2,1)} async-done(((bf16[704,2048]{1,0:T(8,128)(2,1)}), bf16[5632,2048]{1,0:T(8,128)(2,1)}) %all-gather.30.cloned.1.call-update) | async-done | bytes 23068688 | tf_op jit(solution)/shard_map/all_gather | solution.py:157
  1925.4 18.5 multiply_convert_fusion.2
  1944.0 22.1 multiply_reduce_fusion.1
  1969.3 18.0 convolution_convert_fusion.5
  1987.3 4.2 squeeze_reshape.2
  1991.5 39.6 multiply_reduce_fusion
  2031.1 38.9 multiply_convert_fusion
  2069.9 11.4 fusion.15
  2081.4 8.6 fusion.14
  2091.6 15.3 copy.59
  2106.9 4.7 convolution_multiply_fusion
  2124.5 6.0 multiply_reduce_fusion.4
  2131.6 4.7 convolution_convert_fusion.6
  2136.4 22.0 reduce-scatter.10.cloned.1.call-done
  2164.4 7.5 convolution_convert_fusion.3
  2171.9 9.9 convolution_convert_fusion.2
  2181.9 13.5 convolution_convert_fusion.1
  2196.2 21.6 convolution_convert_fusion
  2217.9 13.0 fusion.12
  2238.3 13.5 reduce-scatter.12.cloned.1.call-done
  2251.8 69.3 %reduce-scatter.14.cloned.1.call-done = bf16[256,512]{1,0:T(8,128)(2,1)} async-done(((bf16[2048,512]{1,0:T(8,128)(2,1)}), bf16[256,512]{1,0:T(8,128)(2,1)}) %reduce-scatter.14.cloned.1.call-update) | async-done | bytes 262160 | tf_op jit(solution)/shard_map/reduce_scatter | solution.py:279
  2321.2 153.2 %reduce-scatter.16.cloned.1.call-done = bf16[128,4096]{1,0:T(8,128)(2,1)} async-done(((bf16[1024,4096]{1,0:T(8,128)(2,1)}), bf16[128,4096]{1,0:T(8,128)(2,1)}) %reduce-scatter.16.cloned.1.call-update) | async-done | bytes 1048592 | tf_op jit(solution)/shard_map/reduce_scatter | solution.py:285
  2474.4 285.1 %reduce-scatter.18.cloned.1.call-done = bf16[512,2048]{1,0:T(8,128)(2,1)} async-done(((bf16[4096,2048]{1,0:T(8,128)(2,1)}), bf16[512,2048]{1,0:T(8,128)(2,1)}) %reduce-scatter.18.cloned.1.call-update) | async-done | bytes 2097168 | tf_op jit(solution)/shard_map/reduce_scatter | solution.py:288
  2759.5 376.9 %reduce-scatter.20.cloned.1.call-done = bf16[704,2048]{1,0:T(8,128)(2,1)} async-done(((bf16[5632,2048]{1,0:T(8,128)(2,1)}), bf16[704,2048]{1,0:T(8,128)(2,1)}) %reduce-scatter.20.cloned.1.call-update) | async-done | bytes 2883600 | tf_op jit(solution)/shard_map/reduce_scatter | solution.py:196
  3136.4 730.1 %reduce-scatter.22.cloned.1.call-done = bf16[256,11264]{1,0:T(8,128)(2,1)} async-done(((bf16[2048,11264]{1,0:T(8,128)(2,1)}), bf16[256,11264]{1,0:T(8,128)(2,1)}) %reduce-scatter.22.cloned.1.call-update) | async-done | bytes 5767184
  3871.7 24.4 all-reduce.4
  3896.3 11.9 all-reduce.5
  3912.2 28.5 all-gather.38.cloned.1.call-done
  3943.1 222.7 %all-reduce.9.cloned.1.call-done = (bf16[256,1024]{1,0:T(8,128)(2,1)}, bf16[256,512]{1,0:T(8,128)(2,1)}, bf16[128,4096]{1,0:T(8,128)(2,1)}, bf16[512,2048]{1,0:T...) async-done(((bf16[256,1024]{1,0:T(8,128)(2,1)}, bf16[256,512]{1,0:T(8,128)(2,1)}, bf16[128,4096]{1,0:T(8,128)(2,1)}, bf16[512,2048]{1,0:T(8,128)(2,1)}, ...) | async-done | bytes 12582928 | tf_op jit(solution)/shard_map/psum | solution.py:308
  4176.7 5.8 convert_element_type.227
  (201 shorter events, 82.4 us)
Async XLA Ops:
  7.2 7.7 copy-start.39
  7.2 38.4 all-gather.18.cloned.1.call-start
  7.9 87.0 %all-gather.24.cloned.1.call-start = ((), (), s32[]{:S(2)}) async-start(), calls=%async_computation.10 | async-start | bytes 2359296 | tf_op jit(solution)/shard_map/all_gather | solution.py:149
  8.7 159.5 %all-gather.20.cloned.1.call-start = ((), (), s32[]{:S(2)}) async-start(), calls=%async_computation.8 | async-start | bytes 4718592 | tf_op jit(solution)/shard_map/all_gather | solution.py:148
  9.4 283.5 %all-gather.22.cloned.1.call-start = ((), (), s32[]{:S(2)}) async-start(), calls=%async_computation.9 | async-start | bytes 9437184 | tf_op jit(solution)/shard_map/all_gather | solution.py:151
  10.0 334.3 %all-gather.34.cloned.1.call-start = ((), (), s32[]{:S(2)}) async-start(), calls=%async_computation.21 | async-start | bytes 2359296 | tf_op jit(solution)/shard_map/all_gather | solution.py:174
  11.6 86.0 %copy-start.43 = (s32[4]{0:T(128)}, s32[4]{0:T(128)S(1)}, u32[]{:S(2)}) copy-start(s32[4]{0:T(128)S(1)} %fusion.64) | copy-start | bytes 52
  26.3 141.9 %copy-start.26 = (f32[8,1,256]{2,1,0:T(1,128)}, f32[8,1,256]{2,1,0:T(1,128)S(1)}, u32[]{:S(2)}) copy-start(f32[8,1,256]{2,1,0:T(1,128)S(1)} %convert_element_type.232) | copy-start | bytes 24580
  26.3 71.3 %copy-start.35 = (f32[128]{0:T(128)}, f32[128]{0:T(128)S(1)}, u32[]{:S(2)}) copy-start(f32[128]{0:T(128)S(1)} %multiply_exponential_fusion) | copy-start | bytes 1540
  26.3 71.3 %copy-start.30 = (f32[256]{0:T(256)}, f32[256]{0:T(256)S(1)}, u32[]{:S(2)}) copy-start(f32[256]{0:T(256)S(1)} %fusion.63) | copy-start | bytes 3076
  47.2 121.0 %copy-start.32 = (f32[256]{0:T(256)}, f32[256]{0:T(256)S(1)}, u32[]{:S(2)}) copy-start(f32[256]{0:T(256)S(1)} %add_rsqrt_fusion.2) | copy-start | bytes 3076
  99.0 472.1 %all-gather.26.cloned.1.call-start = ((), (), s32[]{:S(2)}) async-start(), calls=%async_computation.11 | async-start | bytes 18874368 | tf_op jit(solution)/shard_map/all_gather | solution.py:152
  99.5 1347.2 %all-gather.28.cloned.1.call-start = ((), (), s32[]{:S(2)}) async-start(), calls=%async_computation.12 | async-start | bytes 51904512 | tf_op jit(solution)/shard_map/all_gather | solution.py:156
  100.3 14.2 copy-start.41
  100.3 1383.7 %all-gather.32.cloned.1.call-start = ((), (), s32[]{:S(2)}) async-start(), calls=%async_computation.14 | async-start | bytes 5242880 | tf_op jit(solution)/shard_map/all_gather | solution.py:132
  101.1 1824.4 %all-gather.30.cloned.1.call-start = ((), (), s32[]{:S(2)}) async-start(), calls=%async_computation.13 | async-start | bytes 25952256 | tf_op jit(solution)/shard_map/all_gather | solution.py:157
  101.8 2056.5 %reduce-scatter.10.cloned.1.call-start = ((), (), s32[]{:S(2)}) async-start(), calls=%async_computation.15 | async-start | bytes 2359296 | tf_op jit(solution)/shard_map/reduce_scatter | solution.py:235
  114.5 178.4 %copy-start.24 = (f32[8,1,128]{2,1,0:T(1,128)}, f32[8,1,128]{2,1,0:T(1,128)S(1)}, u32[]{:S(2)}) copy-start(f32[8,1,128]{2,1,0:T(1,128)S(1)} %convert_element_type.233) | copy-start | bytes 12292
  129.2 1836.8 %copy-start.16 = (f32[8,1,256]{2,1,0:T(1,128)}, f32[8,1,256]{2,1,0:T(1,128)S(1)}, u32[]{:S(2)}) copy-start(f32[8,1,256]{2,1,0:T(1,128)S(1)} %convert_element_type.234) | copy-start | bytes 24580
  130.5 169.3 %copy-start.11 = (f32[256,128]{0,1:T(8,128)}, f32[256,128]{0,1:T(8,128)S(1)}, u32[]{:S(2)}) copy-start(f32[256,128]{0,1:T(8,128)S(1)} %copy.53) | copy-start | bytes 393220
  130.6 169.2 %copy-start.13 = (f32[256,128]{0,1:T(8,128)}, f32[256,128]{0,1:T(8,128)S(1)}, u32[]{:S(2)}) copy-start(f32[256,128]{0,1:T(8,128)S(1)} %copy.51) | copy-start | bytes 393220
  172.1 127.6 %copy-start.4 = (f32[256,1024]{1,0:T(8,128)}, f32[256,1024]{1,0:T(8,128)S(1)}, u32[]{:S(2)}) copy-start(f32[256,1024]{1,0:T(8,128)S(1)} %get-tuple-element.76) | copy-start | bytes 3145732
  172.1 127.6 %copy-start.28 = (f32[256]{0:T(256)}, f32[256]{0:T(256)S(1)}, u32[]{:S(2)}) copy-start(f32[256]{0:T(256)S(1)} %add_rsqrt_fusion.1) | copy-start | bytes 3076
  300.4 61.3 %copy-start.6 = (bf16[256,16,128]{0,2,1:T(8,128)(2,1)}, bf16[256,16,128]{0,2,1:T(8,128)(2,1)S(1)}, u32[]{:S(2)}) copy-start(bf16[256,16,128]{0,2,1:T(8,128)(2,1)S(1)} %get-tuple-element.65) | copy-start | bytes 3145732
  300.4 61.2 %copy-start.7 = (bf16[256,16,128]{0,2,1:T(8,128)(2,1)}, bf16[256,16,128]{0,2,1:T(8,128)(2,1)S(1)}, u32[]{:S(2)}) copy-start(bf16[256,16,128]{0,2,1:T(8,128)(2,1)S(1)} %get-tuple-element.66) | copy-start | bytes 3145732
  377.0 27.4 copy-start.18
  417.0 164.4 %copy-start = (bf16[256,4096]{1,0:T(8,128)(2,1)}, bf16[256,4096]{1,0:T(8,128)(2,1)S(1)}, u32[]{:S(2)}) copy-start(bf16[256,4096]{1,0:T(8,128)(2,1)S(1)} %convert_element_type.196) | copy-start | bytes 6291460
  581.4 1384.7 %copy-start.22 = (f32[256]{0:T(256)}, f32[256]{0:T(256)S(1)}, u32[]{:S(2)}) copy-start(f32[256]{0:T(256)S(1)} %add_rsqrt_fusion) | copy-start | bytes 3076
  1471.6 472.3 %copy-start.1 = (f32[256,2048]{1,0:T(8,128)S(1)}, f32[256,2048]{1,0:T(8,128)}, u32[]{:S(2)}) copy-start(f32[256,2048]{1,0:T(8,128)} %get-tuple-element.80) | copy-start | bytes 6291460
  2069.9 11.4 copy-start.10
  2091.5 160.3 %reduce-scatter.12.cloned.1.call-start = ((), (), s32[]{:S(2)}) async-start(), calls=%async_computation.16 | async-start | bytes 4718592 | tf_op jit(solution)/shard_map/reduce_scatter | solution.py:276
  2091.6 15.3 copy-start.19
  2123.2 7.4 copy-start.2
  2124.5 7.1 copy-start.27
  2124.5 7.1 copy-start.33
  2136.3 24.0 copy-start.31
  2136.3 24.0 copy-start.36
  2136.3 184.8 %reduce-scatter.14.cloned.1.call-start = ((), (), s32[]{:S(2)}) async-start(), calls=%async_computation.17 | async-start | bytes 2359296 | tf_op jit(solution)/shard_map/reduce_scatter | solution.py:279
  2164.3 310.1 %reduce-scatter.16.cloned.1.call-start = ((), (), s32[]{:S(2)}) async-start(), calls=%async_computation.18 | async-start | bytes 9437184 | tf_op jit(solution)/shard_map/reduce_scatter | solution.py:285
  2171.9 587.6 %reduce-scatter.18.cloned.1.call-start = ((), (), s32[]{:S(2)}) async-start(), calls=%async_computation.19 | async-start | bytes 18874368 | tf_op jit(solution)/shard_map/reduce_scatter | solution.py:288
  2181.9 954.5 %reduce-scatter.20.cloned.1.call-start = ((), (), s32[]{:S(2)}) async-start(), calls=%async_computation.20 | async-start | bytes 25952256 | tf_op jit(solution)/shard_map/reduce_scatter | solution.py:196
  2195.5 1671.0 %reduce-scatter.22.cloned.1.call-start = ((), (), s32[]{:S(2)}) async-start(), calls=%async_computation.24 | async-start | bytes 51904512
  2217.8 13.2 copy-start.21
  2217.8 1692.1 %all-gather.36.cloned.1.call-start = ((), (), s32[]{:S(2)}) async-start(), calls=%async_computation.22 | async-start | bytes 5242880 | tf_op jit(solution)/shard_map/all_gather | solution.py:320
  2230.9 1709.8 %all-gather.38.cloned.1.call-start = ((), (), s32[]{:S(2)}) async-start(), calls=%async_computation.23 | async-start | bytes 5242880 | tf_op jit(solution)/shard_map/all_gather | solution.py:321
  2238.2 1927.5 %all-reduce.9.cloned.1.call-start = ((), (), s32[]{:S(2)}) async-start(), calls=%async_computation.25 | async-start | bytes 25165824 | tf_op jit(solution)/shard_map/psum | solution.py:308
  4165.7 6.8 copy-start.9
  4176.7 5.8 copy-start.8
  (16 other events, 39.7 us)
Sparse Core Ops, SparseCore 0:
  9.6 35.9 all-gather.17
  47.8 47.0 all-gather.23
  97.0 71.1 all-gather.19
  170.2 122.7 all-gather.21
  295.5 48.7 all-gather.33
  346.3 224.7 all-gather.25
  572.6 874.0 all-gather.27
  1448.3 35.7 all-gather.31
  1485.6 439.8 all-gather.29
  2091.6 66.6 reduce-scatter.9
  2162.5 89.2 reduce-scatter.11
  2255.6 65.4 reduce-scatter.13
  2325.8 148.5 reduce-scatter.15
  2478.0 281.4 reduce-scatter.17
  2763.7 372.6 reduce-scatter.19
  3140.7 725.8 reduce-scatter.21
  3868.5 35.6 all-gather.35
  3906.2 34.4 all-gather.37
  3943.8 221.8 all-reduce.8
where the time goes:
time: 4200 us; the launch traced here: 4190 us
  waiting for transfers between devices  3650 us (87%)
  matrix products  283 us (7%)
  other arithmetic  124 us (3%)
  blocking collectives  74.5 us (2%)
  local copies, waits for them, and re-layouts  44.2 us (1%)
    all_gather x1, waiting for transfers between devices, on_device(): lax.all_gather(gate_up, 'shard', axis=0, tiled=True)  865 us
    unnamed x20, waiting for transfers between devices  735 us
    all_gather x1, waiting for transfers between devices, on_device(): lax.all_gather(down_proj, 'shard', axis=0, tiled=True)  441 us
    reduce_scatter x1, waiting for transfers between devices, on_device(): lax.psum_scatter(contract_rows(hidden_low, cot_low).astype(jnp.bfloat16),...  377 us
    reduce_scatter x1, waiting for transfers between devices, on_device(): lax.psum_scatter(out_term.astype(jnp.bfloat16), 'shard', scatter_dimensio...  285 us
    psum x1, waiting for transfers between devices, on_device(): lax.psum(grads[1].astype(jnp.bfloat16), 'replica').astype(jnp.float32)  223 us
    all_gather x1, waiting for transfers between devices, on_device(): lax.all_gather(out_proj, 'shard', axis=0, tiled=True)  154 us
    reduce_scatter x1, waiting for transfers between devices, on_device(): lax.psum_scatter(qup_term.astype(jnp.bfloat16), 'shard', scatter_dimensio...  153 us
  transfers between devices with their start and end apart: 19, of which 18 were waited for; matrix products, arithmetic and copies ran while one was open for 6% of the time, Pallas kernels for 0%

commit v1 on v0

v1 whole, which is shorter than its diff:
```python
import math

import jax
import jax.numpy as jnp
from jax import lax
from jax.experimental import pallas as pl
from jax.experimental.pallas import tpu as pltpu
from jax.sharding import Mesh
from jax.sharding import PartitionSpec as P

HEADS = 16
HD = 256
FF = 5632
Z = 4
CORES = 2


EPSILON = 1e-06
BF = jnp.bfloat16
F32 = jnp.float32


def inv_rms(values):
    return lax.rsqrt(jnp.mean(values * values, axis=-1, keepdims=True) + EPSILON)


def rope_tables(positions, head_dim):
    half_dim = head_dim // 2
    frequency = jnp.exp(-math.log(10000.0) * jnp.arange(half_dim).astype(F32) / half_dim)
    angles = positions.astype(F32)[:, None] * frequency[None, :]
    return (jnp.cos(angles), jnp.sin(angles))


def rotate(values, cosine, sine):
    half_dim = values.shape[-1] // 2
    first_half = values[..., :half_dim]
    second_half = values[..., half_dim:]
    return jnp.concatenate(
        [first_half * cosine - second_half * sine, second_half * cosine + first_half * sine],
        axis=-1,
    )


def rotate_back(grads, cosine, sine):
    half_dim = grads.shape[-1] // 2
    first_half = grads[..., :half_dim]
    second_half = grads[..., half_dim:]
    return jnp.concatenate(
        [first_half * cosine + second_half * sine, second_half * cosine - first_half * sine],
        axis=-1,
    )


def matmul(left, right):
    return jnp.dot(left, right, preferred_element_type=F32)


def contract_rows(left, right):
    return lax.dot_general(left, right, (((0,), (0,)), ((), ())), preferred_element_type=F32)


def contract_cols(left, right):
    return lax.dot_general(left, right, (((1,), (1,)), ((), ())), preferred_element_type=F32)


STEP_HEADS = 2
NEG = -1e30


def dot_last(left, right):
    return lax.dot_general(left, right, (((1,), (1,)), ((), ())), preferred_element_type=F32)


def seen(shape, rows, y_index):
    n_y = shape[0] // rows
    key = lax.broadcasted_iota(jnp.int32, shape, 0)
    row = lax.broadcasted_iota(jnp.int32, shape, 1)
    ahead = key // rows
    block = lax.rem(y_index + ahead, n_y)
    return (block - y_index) * rows + key - ahead * rows <= row


def attend_kernel(
    place_ref, input_ref, up_ref, cos_ref, sin_ref, kv_ref, q_ref, o_ref, lse_ref,
    vt_ref, m_ref, l_ref, acc_ref,
):
    rows = input_ref.shape[0]
    chunk_rows = kv_ref.shape[0] // Z
    half = HD // 2

    @pl.when(pl.program_id(0) == 0)
    def _():
        for c in range(Z):
            at = slice(c * chunk_rows, (c + 1) * chunk_rows)
            vt_ref[:, at] = kv_ref[at, HD:].T

    cosine, sine = cos_ref[...], sin_ref[...]
    scale = 1.0 / math.sqrt(HD)
    raw = matmul(input_ref[...], up_ref[...])
    for j in range(STEP_HEADS):
        first, second = raw[:, j * HD : j * HD + half], raw[:, j * HD + half : (j + 1) * HD]
        turned = jnp.concatenate(
            [first * cosine - second * sine, second * cosine + first * sine], axis=1
        )
        q_ref[:, j * HD : (j + 1) * HD] = (turned.astype(BF).astype(F32) * scale).astype(BF)
    m_ref[...] = jnp.full_like(m_ref, NEG)
    l_ref[...] = jnp.zeros_like(l_ref)
    acc_ref[...] = jnp.zeros_like(acc_ref)

    def chunk(c, masked):
        at = pl.multiple_of(c * chunk_rows, chunk_rows)
        keys = kv_ref[pl.ds(at, chunk_rows), :HD]
        values = vt_ref[:, pl.ds(at, chunk_rows)]
        for j in range(STEP_HEADS):
            scores = dot_last(keys, q_ref[:, j * HD : (j + 1) * HD])
            if masked:
                scores = jnp.where(seen(scores.shape, rows, place_ref[1]), scores, NEG)
            peak = jnp.maximum(m_ref[j], jnp.max(scores, axis=0, keepdims=True))
            alpha = jnp.exp(m_ref[j] - peak)
            expo = jnp.exp(scores - peak)
            m_ref[j] = peak
            l_ref[j] = l_ref[j] * alpha + jnp.sum(expo, axis=0, keepdims=True)
            acc_ref[j] = acc_ref[j] * alpha + matmul(values, expo.astype(BF))

    @pl.loop(Z - place_ref[0], Z)
    def _(c):
        chunk(c, False)

    chunk(0, True)
    for j in range(STEP_HEADS):
        o_ref[:, j * HD : (j + 1) * HD] = (acc_ref[j] / l_ref[j]).T.astype(BF)
        lse_ref[j] = m_ref[j] + jnp.log(l_ref[j])


def attend(place, query_input, up_mat, cosine, sine, kv_whole):
    rows, rank = query_input.shape
    slot_len = kv_whole.shape[0]
    wide = STEP_HEADS * HD
    whole = lambda h, *_: (0, 0)
    by_head = lambda h, *_: (0, h)
    flops = 2 * rows * HEADS * HD * (rank + 2 * slot_len)
    return pl.pallas_call(
        attend_kernel,
        out_shape=(
            jax.ShapeDtypeStruct((rows, HEADS * HD), BF),
            jax.ShapeDtypeStruct((rows, HEADS * HD), BF),
            jax.ShapeDtypeStruct((HEADS, 1, rows), F32),
        ),
        grid_spec=pltpu.PrefetchScalarGridSpec(
            num_scalar_prefetch=1,
            grid=(HEADS // STEP_HEADS,),
            in_specs=[
                pl.BlockSpec((rows, rank), whole),
                pl.BlockSpec((rank, wide), by_head),
                pl.BlockSpec((rows, HD // 2), whole),
                pl.BlockSpec((rows, HD // 2), whole),
                pl.BlockSpec((slot_len, 2 * HD), whole),
            ],
            out_specs=[
                pl.BlockSpec((rows, wide), by_head),
                pl.BlockSpec((rows, wide), by_head),
                pl.BlockSpec((STEP_HEADS, 1, rows), lambda h, *_: (h, 0, 0)),
            ],
            scratch_shapes=[
                pltpu.VMEM((HD, slot_len), BF),
                pltpu.VMEM((STEP_HEADS, 1, rows), F32),
                pltpu.VMEM((STEP_HEADS, 1, rows), F32),
                pltpu.VMEM((STEP_HEADS, HD, rows), F32),
            ],
        ),
        compiler_params=pltpu.CompilerParams(
            dimension_semantics=("arbitrary",), vmem_limit_bytes=40 * 1024 * 1024
        ),
        cost_estimate=pl.CostEstimate(
            flops=flops,
            bytes_accessed=2 * (rank + 3 * rows) * HEADS * HD,
            transcendentals=rows * HEADS * slot_len,
        ),
    )(place, query_input, up_mat, cosine, sine, kv_whole)


def attend_back_kernel(
    place_ref, q_ref, do_ref, o_ref, lse_ref, cos_ref, sin_ref, kv_ref, dq_ref, dkv_ref,
    acc_ref, dqs_ref,
):
    rows = q_ref.shape[0]
    chunk_rows = kv_ref.shape[0] // Z
    half = HD // 2
    step = pl.program_id(0)

    @pl.when(step == 0)
    def _():
        acc_ref[...] = jnp.zeros_like(acc_ref)

    dqs_ref[...] = jnp.zeros_like(dqs_ref)
    deltas = []
    for j in range(STEP_HEADS):
        at = slice(j * HD, (j + 1) * HD)
        prod = do_ref[:, at].astype(F32) * o_ref[:, at].astype(F32)
        deltas.append(jnp.sum(prod.T, axis=0, keepdims=True))

    def chunk(c, masked):
        at = pl.ds(pl.multiple_of(c * chunk_rows, chunk_rows), chunk_rows)
        keys = kv_ref[at, :HD]
        values = kv_ref[at, HD:]
        for j in range(STEP_HEADS):
            query = q_ref[:, j * HD : (j + 1) * HD]
            out_grad = do_ref[:, j * HD : (j + 1) * HD]
            probs = jnp.exp(dot_last(keys, query) - lse_ref[j])
            if masked:
                probs = jnp.where(seen(probs.shape, rows, place_ref[1]), probs, 0.0)
            score_grad = (probs * (dot_last(values, out_grad) - deltas[j])).astype(BF)
            acc_ref[at, HD:] += matmul(probs.astype(BF), out_grad)
            acc_ref[at, :HD] += matmul(score_grad, query)
            dqs_ref[j] += contract_rows(score_grad, keys)

    @pl.loop(Z - place_ref[0], Z)
    def _(c):
        chunk(c, False)

    chunk(0, True)
    cosine, sine = cos_ref[...], sin_ref[...]
    scale = 1.0 / math.sqrt(HD)
    for j in range(STEP_HEADS):
        first, second = dqs_ref[j, :, :half] * scale, dqs_ref[j, :, half:] * scale
        dq_ref[:, j * HD : (j + 1) * HD] = jnp.concatenate(
            [first * cosine + second * sine, second * cosine - first * sine], axis=1
        ).astype(BF)

    @pl.when(step == pl.num_programs(0) - 1)
    def _():
        dkv_ref[...] = acc_ref[...].astype(BF)


def attend_back(place, query, out_grad, attn_low, logsum, cosine, sine, kv_whole):
    rows = query.shape[0]
    slot_len = kv_whole.shape[0]
    wide = STEP_HEADS * HD
    whole = lambda h, *_: (0, 0)
    by_head = lambda h, *_: (0, h)
    return pl.pallas_call(
        attend_back_kernel,
        out_shape=(
            jax.ShapeDtypeStruct((rows, HEADS * HD), BF),
            jax.ShapeDtypeStruct((slot_len, 2 * HD), BF),
        ),
        grid_spec=pltpu.PrefetchScalarGridSpec(
            num_scalar_prefetch=1,
            grid=(HEADS // STEP_HEADS,),
            in_specs=[
                pl.BlockSpec((rows, wide), by_head),
                pl.BlockSpec((rows, wide), by_head),
                pl.BlockSpec((rows, wide), by_head),
                pl.BlockSpec((STEP_HEADS, 1, rows), lambda h, *_: (h, 0, 0)),
                pl.BlockSpec((rows, HD // 2), whole),
                pl.BlockSpec((rows, HD // 2), whole),
                pl.BlockSpec((slot_len, 2 * HD), whole),
            ],
            out_specs=[
                pl.BlockSpec((rows, wide), by_head),
                pl.BlockSpec((slot_len, 2 * HD), whole),
            ],
            scratch_shapes=[
                pltpu.VMEM((slot_len, 2 * HD), F32),
                pltpu.VMEM((STEP_HEADS, rows, HD), F32),
            ],
        ),
        compiler_params=pltpu.CompilerParams(
            dimension_semantics=("arbitrary",), vmem_limit_bytes=40 * 1024 * 1024
        ),
        cost_estimate=pl.CostEstimate(
            flops=10 * rows * HEADS * HD * slot_len,
            bytes_accessed=2 * 4 * rows * HEADS * HD,
            transcendentals=rows * HEADS * slot_len,
        ),
    )(place, query, out_grad, attn_low, logsum, cosine, sine, kv_whole)


def interleave_kernel(n_shard, order_ref, gain_ref, weight_ref, *refs):
    *slot_refs, out_ref, sum_ref = refs
    n_group = len(slot_refs)
    slots = [ref[...].astype(F32) for ref in slot_refs]
    part = slots[0].shape[1] // 2
    unit = part // n_shard
    width = part * n_group
    blocks = []
    for member in range(n_group):
        block = slots[0]
        for k in range(1, n_group):
            block = jnp.where(order_ref[member] == k, slots[k], block)
        blocks.append(block)
    total = 0.0
    gain = gain_ref[...]
    for half in range(2):
        row = jnp.concatenate(
            [
                blocks[member][:, half * part + s * unit : half * part + (s + 1) * unit]
                for s in range(n_shard)
                for member in range(n_group)
            ],
            axis=1,
        )
        at = slice(half * width, (half + 1) * width)
        total = total + jnp.sum(row * weight_ref[:, at].astype(F32), axis=1, keepdims=True)
        out_ref[:, at] = row * gain
    sum_ref[...] = total


def interleave(order, gain, weight, slots, n_shard):
    rows, width = weight.shape
    block = 32
    by_row = lambda i, *_: (i, 0)
    return pl.pallas_call(
        lambda *refs: interleave_kernel(n_shard, *refs),
        out_shape=(
            jax.ShapeDtypeStruct((rows, width), F32),
            jax.ShapeDtypeStruct((rows, 1), F32),
        ),
        grid_spec=pltpu.PrefetchScalarGridSpec(
            num_scalar_prefetch=1,
            grid=(rows // block,),
            in_specs=[
                pl.BlockSpec((block, 1), by_row),
                pl.BlockSpec((block, width), by_row),
                *[pl.BlockSpec((block, slots[0].shape[1]), by_row) for _ in slots],
            ],
            out_specs=[
                pl.BlockSpec((block, width), by_row),
                pl.BlockSpec((block, 1), by_row),
            ],
        ),
        compiler_params=pltpu.CompilerParams(dimension_semantics=("arbitrary",)),
        cost_estimate=pl.CostEstimate(
            flops=4 * rows * width, bytes_accessed=8 * rows * width, transcendentals=0
        ),
    )(order, gain, weight, *slots)


def from_ahead(value, axis, step):
    n = lax.axis_size(axis)
    return lax.ppermute(value, axis, [((j + step) % n, j) for j in range(n)])


def to_ahead(value, axis, step):
    n = lax.axis_size(axis)
    return lax.ppermute(value, axis, [(j, (j + step) % n) for j in range(n)])


def gather_group(value):
    n_x = lax.axis_size("x")
    mine = [value] + [from_ahead(value, "x", k) for k in range(1, n_x)]
    return mine + [from_ahead(v, "c", 1) for v in mine]


def reduce_group(parts):
    n_x = lax.axis_size("x")
    near, far = parts[:n_x], parts[n_x:]
    sums = [a + to_ahead(b.astype(BF), "c", 1).astype(F32) for a, b in zip(near, far)]
    total = sums[0]
    for k in range(1, n_x):
        total = total + to_ahead(sums[k].astype(BF), "x", k).astype(F32)
    return total


def exchange_group(value, pick):
    n_x = lax.axis_size("x")
    x_id, c_id = lax.axis_index("x"), lax.axis_index("c")
    out = []
    for dc in range(CORES):
        for dx in range(n_x):
            member = lax.rem(x_id + n_x - dx, n_x) * CORES + lax.rem(c_id + dc, CORES)
            block = pick(value, member)
            if dx or dc:
                perm = []
                for j in range(n_x):
                    for c in range(CORES):
                        source = ((j + dx) % n_x) * CORES + (c + dc) % CORES
                        perm.append((source, j * CORES + c))
                block = lax.ppermute(block, ("x", "c"), perm)
            out.append(block)
    return out


def shard_offsets():
    return [(dz, dy) for dz in range(Z) for dy in range(lax.axis_size("y"))]


def shard_permute(value, dz, dy, ahead):
    n_y = lax.axis_size("y")
    perm = []
    for z in range(Z):
        for y in range(n_y):
            far, near = ((z + dz) % Z) * n_y + (y + dy) % n_y, z * n_y + y
            perm.append((near, far) if ahead else (far, near))
    return lax.ppermute(value, ("z", "y"), perm)


def position_of(dz, dy):
    n_y = lax.axis_size("y")
    return lax.rem(lax.axis_index("z") + dz, Z) * n_y + lax.rem(lax.axis_index("y") + dy, n_y)


def ring_z(value):
    return [from_ahead(value, "z", k) if k else value for k in range(Z)]


def scatter_small(blocks):
    near = blocks[0]
    total = jnp.stack(near).astype(F32)
    for k, group in enumerate(blocks[1:]):
        total = total + to_ahead(jnp.stack(group).astype(BF), "y", k + 1).astype(F32)
    out = total[0]
    low = total.astype(BF)
    for k in range(1, Z):
        out = out + to_ahead(low[k], "z", k).astype(F32)
    return out


def after(values, done):
    return lax.optimization_barrier((values, done))[0]


def gather_z(value):
    return lax.all_gather(value, "z", axis=0, tiled=True)


def gather_shard(value):
    return lax.all_gather(value, ("z", "y"), axis=0, tiled=True)


def scatter_z(value):
    return lax.psum_scatter(value, "z", scatter_dimension=0, tiled=True)


def begin_reduce_y(value):
    n_y = lax.axis_size("y")
    index = lax.axis_index("y")
    blocks = value.astype(BF).reshape(Z, n_y, -1, value.shape[1])
    own = lax.dynamic_index_in_dim(blocks, index, axis=1, keepdims=False)
    others = []
    for k in range(1, n_y):
        block = lax.dynamic_index_in_dim(blocks, lax.rem(index + k, n_y), axis=1, keepdims=False)
        others.append(to_ahead(block, "y", k))
    return own, others


def end_reduce_y(own, others):
    total = own.astype(F32)
    for block in others:
        total = total + block.astype(F32)
    return total.astype(BF).reshape(-1, own.shape[-1])


def swap_y(wide):
    n_y = lax.axis_size("y")
    return [wide] + [from_ahead(wide, "y", k) for k in range(1, n_y)]


def merge_y(blocks, n):
    n_y = lax.axis_size("y")
    m = blocks[0].shape[1]
    blocks = [block.reshape(Z, 1, n, m) for block in blocks]
    if n_y == 2:
        first, second = blocks
        return jnp.where(
            lax.axis_index("y") == 0,
            jnp.concatenate([first, second], axis=1),
            jnp.concatenate([second, first], axis=1),
        ).reshape(-1, m)
    at = lax.rem(n_y - lax.axis_index("y"), n_y)
    stacked = jnp.concatenate(blocks + blocks[:-1], axis=1)
    return lax.dynamic_slice_in_dim(stacked, at, n_y, axis=1).reshape(-1, m)


def merge_own_y(blocks):
    n_y = lax.axis_size("y")
    if n_y == 2:
        first, second = blocks
        return jnp.where(
            lax.axis_index("y") == 0,
            jnp.concatenate([first, second]),
            jnp.concatenate([second, first]),
        )
    n = blocks[0].shape[0]
    at = lax.rem(n_y - lax.axis_index("y"), n_y) * n
    return lax.dynamic_slice_in_dim(jnp.concatenate(blocks + blocks[:-1]), at, n_y * n)


def reduce_own_y(value):
    n_y = lax.axis_size("y")
    index = lax.axis_index("y")
    blocks = value.reshape(n_y, -1, value.shape[1])
    total = lax.dynamic_index_in_dim(blocks, index, keepdims=False).astype(F32)
    for k in range(1, n_y):
        other = lax.dynamic_index_in_dim(blocks, lax.rem(index + k, n_y), keepdims=False)
        total = total + to_ahead(other, "y", k).astype(F32)
    return total.astype(BF)


def member_of(dc, dx):
    n_x = lax.axis_size("x")
    x_id = lax.rem(lax.axis_index("x") + dx, n_x)
    return x_id * CORES + lax.rem(lax.axis_index("c") + dc, CORES)


def offsets():
    return [(dc, dx) for dc in range(CORES) for dx in range(lax.axis_size("x"))]


def place_group(slots, axis, dtype):
    n = slots[0].shape[axis]
    shape = list(slots[0].shape)
    shape[axis] = n * len(slots)
    out = jnp.zeros(shape, dtype)
    for (dc, dx), slot in zip(offsets(), slots):
        start = [0] * len(shape)
        start[axis] = member_of(dc, dx) * n
        out = lax.dynamic_update_slice(out, slot.astype(dtype), start)
    return out


def spread_begin(wide):
    n_y, n_x = lax.axis_size("y"), lax.axis_size("x")
    over_y = [wide] + [from_ahead(wide, "y", k) for k in range(1, n_y)]
    over_x = [from_ahead(wide, "x", k) for k in range(1, n_x)]
    return over_y, over_x


def spread_next(over_y, over_x):
    n_x = lax.axis_size("x")
    return [[over_y[0]] + over_x] + [
        [block] + [from_ahead(block, "x", k) for k in range(1, n_x)] for block in over_y[1:]
    ]


def spread_end(grid):
    return [group + [from_ahead(block, "c", 1) for block in group] for group in grid]


def place_every(slots, n):
    n_y, n_x = lax.axis_size("y"), lax.axis_size("x")
    m = slots[0][0].shape[1]
    out = jnp.zeros((Z, n_y, n_x * CORES, n, m), BF)
    for ky, group in enumerate(slots):
        at_y = lax.rem(lax.axis_index("y") + ky, n_y)
        for (dc, dx), slot in zip(offsets(), group):
            out = lax.dynamic_update_slice(
                out, slot.reshape(Z, 1, 1, n, m), (0, at_y, member_of(dc, dx), 0, 0)
            )
    return out.reshape(-1, m)


def on_device(
    tokens,
    cotangent,
    lengths,
    attn_gain,
    query_down,
    key_value,
    query_gain,
    query_up,
    out_proj,
    mlp_gain,
    gate_up,
    down_proj,
):
    n_x = lax.axis_size("x")
    n_group = n_x * CORES
    n_y = lax.axis_size("y")
    n_shard = Z * n_y
    _, rows, width = tokens.shape
    rank = query_down.shape[1]
    group_id = lax.axis_index("x") * CORES + lax.axis_index("c")
    shard_id = lax.axis_index("z") * n_y + lax.axis_index("y")

    def quarter_rows(value):
        n = value.shape[0] // n_group
        return lax.dynamic_slice_in_dim(value, group_id * n, n, axis=0)

    def pick_cols(value, member):
        n = value.shape[1] // n_group
        return lax.dynamic_slice_in_dim(value, member * n, n, axis=1)

    def scaled(weight, gain):
        return (weight.astype(F32) * gain.astype(F32)[:, None]).astype(BF)

    def split(value):
        return [value[k * rows : (k + 1) * rows] for k in range(n_group)]

    qkv_own = jnp.concatenate([query_down, key_value], axis=1)
    qkv_ring = ring_z(scaled(pick_cols(qkv_own, group_id), attn_gain))
    qup_wide = gather_z(quarter_rows(scaled(query_up, query_gain)))
    out_wide = gather_z(quarter_rows(out_proj))
    unit = FF // n_shard // n_group
    part = FF // n_group

    my_length = lax.dynamic_index_in_dim(lengths, group_id, keepdims=False)
    positions = shard_id * rows + jnp.arange(rows, dtype=jnp.int32)
    place = jnp.stack([lax.axis_index("z"), lax.axis_index("y")]).astype(jnp.int32)
    valid = (positions < my_length).astype(F32)[:, None]
    cosine, sine = rope_tables(positions, HD)

    x_rows = tokens[0].astype(F32)
    rms_first = inv_rms(x_rows)
    normed_first = x_rows * rms_first
    attn_input = normed_first.astype(BF)
    input_all = jnp.concatenate(gather_group(attn_input), axis=0)

    qkv_stack = jnp.stack(qkv_ring)
    qkv_grid = [qkv_stack] + [from_ahead(qkv_stack, "y", k) for k in range(1, n_y)]

    gate_up_late = after(gate_up, qkv_stack)
    gu_parts = gate_up_late.reshape(gate_up.shape[0], 2, n_shard, n_group, unit)
    gu_own = lax.dynamic_index_in_dim(gu_parts, group_id, axis=3, keepdims=False)
    gu_own = scaled(gu_own.reshape(-1, 2 * part), mlp_gain)
    gate_own, up_own = gu_own[:, :part], gu_own[:, part:]
    gate_wide = gather_z(gate_own)

    qup_first = spread_begin(qup_wide)
    qkv_mat = jnp.zeros((width, qkv_stack.shape[2]), BF)
    for dy, stack in enumerate(after(qkv_grid, qup_wide)):
        for dz in range(Z):
            at = position_of(dz, dy) * stack.shape[1]
            qkv_mat = lax.dynamic_update_slice(qkv_mat, stack[dz], (at, 0))
    qkv_flat = matmul(input_all, qkv_mat)
    up_wide = gather_z(up_own)
    blocks = []
    for (dc, dx), block in zip(offsets(), split(qkv_flat)):
        if dc or dx:
            perm = []
            for j in range(n_x):
                for c in range(CORES):
                    target = ((j + dx) % n_x) * CORES + (c + dc) % CORES
                    perm.append((j * CORES + c, target))
            block = lax.ppermute(block, ("x", "c"), perm)
        blocks.append(block)
    qup_grid = spread_next(*qup_first)
    blocks = after(blocks, qup_first)
    qkv_out = jnp.zeros((rows, qkv_own.shape[1]), F32)
    n_cols = qkv_own.shape[1] // n_group
    for (dc, dx), block in zip(offsets(), blocks):
        member = lax.rem(lax.axis_index("x") + n_x - dx, n_x) * CORES
        member = member + lax.rem(lax.axis_index("c") + dc, CORES)
        qkv_out = lax.dynamic_update_slice(qkv_out, block, (0, member * n_cols))
    qdown_out, kv_out = qkv_out[:, :rank], qkv_out[:, rank:]

    key_rot = rotate(kv_out[:, :HD], cosine, sine).astype(BF)
    kv_local = jnp.concatenate([key_rot, kv_out[:, HD:].astype(BF)], axis=1)
    out_first = spread_begin(out_wide)
    kv_local = after(kv_local, out_wide)
    kv_ring = ring_z(kv_local)
    down_both = [quarter_rows(down_proj)]
    down_both += [from_ahead(after(down_both[0], qkv_flat), "y", k) for k in range(1, n_y)]
    down_mat = gather_z(merge_own_y(down_both))
    rms_query = inv_rms(qdown_out)
    normed_query = qdown_out * rms_query
    query_input = normed_query.astype(BF)
    qup_slots = spread_end(qup_grid)
    kv_stack = jnp.stack(after(kv_ring, qup_grid))
    kv_grid = [kv_stack] + [from_ahead(kv_stack, "y", k) for k in range(1, n_y)]
    qup_mat = place_every(after(qup_slots, kv_stack), query_up.shape[0] // n_group)
    kv_grid = after(kv_grid, qup_mat)
    kv_whole = jnp.concatenate([stack[dz] for dz in range(Z) for stack in kv_grid])
    query_late = after(query_input, out_first)
    out_grid = spread_next(*out_first)
    query_rot, attn_low, logsum = attend(place, query_late, qup_mat, cosine, sine, kv_whole)
    gate_blocks = swap_y(after(gate_wide, attn_low))
    out_mat = place_every(after(spread_end(out_grid), attn_low), out_proj.shape[0] // n_group)
    middle = x_rows + matmul(attn_low, out_mat)
    rms_second = inv_rms(middle)
    normed_second = middle * rms_second
    mlp_input = normed_second.astype(BF)

    mlp_all = jnp.concatenate(gather_group(mlp_input), axis=0)
    up_blocks = swap_y(after(up_wide, mlp_input))
    cot_rows = cotangent[0].astype(F32) * valid
    cot_late = after(cot_rows.astype(BF), mlp_input)
    cot_all = jnp.concatenate(gather_group(cot_late), axis=0)
    gate_mat = merge_y(after(gate_blocks, mlp_all), mlp_gain.shape[0])
    gate_part = matmul(mlp_all, gate_mat)
    up_mat = merge_y(after(up_blocks, (gate_part, down_mat)), mlp_gain.shape[0])
    up_part = matmul(mlp_all, up_mat)
    sigmoid_gate = jax.nn.sigmoid(gate_part)
    activated = gate_part * sigmoid_gate
    hidden_low = (activated * up_part).astype(BF)

    def pick_out(value, member):
        parts = value.reshape(rows, n_shard, n_group, -1)
        return lax.dynamic_index_in_dim(parts, member, axis=2, keepdims=False).reshape(rows, -1)

    attn_late, query_late = after((attn_low, query_input), cot_all)
    attn_all = jnp.concatenate(exchange_group(attn_late, pick_out), axis=0)
    query_all = jnp.concatenate(gather_group(query_late), axis=0)

    down_term = contract_rows(hidden_low, cot_all).astype(BF)
    down_half = scatter_z(down_term)
    down_mat = after(down_mat, (down_term, attn_all, query_all))
    hidden_grad = contract_cols(cot_all, down_mat)
    gate_grad = hidden_grad * up_part * (sigmoid_gate * (1.0 + gate_part * (1.0 - sigmoid_gate)))
    gate_low = gate_grad.astype(BF)
    up_low = (hidden_grad * activated).astype(BF)
    partial_in = contract_cols(gate_low, gate_mat) + contract_cols(up_low, up_mat)
    gate_low, up_low = after((gate_low, up_low), partial_in)
    gate_term = contract_rows(mlp_all, gate_low).astype(BF)
    gate_ends = begin_reduce_y(gate_term)
    up_term = contract_rows(mlp_all, after(up_low, gate_term)).astype(BF)
    up_ends = begin_reduce_y(up_term)
    mlp_in_grad = after(reduce_group(split(partial_in)), up_term)

    middle_grad = cot_rows + rms_second * (
        mlp_in_grad
        - normed_second * jnp.mean(mlp_in_grad * normed_second, axis=-1, keepdims=True)
    )
    middle_low = middle_grad.astype(BF)
    middle_all = jnp.concatenate(gather_group(middle_low), axis=0)
    attn_val_grad = contract_cols(middle_low, out_mat).astype(BF)
    query_raw_grad, kv_term = attend_back(
        place, query_rot, attn_val_grad, attn_low, logsum, cosine, sine, kv_whole
    )
    kv_slots = [kv_term[k * rows : (k + 1) * rows] for k in range(Z * n_y)]
    kv_grad = scatter_small([kv_slots[k::n_y] for k in range(n_y)])
    gate_pre = end_reduce_y(gate_ends[0], after(gate_ends[1], kv_term))
    gate_sum = scatter_z(gate_pre)
    out_term = contract_rows(attn_all, after(middle_all, gate_pre)).astype(BF)
    out_ends = begin_reduce_y(out_term)
    raw_all = jnp.concatenate(exchange_group(query_raw_grad, pick_cols), axis=0)
    query_in_grad = contract_cols(query_raw_grad, qup_mat)
    qup_term = contract_rows(query_all, raw_all).astype(BF)
    qup_ends = begin_reduce_y(qup_term)
    hidden_late = after(hidden_low, (qup_term, out_term))
    layer_part = matmul(hidden_late, down_mat)
    layer = (middle + reduce_group(split(layer_part))) * valid
    qdown_grad = rms_query * (
        query_in_grad
        - normed_query * jnp.mean(query_in_grad * normed_query, axis=-1, keepdims=True)
    )
    kv_grad = after(kv_grad, down_half)
    key_raw_grad = rotate_back(kv_grad[:, :HD], cosine, sine)
    qkv_low = jnp.concatenate([qdown_grad, key_raw_grad, kv_grad[:, HD:]], axis=1).astype(BF)
    qkv_all = jnp.concatenate(exchange_group(qkv_low, pick_cols), axis=0)
    qkv_term = contract_rows(input_all, qkv_all).astype(BF)
    n_own = query_down.shape[0]
    qkv_sum = scatter_small(
        [
            [
                lax.dynamic_slice_in_dim(qkv_term, position_of(dz, dy) * n_own, n_own)
                for dz in range(Z)
            ]
            for dy in range(n_y)
        ]
    ).astype(BF)
    down_sum = reduce_own_y(down_half)
    first_part = contract_cols(after(qkv_all, qkv_term), qkv_mat)
    up_pre = end_reduce_y(up_ends[0], after(up_ends[1], (qkv_low, layer_part)))
    up_sum = scatter_z(up_pre)
    out_pre = end_reduce_y(out_ends[0], after(out_ends[1], (up_pre, first_part)))
    out_sum = scatter_z(out_pre)
    qup_pre = end_reduce_y(qup_ends[0], after(qup_ends[1], out_pre))
    qup_sum = scatter_z(qup_pre)
    first_in_grad = reduce_group(split(first_part))
    input_rows_grad = middle_grad + rms_first * (
        first_in_grad
        - normed_first * jnp.mean(first_in_grad * normed_first, axis=-1, keepdims=True)
    )

    down_grad = place_group(gather_group(down_sum), 0, F32)
    gate_sum = after(gate_sum, down_grad)
    up_sum = after(up_sum, gate_sum)
    gateup_slots = gather_group(jnp.concatenate([gate_sum, up_sum], axis=1))
    out_sum = after(out_sum, up_sum)
    out_grad = place_group(gather_group(out_sum), 0, F32)
    qup_sum = after(qup_sum, out_sum)
    order = jnp.zeros((n_group,), jnp.int32)
    for k, (dc, dx) in enumerate(offsets()):
        order = order.at[member_of(dc, dx)].set(k)
    gateup_grad, second_gain_grad = interleave(
        order, mlp_gain.astype(F32)[:, None], gate_up, gateup_slots, n_shard
    )
    qup_raw = place_group(gather_group(qup_sum), 1, F32)
    qkv_raw = place_group(gather_group(qkv_sum), 1, F32)

    def gain_grad(weight, grad):
        return jnp.sum(weight.astype(F32) * grad, axis=1)

    qkv_weight_grad = qkv_raw * attn_gain.astype(F32)[:, None]
    return (
        layer.astype(BF)[None],
        input_rows_grad.astype(BF)[None],
        gain_grad(qkv_own, qkv_raw),
        qkv_weight_grad[:, :rank],
        qkv_weight_grad[:, rank:],
        gain_grad(query_up, qup_raw),
        qup_raw * query_gain.astype(F32)[:, None],
        out_grad,
        second_gain_grad[:, 0],
        gateup_grad,
        down_grad,
    )


def solution(mesh):
    n_replica, n_shard = mesh.devices.shape
    devices = mesh.devices.reshape(n_replica // CORES, CORES, Z, n_shard // Z)
    inner = Mesh(devices, ("x", "c", "z", "y"))
    group, shard = ("x", "c"), ("z", "y")
    acts = P(group, shard, None)
    vec = P(shard)
    mat = P(shard, None)
    in_specs = (acts, acts, P(), vec, mat, mat, vec, mat, mat, vec, mat, mat)
    out_specs = (acts, acts, vec, mat, mat, vec, mat, mat, vec, mat, mat)
    return jax.shard_map(
        on_device, mesh=inner, in_specs=in_specs, out_specs=out_specs, check_vma=False
    )
```

time: 4200 us -> 1120 us (0.27)
  waiting for transfers between devices: 3650 us -> 479 us
  starting transfers between devices: 0.76 us -> 142 us
  matrix products: 283 us -> 152 us
  local copies, waits for them, and re-layouts: 44.2 us -> 169 us
  blocking collectives: 74.5 us -> 0 us
  Pallas kernels: 0 us -> 60.6 us
    all_gather x11 -> x5, waiting for transfers between devices: 1770 us -> 0.03 us  [gather_z(): return lax.all_gather(value, 'z', axis=0, tiled=True)]
    reduce_scatter x6 -> x5, waiting for transfers between devices: 920 us -> 0.02 us  [scatter_z(): return lax.psum_scatter(value, 'z', scatter_dimension=0, tiled=True)]
    unnamed x20 -> x10, waiting for transfers between devices: 735 us -> 0.16 us
    ppermute x0 -> x89, waiting for transfers between devices: none -> 479 us  [the longest x55 265 us: from_ahead(): return lax.ppermute(value, axis, [((j + step) % n, j) for j in range(n)])]
    psum x1 -> x0, waiting for transfers between devices: 223 us -> none  [on_device(): lax.psum(grads[1].astype(jnp.bfloat16), 'replica').astype(jnp.float32)]
    ppermute x0 -> x89, starting transfers between devices: none -> 142 us  [the longest x22 67.9 us: to_ahead(): return lax.ppermute(value, axis, [(j, (j + step) % n) for j in range(n)])]
    dot_general x8 -> x6, matrix products: 127 us -> 63.1 us  [contract_cols(): lax.dot_general(left, right, (((1,), (1,)), ((), ())), preferred_element_...]
    pallas_call x0 -> x3, Pallas kernels: none -> 60.6 us  [the longest x1 25.5 us: attend(): pl.pallas_call(attend_kernel, out_shape=(jax.ShapeDtypeStruct((rows, HEAD...]
  transfers between devices with their start and end apart: 19 -> 99, of which waited for: 18 -> 31; matrix products, arithmetic and copies ran while one was open for 6% -> 35% of each run, Pallas kernels for 0% -> 4%
where the time goes in v1:
time: 1120 us; the launch traced here: 1110 us
  waiting for transfers between devices  479 us (43%)
  local copies, waits for them, and re-layouts  169 us (15%)
  matrix products  152 us (14%)
  starting transfers between devices  142 us (13%)
  other arithmetic  89.7 us (8%)
  Pallas kernels  60.6 us (5%)
  between operations  15.9 us (1%)
    ppermute x55, waiting for transfers between devices, from_ahead(): return lax.ppermute(value, axis, [((j + step) % n, j) for j in range(n)])  265 us
    ppermute x22, waiting for transfers between devices, to_ahead(): return lax.ppermute(value, axis, [(j, (j + step) % n) for j in range(n)])  171 us
    ppermute x22, starting transfers between devices, to_ahead(): return lax.ppermute(value, axis, [(j, (j + step) % n) for j in range(n)])  67.9 us
    dot_general x6, matrix products, contract_cols(): lax.dot_general(left, right, (((1,), (1,)), ((), ())), preferred_element_...  63.1 us
    ppermute x55, starting transfers between devices, from_ahead(): return lax.ppermute(value, axis, [((j + step) % n, j) for j in range(n)])  62.3 us
    dot_general x5, matrix products, matmul(): return jnp.dot(left, right, preferred_element_type=F32)  45.8 us
    unnamed x165, local copies, waits for them, and re-layouts  44.1 us
    dot_general x6, matrix products, contract_rows(): lax.dot_general(left, right, (((0,), (0,)), ((), ())), preferred_element_...  43.3 us
  transfers between devices with their start and end apart: 99, of which 31 were waited for; matrix products, arithmetic and copies ran while one was open for 35% of the time, Pallas kernels for 4%

profile of v1, /device:TPU:13, one launch (start us, length us, event | category | flops | bytes accessed | tf_op | source)
XLA Modules:
  0.0 1109.3 jit_solution(9815245764030850209)
XLA Ops:
  22.8 22.4 %collective-permute-done.4 = bf16[256,384]{1,0:T(8,128)(2,1)S(1)} collective-permute-done((bf16[256,384]{1,0:T(8,128)(2,1)}, bf16[256,384]{1,0:T(8,128)(2,1)S(1)}, u32[]{:S(2)}, u32[]{:S(2)}) %collective-permute-start.4) | collective-permute-done | bytes 196640 | tf_op jit(solution)/shard_map/ppermute | solution.py:341
  45.3 8.1 collective-permute-done.3
  54.3 8.3 copy.49
  73.3 21.1 %collective-permute-done = bf16[256,2048]{1,0:T(8,128)(2,1)} collective-permute-done((bf16[256,2048]{1,0:T(8,128)(2,1)}, bf16[256,2048]{1,0:T(8,128)(2,1)}, u32[]{:S(2)}, u32[]{:S(2)}) %collective-permute-start) | collective-permute-done | bytes 1048608 | tf_op jit(solution)/shard_map/ppermute | solution.py:341
  105.7 5.6 fusion.41
  116.7 19.0 %collective-permute-done.7 = f32[256,384]{1,0:T(8,128)} collective-permute-done((f32[256,384]{1,0:T(8,128)}, f32[256,384]{1,0:T(8,128)}, u32[]{:S(2)}, u32[]{:S(2)}) %collective-permute-start.7) | collective-permute-done | bytes 393248 | tf_op jit(solution)/shard_map/ppermute | solution.py:635
  136.9 7.9 collective-permute-done.9
  154.6 15.7 %collective-permute-done.16 = bf16[128,4096]{1,0:T(8,128)(2,1)} collective-permute-done((bf16[128,4096]{1,0:T(8,128)(2,1)}, bf16[128,4096]{1,0:T(8,128)(2,1)}, u32[]{:S(2)}, u32[]{:S(2)}) %collective-permute-start.16) | collective-permute-done | bytes 1048608 | tf_op jit(solution)/shard_map/ppermute | solution.py:341
  171.1 31.6 %collective-permute-done.20 = bf16[256,512]{1,0:T(8,128)(2,1)S(1)} collective-permute-done((bf16[256,512]{1,0:T(8,128)(2,1)S(1)}, bf16[256,512]{1,0:T(8,128)(2,1)S(1)}, u32[]{:S(2)}, u32[]{:S(2)}) %collective-permute-start.20) | collective-permute-done | bytes 262176 | tf_op jit(solution)/shard_map/ppermute | solution.py:341
  206.5 7.6 collective-permute-done.21
  227.0 33.4 %collective-permute-done.12 = bf16[512,2048]{1,0:T(8,128)(2,1)} collective-permute-done((bf16[512,2048]{1,0:T(8,128)(2,1)}, bf16[512,2048]{1,0:T(8,128)(2,1)}, u32[]{:S(2)}, u32[]{:S(2)}) %collective-permute-start.12) | collective-permute-done | bytes 2097184 | tf_op jit(solution)/shard_map/ppermute | solution.py:341
  265.7 17.2 %collective-permute-done.22 = bf16[4,256,512]{2,1,0:T(8,128)(2,1)S(1)} collective-permute-done((bf16[4,256,512]{2,1,0:T(8,128)(2,1)S(1)}, bf16[4,256,512]{2,1,0:T(8,128)(2,1)S(1)}, u32[]{:S(2)}, u32[]{:S(2)}) %collective-permute-start.22) | collective-permute-done | bytes 1048608 | tf_op jit(solution)/shard_map/ppermute | solution.py:341
  285.2 19.6 %collective-permute-done.25 = bf16[512,2048]{1,0:T(8,128)(2,1)} collective-permute-done((bf16[512,2048]{1,0:T(8,128)(2,1)}, bf16[512,2048]{1,0:T(8,128)(2,1)}, u32[]{:S(2)}, u32[]{:S(2)}) %collective-permute-start.25) | collective-permute-done | bytes 2097184 | tf_op jit(solution)/shard_map/ppermute | solution.py:341
  309.4 25.5 %shard_map.203 = (bf16[256,4096]{1,0:T(8,128)(2,1)S(1)}, bf16[256,4096]{1,0:T(8,128)(2,1)S(1)}, f32[16,1,256]{2,1,0:T(1,128)S(1)}) custom-call(s32[2]{0:T(128)S(1)} %pad_add_fusion.place_ref, bf16[256,1024]{1,0:T(8,128)(2,1)S(1)} %fusion.40.input_ref, bf16[1024,4096]{1,0:T(8,128)(2,1)} %bitcast.241, f32[256,128]{1,0:T(8,128)S(1)} %get-tuple-element.256.cos_ref, ...), custom_call_target="tpu_custom_call" | custom-call | flops 10737418240 | bytes 14680064 | tf_op jit(solution)/shard_map/pallas_call | solution.py:142
  365.2 36.6 %collective-permute-done.31 = bf16[1024,1408]{0,1:T(8,128)(2,1)} collective-permute-done((bf16[1024,1408]{0,1:T(8,128)(2,1)}, bf16[1024,1408]{0,1:T(8,128)(2,1)}, u32[]{:S(2)}, u32[]{:S(2)}) %collective-permute-start.31) | collective-permute-done | bytes 2883616 | tf_op jit(solution)/shard_map/ppermute | solution.py:341
  412.4 7.7 maximum_select_fusion
  430.9 11.4 %fusion.73 = f32[1024,1408]{1,0:T(8,128)} fusion(bf16[2048,1408]{1,0:T(8,128)(2,1)S(1)} %bitcast.246, bf16[256,2048]{1,0:T(8,128)(2,1)} %collective-permute-done.30, bf16[256,2048]{1,0:T(8,128)(2,1)} %collective-permute-done.29, bf16[256,2048]{1,0:T(8,128)(2,1)} %collective-permute-done.28, bf16[256,2048]{1,0:T(8,128)(2,1)} %multiply_convert_fusion.3), kind=kOutput, calls=%fused_computation.252 | convolution fusion | flops 5922357248 | bytes 15728640 | tf_op jit(solution)/shard_map/dot_general | solution.py:55
  445.1 9.7 constant_dynamic-slice_fusion.19
  472.3 11.8 %collective-permute-done.32 = bf16[1024,1408]{0,1:T(8,128)(2,1)} collective-permute-done((bf16[1024,1408]{0,1:T(8,128)(2,1)}, bf16[1024,1408]{0,1:T(8,128)(2,1)}, u32[]{:S(2)}, u32[]{:S(2)}) %collective-permute-start.32) | collective-permute-done | bytes 2883616 | tf_op jit(solution)/shard_map/ppermute | solution.py:341
  498.4 14.4 %multiply_convert_fusion.2 = (bf16[1024,1408]{1,0:T(8,128)(2,1)S(1)}, f32[1024,1408]{1,0:T(8,128)}) fusion(f32[1024,1408]{1,0:T(8,128)} %fusion.73, bf16[2048,1408]{1,0:T(8,128)(2,1)S(1)} %bitcast.251, bf16[256,2048]{1,0:T(8,128)(2,1)} %collective-permute-done.30, bf16[256,2048]{1,0:T(8,128)(2,1)} %collective-permute-done.29, ...), kind=kOutput, calls=%fused_computation.11 | convolution fusion | flops 5931008000 | bytes 24379392 | tf_op jit(solution)/shard_map/dot_general | solution.py:55
  514.4 8.1 convolution_convert_fusion.2
  524.5 14.6 %multiply_convert_fusion = (bf16[1024,1408]{1,0:T(8,128)(2,1)S(1)}, bf16[1024,1408]{1,0:T(8,128)(2,1)S(1)}) fusion(f32[1024,1408]{1,0:T(8,128)} %fusion.73, f32[1024,1408]{1,0:T(8,128)} %get-tuple-element.260, bf16[1024,2048]{1,0:T(8,128)(2,1)} %copy-done.41, bf16[1408,2048]{1,0:T(8,128)(2,1)} %all-gather.14.cloned.1.call-done), kind=kOutput, calls=%fused_computation.9 | convolution fusion | flops 5924323328 | bytes 27262976 | tf_op jit(solution)/shard_map/dot_general | solution.py:63
  539.2 12.7 %fusion.86 = f32[1024,2048]{1,0:T(8,128)} fusion(bf16[1024,1408]{1,0:T(8,128)(2,1)S(1)} %get-tuple-element.169, bf16[2048,1408]{1,0:T(8,128)(2,1)} %bitcast.245), kind=kOutput, calls=%fused_computation.262 | convolution fusion | flops 5905580032 | bytes 17039360 | tf_op jit(solution)/shard_map/dot_general | solution.py:63
  551.9 10.1 fusion.83
  563.7 9.4 convolution_convert_fusion.1
  578.9 8.7 convolution_convert_fusion
  591.0 10.8 collective-permute-done.45
  608.7 12.0 %convolution_convert_fusion.3.do_ref = bf16[256,4096]{1,0:T(8,128)(2,1)} fusion(bf16[256,2048]{1,0:T(8,128)(2,1)} %get-tuple-element.193, bf16[4096,2048]{1,0:T(8,128)(2,1)} %bitcast.232), kind=kOutput, calls=%fused_computation.14 | convolution fusion | flops 4296015872 | bytes 19922944 | tf_op jit(solution)/shard_map/dot_general | solution.py:63
  625.5 21.4 %shard_map.204 = (bf16[256,4096]{1,0:T(8,128)(2,1)S(1)}, bf16[2048,512]{1,0:T(8,128)(2,1)S(1)}) custom-call(s32[2]{0:T(128)S(1)} %pad_add_fusion.place_ref, bf16[256,4096]{1,0:T(8,128)(2,1)S(1)} %copy-done.6, bf16[256,4096]{1,0:T(8,128)(2,1)S(1)} %copy-done.4, bf16[256,4096]{1,0:T(8,128)(2,1)S(1)} %get-tuple-element.166.o_ref, ...), custom_call_target="tpu_custom_call" | custom-call | flops 21474836480 | bytes 8388608 | tf_op jit(solution)/shard_map/pallas_call | solution.py:241
  650.2 6.5 multiply_reduce_fusion.4
  663.1 11.0 collective-permute-done.56
  676.0 49.4 %collective-permute-start.58 = (bf16[256,512]{1,0:T(8,128)(2,1)S(1)}, bf16[256,512]{1,0:T(8,128)(2,1)S(1)}, u32[]{:S(2)}, u32[]{:S(2)}) collective-permute-start(bf16[256,512]{1,0:T(8,128)(2,1)S(1)} %get-tuple-element.245), channel_id=1, source_target_pairs={{0,4},{2,6},{4,0},{6,2},{1,5},{3,7},{5,1},{7,3},{8,12},{10,14},{12... | collective-permute-start | bytes 786440 | tf_op jit(solution)/shard_map/ppermute | solution.py:346
  727.7 5.7 fusion.34
  735.4 20.0 %collective-permute-done.58 = bf16[256,512]{1,0:T(8,128)(2,1)S(1)} collective-permute-done((bf16[256,512]{1,0:T(8,128)(2,1)S(1)}, bf16[256,512]{1,0:T(8,128)(2,1)S(1)}, u32[]{:S(2)}, u32[]{:S(2)}) %collective-permute-start.58) | collective-permute-done | bytes 262176 | tf_op jit(solution)/shard_map/ppermute | solution.py:346
  756.3 19.9 %collective-permute-done.57 = bf16[256,512]{1,0:T(8,128)(2,1)S(1)} collective-permute-done((bf16[256,512]{1,0:T(8,128)(2,1)S(1)}, bf16[256,512]{1,0:T(8,128)(2,1)S(1)}, u32[]{:S(2)}, u32[]{:S(2)}) %collective-permute-start.57) | collective-permute-done | bytes 262176 | tf_op jit(solution)/shard_map/ppermute | solution.py:346
  780.4 8.4 collective-permute-done.40
  788.9 6.0 convolution_convert_fusion.4
  795.0 9.6 fusion.84
  805.2 36.1 %collective-permute-done.75 = bf16[4,256,1408]{2,1,0:T(8,128)(2,1)} collective-permute-done((bf16[4,256,1408]{2,1,0:T(8,128)(2,1)}, bf16[4,256,1408]{2,1,0:T(8,128)(2,1)}, u32[]{:S(2)}, u32[]{:S(2)}) %collective-permute-start.75) | collective-permute-done | bytes 2883616 | tf_op jit(solution)/shard_map/ppermute | solution.py:346
  861.1 5.3 convolution_convert_fusion.5
  866.4 7.1 fusion.85
  873.6 20.4 %collective-permute-done.74 = bf16[4,128,2048]{2,1,0:T(8,128)(2,1)S(1)} collective-permute-done((bf16[4,128,2048]{2,1,0:T(8,128)(2,1)S(1)}, bf16[4,128,2048]{2,1,0:T(8,128)(2,1)S(1)}, u32[]{:S(2)}, u32[]{:S(2)}) %collective-permute-start.74) | collective-permute-done | bytes 2097184 | tf_op jit(solution)/shard_map/ppermute | solution.py:346
  906.4 20.4 %collective-permute-done.55 = bf16[256,2048]{1,0:T(8,128)(2,1)} collective-permute-done((bf16[256,2048]{1,0:T(8,128)(2,1)}, bf16[256,2048]{1,0:T(8,128)(2,1)}, u32[]{:S(2)}, u32[]{:S(2)}) %collective-permute-start.55) | collective-permute-done | bytes 1048608 | tf_op jit(solution)/shard_map/ppermute | solution.py:346
  950.3 15.3 %collective-permute-done.66 = bf16[4,256,384]{2,1,0:T(8,128)(2,1)} collective-permute-done((bf16[4,256,384]{2,1,0:T(8,128)(2,1)}, bf16[4,256,384]{2,1,0:T(8,128)(2,1)}, u32[]{:S(2)}, u32[]{:S(2)}) %collective-permute-start.66) | collective-permute-done | bytes 786464 | tf_op jit(solution)/shard_map/ppermute | solution.py:346
  993.2 7.8 collective-permute-done.70
  1014.3 8.7 collective-permute-done.65
  1053.5 25.8 %collective-permute-done.86.refs_4_ = bf16[256,2816]{1,0:T(8,128)(2,1)S(1)} collective-permute-done((bf16[256,2816]{1,0:T(8,128)(2,1)}, bf16[256,2816]{1,0:T(8,128)(2,1)S(1)}, u32[]{:S(2)}, u32[]{:S(2)}) %collective-permute-start.86) | collective-permute-done | bytes 1441824 | tf_op jit(solution)/shard_map/ppermute | solution.py:341
  1087.0 13.7 %shard_map.205 = (f32[256,11264]{1,0:T(8,128)}, f32[256,1]{1,0:T(8,128)}) custom-call(s32[4]{0:T(128)} %copy-done.52, f32[256,1]{1,0:T(8,128)} %copy.72.refs_1_, bf16[256,11264]{1,0:T(8,128)(2,1)} %refs_2_.1, bf16[256,2816]{1,0:T(8,128)(2,1)} %constant_dynamic-update-slice_fusion.10.refs_3_, bf16[256,2816]{1,0:T(8,128)(2,1)} %copy-done.32, ...), custom_call_target="tpu_custom_call" | custom-call | flops 11534336 | bytes 23068672 | tf_op jit(solution)/shard_map/pallas_call | solution.py:313
  (507 shorter events, 353.3 us)
Async XLA Ops:
  7.2 89.0 %all-gather.6.cloned.1.call-start = ((), (), s32[]{:S(2)}) async-start(), calls=%async_computation.5 | async-start | bytes 1310720 | tf_op jit(solution)/shard_map/all_gather | solution.py:424
  12.1 138.1 %all-gather.8.cloned.1.call-start = ((), (), s32[]{:S(2)}) async-start(), calls=%async_computation.6 | async-start | bytes 2621440 | tf_op jit(solution)/shard_map/all_gather | solution.py:424
  14.1 323.3 %all-gather.10.cloned.1.call-start = ((), (), s32[]{:S(2)}) async-start(), calls=%async_computation.7 | async-start | bytes 3604480 | tf_op jit(solution)/shard_map/all_gather | solution.py:424
  65.8 354.4 %all-gather.12.cloned.1.call-start = ((), (), s32[]{:S(2)}) async-start(), calls=%async_computation.8 | async-start | bytes 3604480 | tf_op jit(solution)/shard_map/all_gather | solution.py:424
  73.3 399.0 %all-gather.14.cloned.1.call-start = ((), (), s32[]{:S(2)}) async-start(), calls=%async_computation.9 | async-start | bytes 7208960 | tf_op jit(solution)/shard_map/all_gather | solution.py:424
  102.2 42.7 %collective-permute-start.10 = (bf16[128,4096]{1,0:T(8,128)(2,1)}, bf16[128,4096]{1,0:T(8,128)(2,1)}, u32[]{:S(2)}, u32[]{:S(2)}) collective-permute-start(bf16[128,4096]{1,0:T(8,128)(2,1)} %all-gather.6.cloned.1.call-done), channel_id=1, source_target_pairs={{1,0},{0,1},{3,2},{2,3},{5,4},{4,5},{7,6},{6,7},{9,8},{8,9},{11,10... | collective-permute-start | bytes 3145736 | tf_op jit(solution)/shard_map/ppermute | solution.py:341
  102.5 42.4 %collective-permute-start.11 = (bf16[128,4096]{1,0:T(8,128)(2,1)}, bf16[128,4096]{1,0:T(8,128)(2,1)}, u32[]{:S(2)}, u32[]{:S(2)}) collective-permute-start(bf16[128,4096]{1,0:T(8,128)(2,1)} %all-gather.6.cloned.1.call-done), channel_id=1, source_target_pairs={{16,0},{0,16},{17,1},{1,17},{18,2},{2,18},{19,3},{3,19},{20,4},{4,... | collective-permute-start | bytes 3145736 | tf_op jit(solution)/shard_map/ppermute | solution.py:341
  151.5 64.3 %collective-permute-start.14 = (bf16[128,4096]{1,0:T(8,128)(2,1)}, bf16[128,4096]{1,0:T(8,128)(2,1)}, u32[]{:S(2)}, u32[]{:S(2)}) collective-permute-start(bf16[128,4096]{1,0:T(8,128)(2,1)} %all-gather.6.cloned.1.call-done), channel_id=1, source_target_pairs={{8,0},{0,8},{9,1},{1,9},{10,2},{2,10},{11,3},{3,11},{12,4},{4,12},... | collective-permute-start | bytes 3145736 | tf_op jit(solution)/shard_map/ppermute | solution.py:341
  151.5 65.6 %collective-permute-start.15 = (bf16[128,4096]{1,0:T(8,128)(2,1)}, bf16[128,4096]{1,0:T(8,128)(2,1)}, u32[]{:S(2)}, u32[]{:S(2)}) collective-permute-start(bf16[128,4096]{1,0:T(8,128)(2,1)} %collective-permute-done.11), channel_id=1, source_target_pairs={{8,0},{0,8},{9,1},{1,9},{10,2},{2,10},{11,3},{3,11},{12,4},{4,12},... | collective-permute-start | bytes 3145736 | tf_op jit(solution)/shard_map/ppermute | solution.py:341
  152.0 67.2 %collective-permute-start.17 = (bf16[128,4096]{1,0:T(8,128)(2,1)}, bf16[128,4096]{1,0:T(8,128)(2,1)}, u32[]{:S(2)}, u32[]{:S(2)}) collective-permute-start(bf16[128,4096]{1,0:T(8,128)(2,1)} %collective-permute-done.10), channel_id=1, source_target_pairs={{8,0},{0,8},{9,1},{1,9},{10,2},{2,10},{11,3},{3,11},{12,4},{4,12},... | collective-permute-start | bytes 3145736 | tf_op jit(solution)/shard_map/ppermute | solution.py:341
  170.3 48.9 %collective-permute-start.18 = (bf16[128,4096]{1,0:T(8,128)(2,1)}, bf16[128,4096]{1,0:T(8,128)(2,1)}, u32[]{:S(2)}, u32[]{:S(2)}) collective-permute-start(bf16[128,4096]{1,0:T(8,128)(2,1)} %collective-permute-done.16), channel_id=1, source_target_pairs={{8,0},{0,8},{9,1},{1,9},{10,2},{2,10},{11,3},{3,11},{12,4},{4,12},... | collective-permute-start | bytes 3145736 | tf_op jit(solution)/shard_map/ppermute | solution.py:341
  206.5 598.0 %reduce-scatter.6.cloned.1.call-start = ((), (), s32[]{:S(2)}) async-start(), calls=%async_computation.10 | async-start | bytes 7208960 | tf_op jit(solution)/shard_map/reduce_scatter | solution.py:432
  214.2 46.3 %collective-permute-start.12 = (bf16[512,2048]{1,0:T(8,128)(2,1)}, bf16[512,2048]{1,0:T(8,128)(2,1)}, u32[]{:S(2)}, u32[]{:S(2)}) collective-permute-start(bf16[512,2048]{1,0:T(8,128)(2,1)} %all-gather.8.cloned.1.call-done), channel_id=1, source_target_pairs={{1,0},{0,1},{3,2},{2,3},{5,4},{4,5},{7,6},{6,7},{9,8},{8,9},{11,10... | collective-permute-start | bytes 6291464 | tf_op jit(solution)/shard_map/ppermute | solution.py:341
  215.9 69.3 %collective-permute-start.13 = (bf16[512,2048]{1,0:T(8,128)(2,1)}, bf16[512,2048]{1,0:T(8,128)(2,1)}, u32[]{:S(2)}, u32[]{:S(2)}) collective-permute-start(bf16[512,2048]{1,0:T(8,128)(2,1)} %all-gather.8.cloned.1.call-done), channel_id=1, source_target_pairs={{16,0},{0,16},{17,1},{1,17},{18,2},{2,18},{19,3},{3,19},{20,4},{4,... | collective-permute-start | bytes 6291464 | tf_op jit(solution)/shard_map/ppermute | solution.py:341
  217.1 121.1 %collective-permute-start.23 = (bf16[512,2048]{1,0:T(8,128)(2,1)}, bf16[512,2048]{1,0:T(8,128)(2,1)}, u32[]{:S(2)}, u32[]{:S(2)}) collective-permute-start(bf16[512,2048]{1,0:T(8,128)(2,1)} %all-gather.8.cloned.1.call-done), channel_id=1, source_target_pairs={{8,0},{0,8},{9,1},{1,9},{10,2},{2,10},{11,3},{3,11},{12,4},{4,12},... | collective-permute-start | bytes 6291464 | tf_op jit(solution)/shard_map/ppermute | solution.py:341
  219.2 63.7 %collective-permute-start.22 = (bf16[4,256,512]{2,1,0:T(8,128)(2,1)S(1)}, bf16[4,256,512]{2,1,0:T(8,128)(2,1)S(1)}, u32[]{:S(2)}, u32[]{:S(2)}) collective-permute-start(bf16[4,256,512]{2,1,0:T(8,128)(2,1)S(1)} %pad_maximum_fusion.4), channel_id=1, source_target_pairs={{1,0},{0,1},{3,2},{2,3},{5,4},{4,5},{7,6},{6,7},{9,8},{8,9},{11,10... | collective-permute-start | bytes 3145736 | tf_op jit(solution)/shard_map/ppermute | solution.py:341
  260.5 44.4 %collective-permute-start.25 = (bf16[512,2048]{1,0:T(8,128)(2,1)}, bf16[512,2048]{1,0:T(8,128)(2,1)}, u32[]{:S(2)}, u32[]{:S(2)}) collective-permute-start(bf16[512,2048]{1,0:T(8,128)(2,1)} %collective-permute-done.12), channel_id=1, source_target_pairs={{16,0},{0,16},{17,1},{1,17},{18,2},{2,18},{19,3},{3,19},{20,4},{4,... | collective-permute-start | bytes 6291464 | tf_op jit(solution)/shard_map/ppermute | solution.py:341
  283.0 55.2 %collective-permute-start.26 = (bf16[512,2048]{1,0:T(8,128)(2,1)}, bf16[512,2048]{1,0:T(8,128)(2,1)}, u32[]{:S(2)}, u32[]{:S(2)}) collective-permute-start(bf16[512,2048]{1,0:T(8,128)(2,1)} %collective-permute-done.12), channel_id=1, source_target_pairs={{8,0},{0,8},{9,1},{1,9},{10,2},{2,10},{11,3},{3,11},{12,4},{4,12},... | collective-permute-start | bytes 6291464 | tf_op jit(solution)/shard_map/ppermute | solution.py:341
  285.1 53.1 %collective-permute-start.24 = (bf16[512,2048]{1,0:T(8,128)(2,1)}, bf16[512,2048]{1,0:T(8,128)(2,1)}, u32[]{:S(2)}, u32[]{:S(2)}) collective-permute-start(bf16[512,2048]{1,0:T(8,128)(2,1)} %collective-permute-done.13), channel_id=1, source_target_pairs={{8,0},{0,8},{9,1},{1,9},{10,2},{2,10},{11,3},{3,11},{12,4},{4,12},... | collective-permute-start | bytes 6291464 | tf_op jit(solution)/shard_map/ppermute | solution.py:341
  337.4 64.4 %collective-permute-start.31 = (bf16[1024,1408]{0,1:T(8,128)(2,1)}, bf16[1024,1408]{0,1:T(8,128)(2,1)}, u32[]{:S(2)}, u32[]{:S(2)}) collective-permute-start(bf16[1024,1408]{0,1:T(8,128)(2,1)} %all-gather.10.cloned.1.call-done), channel_id=1, source_target_pairs={{1,0},{0,1},{3,2},{2,3},{5,4},{4,5},{7,6},{6,7},{9,8},{8,9},{11,10... | collective-permute-start | bytes 8650760 | tf_op jit(solution)/shard_map/ppermute | solution.py:341
  363.8 48.1 %collective-permute-start.28 = (bf16[256,2048]{1,0:T(8,128)(2,1)}, bf16[256,2048]{1,0:T(8,128)(2,1)}, u32[]{:S(2)}, u32[]{:S(2)}) collective-permute-start(bf16[256,2048]{1,0:T(8,128)(2,1)} %multiply_convert_fusion.3), channel_id=1, source_target_pairs={{16,0},{0,16},{17,1},{1,17},{18,2},{2,18},{19,3},{3,19},{20,4},{4,... | collective-permute-start | bytes 3145736 | tf_op jit(solution)/shard_map/ppermute | solution.py:341
  365.0 47.4 %collective-permute-start.34 = (bf16[256,2048]{1,0:T(8,128)(2,1)}, bf16[256,2048]{1,0:T(8,128)(2,1)}, u32[]{:S(2)}, u32[]{:S(2)}) collective-permute-start(bf16[256,2048]{1,0:T(8,128)(2,1)} %fusion.33), channel_id=1, source_target_pairs={{16,0},{0,16},{17,1},{1,17},{18,2},{2,18},{19,3},{3,19},{20,4},{4,... | collective-permute-start | bytes 3145736 | tf_op jit(solution)/shard_map/ppermute | solution.py:341
  420.2 63.9 %collective-permute-start.32 = (bf16[1024,1408]{0,1:T(8,128)(2,1)}, bf16[1024,1408]{0,1:T(8,128)(2,1)}, u32[]{:S(2)}, u32[]{:S(2)}) collective-permute-start(bf16[1024,1408]{0,1:T(8,128)(2,1)} %all-gather.12.cloned.1.call-done), channel_id=1, source_target_pairs={{1,0},{0,1},{3,2},{2,3},{5,4},{4,5},{7,6},{6,7},{9,8},{8,9},{11,10... | collective-permute-start | bytes 8650760 | tf_op jit(solution)/shard_map/ppermute | solution.py:341
  428.7 40.9 %collective-permute-start.37 = (bf16[256,1024]{1,0:T(8,128)(2,1)S(1)}, bf16[256,1024]{1,0:T(8,128)(2,1)S(1)}, u32[]{:S(2)}, u32[]{:S(2)}) collective-permute-start(bf16[256,1024]{1,0:T(8,128)(2,1)S(1)} %fusion.40.input_ref), channel_id=1, source_target_pairs={{16,0},{0,16},{17,1},{1,17},{18,2},{2,18},{19,3},{3,19},{20,4},{4,... | collective-permute-start | bytes 1572872 | tf_op jit(solution)/shard_map/ppermute | solution.py:341
  429.9 40.5 %collective-permute-start.38 = (bf16[256,1024]{1,0:T(8,128)(2,1)S(1)}, bf16[256,1024]{1,0:T(8,128)(2,1)}, u32[]{:S(2)}, u32[]{:S(2)}) collective-permute-start(bf16[256,1024]{1,0:T(8,128)(2,1)S(1)} %fusion.40.input_ref), channel_id=1, source_target_pairs={{8,0},{0,8},{9,1},{1,9},{10,2},{2,10},{11,3},{3,11},{12,4},{4,12},... | collective-permute-start | bytes 1572872 | tf_op jit(solution)/shard_map/ppermute | solution.py:341
  469.5 53.1 %collective-permute-start.39 = (bf16[256,1024]{1,0:T(8,128)(2,1)S(1)}, bf16[256,1024]{1,0:T(8,128)(2,1)}, u32[]{:S(2)}, u32[]{:S(2)}) collective-permute-start(bf16[256,1024]{1,0:T(8,128)(2,1)S(1)} %collective-permute-done.37), channel_id=1, source_target_pairs={{8,0},{0,8},{9,1},{1,9},{10,2},{2,10},{11,3},{3,11},{12,4},{4,12},... | collective-permute-start | bytes 1572872 | tf_op jit(solution)/shard_map/ppermute | solution.py:341
  522.6 489.7 %reduce-scatter.14.cloned.1.call-start = ((), (), s32[]{:S(2)}) async-start(), calls=%async_computation.14 | async-start | bytes 3604480 | tf_op jit(solution)/shard_map/reduce_scatter | solution.py:432
  576.5 80.5 %collective-permute-start.52 = (bf16[4,256,1408]{2,1,0:T(8,128)(2,1)}, bf16[4,256,1408]{2,1,0:T(8,128)(2,1)}, u32[]{:S(2)}, u32[]{:S(2)}) collective-permute-start(bf16[4,256,1408]{2,1,0:T(8,128)(2,1)} %dynamic-slice_bitcast_fusion.1), channel_id=1, source_target_pairs={{0,1},{1,0},{2,3},{3,2},{4,5},{5,4},{6,7},{7,6},{8,9},{9,8},{10,11... | collective-permute-start | bytes 8650760 | tf_op jit(solution)/shard_map/ppermute | solution.py:346
  605.7 56.1 %collective-permute-start.49 = (bf16[256,2048]{1,0:T(8,128)(2,1)}, bf16[256,2048]{1,0:T(8,128)(2,1)}, u32[]{:S(2)}, u32[]{:S(2)}) collective-permute-start(bf16[256,2048]{1,0:T(8,128)(2,1)} %get-tuple-element.193), channel_id=1, source_target_pairs={{16,0},{0,16},{17,1},{1,17},{18,2},{2,18},{19,3},{3,19},{20,4},{4,... | collective-permute-start | bytes 3145736 | tf_op jit(solution)/shard_map/ppermute | solution.py:341
  606.9 170.6 %collective-permute-start.50 = (bf16[256,2048]{1,0:T(8,128)(2,1)}, bf16[256,2048]{1,0:T(8,128)(2,1)}, u32[]{:S(2)}, u32[]{:S(2)}) collective-permute-start(bf16[256,2048]{1,0:T(8,128)(2,1)} %get-tuple-element.193), channel_id=1, source_target_pairs={{8,0},{0,8},{9,1},{1,9},{10,2},{2,10},{11,3},{3,11},{12,4},{4,12},... | collective-permute-start | bytes 3145736 | tf_op jit(solution)/shard_map/ppermute | solution.py:341
  661.7 367.1 %reduce-scatter.12.cloned.1.call-start = ((), (), s32[]{:S(2)}) async-start(), calls=%async_computation.13 | async-start | bytes 3604480 | tf_op jit(solution)/shard_map/reduce_scatter | solution.py:432
  661.8 63.6 %collective-permute-start.46 = (bf16[256,1024]{1,0:T(8,128)(2,1)}, bf16[256,1024]{1,0:T(8,128)(2,1)S(1)}, u32[]{:S(2)}, u32[]{:S(2)}) collective-permute-start(bf16[256,1024]{1,0:T(8,128)(2,1)} %get-tuple-element.222), channel_id=1, source_target_pairs={{16,0},{24,8},{0,16},{8,24},{17,1},{25,9},{1,17},{9,25},{18,2},{26... | collective-permute-start | bytes 1572872 | tf_op jit(solution)/shard_map/ppermute | solution.py:379
  674.1 103.7 %collective-permute-start.51 = (bf16[256,2048]{1,0:T(8,128)(2,1)}, bf16[256,2048]{1,0:T(8,128)(2,1)S(1)}, u32[]{:S(2)}, u32[]{:S(2)}) collective-permute-start(bf16[256,2048]{1,0:T(8,128)(2,1)} %collective-permute-done.49), channel_id=1, source_target_pairs={{8,0},{0,8},{9,1},{1,9},{10,2},{2,10},{11,3},{3,11},{12,4},{4,12},... | collective-permute-start | bytes 3145736 | tf_op jit(solution)/shard_map/ppermute | solution.py:341
  675.9 57.5 %collective-permute-start.59 = (bf16[256,512]{1,0:T(8,128)(2,1)S(1)}, bf16[256,512]{1,0:T(8,128)(2,1)S(1)}, u32[]{:S(2)}, u32[]{:S(2)}) collective-permute-start(bf16[256,512]{1,0:T(8,128)(2,1)S(1)} %get-tuple-element.244), channel_id=1, source_target_pairs={{0,6},{2,0},{4,2},{6,4},{1,7},{3,1},{5,3},{7,5},{8,14},{10,8},{12,... | collective-permute-start | bytes 786440 | tf_op jit(solution)/shard_map/ppermute | solution.py:346
  676.0 79.5 %collective-permute-start.58 = (bf16[256,512]{1,0:T(8,128)(2,1)S(1)}, bf16[256,512]{1,0:T(8,128)(2,1)S(1)}, u32[]{:S(2)}, u32[]{:S(2)}) collective-permute-start(bf16[256,512]{1,0:T(8,128)(2,1)S(1)} %get-tuple-element.245), channel_id=1, source_target_pairs={{0,4},{2,6},{4,0},{6,2},{1,5},{3,7},{5,1},{7,3},{8,12},{10,14},{12... | collective-permute-start | bytes 786440 | tf_op jit(solution)/shard_map/ppermute | solution.py:346
  725.4 50.8 %collective-permute-start.57 = (bf16[256,512]{1,0:T(8,128)(2,1)S(1)}, bf16[256,512]{1,0:T(8,128)(2,1)S(1)}, u32[]{:S(2)}, u32[]{:S(2)}) collective-permute-start(bf16[256,512]{1,0:T(8,128)(2,1)S(1)} %get-tuple-element.243), channel_id=1, source_target_pairs={{0,2},{2,4},{4,6},{6,0},{1,3},{3,5},{5,7},{7,1},{8,10},{10,12},{12... | collective-permute-start | bytes 786440 | tf_op jit(solution)/shard_map/ppermute | solution.py:346
  733.4 47.0 %collective-permute-start.42 = (bf16[256,1024]{0,1:T(8,128)(2,1)S(1)}, bf16[256,1024]{0,1:T(8,128)(2,1)S(1)}, u32[]{:S(2)}, u32[]{:S(2)}) collective-permute-start(bf16[256,1024]{0,1:T(8,128)(2,1)S(1)} %bitcast.272), channel_id=1, source_target_pairs={{24,0},{16,8},{8,16},{0,24},{25,1},{17,9},{9,17},{1,25},{26,2},{18... | collective-permute-start | bytes 1572872 | tf_op jit(solution)/shard_map/ppermute | solution.py:379
  777.6 63.7 %collective-permute-start.75 = (bf16[4,256,1408]{2,1,0:T(8,128)(2,1)}, bf16[4,256,1408]{2,1,0:T(8,128)(2,1)}, u32[]{:S(2)}, u32[]{:S(2)}) collective-permute-start(bf16[4,256,1408]{2,1,0:T(8,128)(2,1)} %dynamic-slice_bitcast_fusion), channel_id=1, source_target_pairs={{0,1},{1,0},{2,3},{3,2},{4,5},{5,4},{6,7},{7,6},{8,9},{9,8},{10,11... | collective-permute-start | bytes 8650760 | tf_op jit(solution)/shard_map/ppermute | solution.py:346
  846.3 182.6 %reduce-scatter.10.cloned.1.call-start = ((), (), s32[]{:S(2)}) async-start(), calls=%async_computation.12 | async-start | bytes 2621440 | tf_op jit(solution)/shard_map/reduce_scatter | solution.py:432
  848.2 45.8 %collective-permute-start.74 = (bf16[4,128,2048]{2,1,0:T(8,128)(2,1)S(1)}, bf16[4,128,2048]{2,1,0:T(8,128)(2,1)S(1)}, u32[]{:S(2)}, u32[]{:S(2)}) collective-permute-start(bf16[4,128,2048]{2,1,0:T(8,128)(2,1)S(1)} %dynamic-slice_bitcast_fusion.2), channel_id=1, source_target_pairs={{0,1},{1,0},{2,3},{3,2},{4,5},{5,4},{6,7},{7,6},{8,9},{9,8},{10,11... | collective-permute-start | bytes 6291464 | tf_op jit(solution)/shard_map/ppermute | solution.py:346
  852.9 45.7 %collective-permute-start.54 = (bf16[256,2048]{1,0:T(8,128)(2,1)S(1)}, bf16[256,2048]{1,0:T(8,128)(2,1)}, u32[]{:S(2)}, u32[]{:S(2)}) collective-permute-start(bf16[256,2048]{1,0:T(8,128)(2,1)S(1)} %get-tuple-element.200), channel_id=1, source_target_pairs={{0,8},{8,0},{1,9},{9,1},{2,10},{10,2},{3,11},{11,3},{4,12},{12,4},... | collective-permute-start | bytes 3145736 | tf_op jit(solution)/shard_map/ppermute | solution.py:346
  896.1 132.8 %reduce-scatter.8.cloned.1.call-start = ((), (), s32[]{:S(2)}) async-start(), calls=%async_computation.11 | async-start | bytes 1310720 | tf_op jit(solution)/shard_map/reduce_scatter | solution.py:432
  905.7 41.6 %collective-permute-start.73 = (bf16[4,128,1024]{2,1,0:T(8,128)(2,1)}, bf16[4,128,1024]{2,1,0:T(8,128)(2,1)}, u32[]{:S(2)}, u32[]{:S(2)}) collective-permute-start(bf16[4,128,1024]{2,1,0:T(8,128)(2,1)} %dynamic-slice_bitcast_fusion.3), channel_id=1, source_target_pairs={{0,1},{1,0},{2,3},{3,2},{4,5},{5,4},{6,7},{7,6},{8,9},{9,8},{10,11... | collective-permute-start | bytes 3145736 | tf_op jit(solution)/shard_map/ppermute | solution.py:346
  938.9 50.7 %collective-permute-start.64 = (bf16[256,2048]{1,0:T(8,128)(2,1)}, bf16[256,2048]{1,0:T(8,128)(2,1)S(1)}, u32[]{:S(2)}, u32[]{:S(2)}) collective-permute-start(bf16[256,2048]{1,0:T(8,128)(2,1)} %get-tuple-element.198), channel_id=1, source_target_pairs={{0,8},{8,0},{1,9},{9,1},{2,10},{10,2},{3,11},{11,3},{4,12},{12,4},... | collective-permute-start | bytes 3145736 | tf_op jit(solution)/shard_map/ppermute | solution.py:346
  940.3 74.0 %collective-permute-start.63 = (bf16[256,2048]{1,0:T(8,128)(2,1)}, bf16[256,2048]{1,0:T(8,128)(2,1)S(1)}, u32[]{:S(2)}, u32[]{:S(2)}) collective-permute-start(bf16[256,2048]{1,0:T(8,128)(2,1)} %get-tuple-element.197), channel_id=1, source_target_pairs={{0,8},{8,0},{1,9},{9,1},{2,10},{10,2},{3,11},{11,3},{4,12},{12,4},... | collective-permute-start | bytes 3145736 | tf_op jit(solution)/shard_map/ppermute | solution.py:346
  1034.5 49.2 %collective-permute-start.84 = (bf16[128,2048]{1,0:T(8,128)(2,1)}, bf16[128,2048]{1,0:T(8,128)(2,1)S(1)}, u32[]{:S(2)}, u32[]{:S(2)}) collective-permute-start(bf16[128,2048]{1,0:T(8,128)(2,1)} %reduce-scatter.10.cloned.1.call-done), channel_id=1, source_target_pairs={{8,0},{0,8},{9,1},{1,9},{10,2},{2,10},{11,3},{3,11},{12,4},{4,12},... | collective-permute-start | bytes 1572872 | tf_op jit(solution)/shard_map/ppermute | solution.py:341
  1036.8 42.5 %collective-permute-start.86 = (bf16[256,2816]{1,0:T(8,128)(2,1)}, bf16[256,2816]{1,0:T(8,128)(2,1)S(1)}, u32[]{:S(2)}, u32[]{:S(2)}) collective-permute-start(bf16[256,2816]{1,0:T(8,128)(2,1)} %constant_dynamic-update-slice_fusion.10.refs_3_), channel_id=1, source_target_pairs={{16,0},{0,16},{17,1},{1,17},{18,2},{2,18},{19,3},{3,19},{20,4},{4,... | collective-permute-start | bytes 4325384 | tf_op jit(solution)/shard_map/ppermute | solution.py:341
  1042.4 43.4 %collective-permute-start.87 = (bf16[256,2816]{1,0:T(8,128)(2,1)S(1)}, bf16[256,2816]{1,0:T(8,128)(2,1)S(1)}, u32[]{:S(2)}, u32[]{:S(2)}) collective-permute-start(bf16[256,2816]{1,0:T(8,128)(2,1)S(1)} %copy-done.29), channel_id=1, source_target_pairs={{8,0},{0,8},{9,1},{1,9},{10,2},{2,10},{11,3},{3,11},{12,4},{4,12},... | collective-permute-start | bytes 4325384 | tf_op jit(solution)/shard_map/ppermute | solution.py:341
  (124 other events, 2096.9 us)
Sparse Core Ops, SparseCore 0:
  12.3 41.8 all-gather.5
  56.3 44.5 all-gather.7
  103.0 62.5 all-gather.9
  167.0 67.3 all-gather.11
  235.8 107.4 all-gather.13
  522.7 133.2 reduce-scatter.5
  661.9 123.8 reduce-scatter.13
  846.4 57.1 reduce-scatter.11
  905.9 41.9 reduce-scatter.9
  950.6 30.2 reduce-scatter.7

commit v2 on v1

--- a/solution.py
+++ b/solution.py
@@ -64,6 +64,7 @@
 
 
 STEP_HEADS = 2
+LIGHT = 1000
 NEG = -1e30
 
 
@@ -138,7 +139,6 @@
     wide = STEP_HEADS * HD
     whole = lambda h, *_: (0, 0)
     by_head = lambda h, *_: (0, h)
-    flops = 2 * rows * HEADS * HD * (rank + 2 * slot_len)
     return pl.pallas_call(
         attend_kernel,
         out_shape=(
@@ -172,9 +172,7 @@
             dimension_semantics=("arbitrary",), vmem_limit_bytes=40 * 1024 * 1024
         ),
         cost_estimate=pl.CostEstimate(
-            flops=flops,
-            bytes_accessed=2 * (rank + 3 * rows) * HEADS * HD,
-            transcendentals=rows * HEADS * slot_len,
+            flops=LIGHT, bytes_accessed=LIGHT, transcendentals=0
         ),
     )(place, query_input, up_mat, cosine, sine, kv_whole)
 
@@ -269,32 +267,30 @@
             dimension_semantics=("arbitrary",), vmem_limit_bytes=40 * 1024 * 1024
         ),
         cost_estimate=pl.CostEstimate(
-            flops=10 * rows * HEADS * HD * slot_len,
-            bytes_accessed=2 * 4 * rows * HEADS * HD,
-            transcendentals=rows * HEADS * slot_len,
+            flops=LIGHT, bytes_accessed=LIGHT, transcendentals=0
         ),
     )(place, query, out_grad, attn_low, logsum, cosine, sine, kv_whole)
 
 
 def interleave_kernel(n_shard, order_ref, gain_ref, weight_ref, *refs):
     *slot_refs, out_ref, sum_ref = refs
-    n_group = len(slot_refs)
-    slots = [ref[...].astype(F32) for ref in slot_refs]
-    part = slots[0].shape[1] // 2
+    n_group = len(slot_refs) // 2
+    part = slot_refs[0].shape[1]
     unit = part // n_shard
     width = part * n_group
-    blocks = []
-    for member in range(n_group):
-        block = slots[0]
-        for k in range(1, n_group):
-            block = jnp.where(order_ref[member] == k, slots[k], block)
-        blocks.append(block)
     total = 0.0
     gain = gain_ref[...]
     for half in range(2):
+        slots = [ref[...].astype(F32) for ref in slot_refs[half * n_group : (half + 1) * n_group]]
+        blocks = []
+        for member in range(n_group):
+            block = slots[0]
+            for k in range(1, n_group):
+                block = jnp.where(order_ref[member] == k, slots[k], block)
+            blocks.append(block)
         row = jnp.concatenate(
             [
-                blocks[member][:, half * part + s * unit : half * part + (s + 1) * unit]
+                blocks[member][:, s * unit : (s + 1) * unit]
                 for s in range(n_shard)
                 for member in range(n_group)
             ],
@@ -306,9 +302,10 @@
     sum_ref[...] = total
 
 
-def interleave(order, gain, weight, slots, n_shard):
+def interleave(order, gain, weight, gate_slots, up_slots, n_shard):
     rows, width = weight.shape
     block = 32
+    slots = [*gate_slots, *up_slots]
     by_row = lambda i, *_: (i, 0)
     return pl.pallas_call(
         lambda *refs: interleave_kernel(n_shard, *refs),
@@ -330,10 +327,46 @@
             ],
         ),
         compiler_params=pltpu.CompilerParams(dimension_semantics=("arbitrary",)),
-        cost_estimate=pl.CostEstimate(
-            flops=4 * rows * width, bytes_accessed=8 * rows * width, transcendentals=0
-        ),
+        cost_estimate=pl.CostEstimate(flops=LIGHT, bytes_accessed=LIGHT, transcendentals=0),
     )(order, gain, weight, *slots)
+
+
+def select_kernel(n_shard, n_group, member_ref, gain_ref, weight_ref, gate_ref, up_ref):
+    width = weight_ref.shape[1] // 2
+    unit = width // n_shard // n_group
+    gain = gain_ref[...]
+    for half, out_ref in enumerate((gate_ref, up_ref)):
+        pieces = []
+        for s in range(n_shard):
+            at = half * width + s * n_group * unit
+            piece = weight_ref[:, at : at + unit].astype(F32)
+            for k in range(1, n_group):
+                other = weight_ref[:, at + k * unit : at + (k + 1) * unit].astype(F32)
+                piece = jnp.where(member_ref[0] == k, other, piece)
+            pieces.append(piece)
+        out_ref[...] = (jnp.concatenate(pieces, axis=1) * gain).astype(BF)
+
+
+def select_units(member, gain, weight, n_shard, n_group):
+    rows, width = weight.shape
+    block = 32
+    part = width // 2 // n_group
+    by_row = lambda i, *_: (i, 0)
+    return pl.pallas_call(
+        lambda *refs: select_kernel(n_shard, n_group, *refs),
+        out_shape=(jax.ShapeDtypeStruct((rows, part), BF),) * 2,
+        grid_spec=pltpu.PrefetchScalarGridSpec(
+            num_scalar_prefetch=1,
+            grid=(rows // block,),
+            in_specs=[
+                pl.BlockSpec((block, 1), by_row),
+                pl.BlockSpec((block, width), by_row),
+            ],
+            out_specs=[pl.BlockSpec((block, part), by_row)] * 2,
+        ),
+        compiler_params=pltpu.CompilerParams(dimension_semantics=("arbitrary",)),
+        cost_estimate=pl.CostEstimate(flops=LIGHT, bytes_accessed=LIGHT, transcendentals=0),
+    )(member, gain, weight)
 
 
 def from_ahead(value, axis, step):
@@ -404,16 +437,23 @@
     return [from_ahead(value, "z", k) if k else value for k in range(Z)]
 
 
-def scatter_small(blocks):
-    near = blocks[0]
-    total = jnp.stack(near).astype(F32)
+def small_over_y(blocks):
+    total = jnp.stack(blocks[0]).astype(F32)
     for k, group in enumerate(blocks[1:]):
         total = total + to_ahead(jnp.stack(group).astype(BF), "y", k + 1).astype(F32)
-    out = total[0]
+    return total
+
+
+def small_over_z(total):
     low = total.astype(BF)
-    for k in range(1, Z):
-        out = out + to_ahead(low[k], "z", k).astype(F32)
-    return out
+    return [total[0]] + [to_ahead(low[k], "z", k) for k in range(1, Z)]
+
+
+def added(blocks):
+    total = blocks[0]
+    for block in blocks[1:]:
+        total = total + block.astype(F32)
+    return total
 
 
 def after(values, done):
@@ -589,10 +629,9 @@
 
     qkv_own = jnp.concatenate([query_down, key_value], axis=1)
     qkv_ring = ring_z(scaled(pick_cols(qkv_own, group_id), attn_gain))
-    qup_wide = gather_z(quarter_rows(scaled(query_up, query_gain)))
+    qup_own = quarter_rows(scaled(query_up, query_gain))
+    qup_mat = lax.all_gather(qup_own, ("z", "y", "x", "c"), axis=0, tiled=True)
     out_wide = gather_z(quarter_rows(out_proj))
-    unit = FF // n_shard // n_group
-    part = FF // n_group
 
     my_length = lax.dynamic_index_in_dim(lengths, group_id, keepdims=False)
     positions = shard_id * rows + jnp.arange(rows, dtype=jnp.int32)
@@ -609,16 +648,18 @@
     qkv_stack = jnp.stack(qkv_ring)
     qkv_grid = [qkv_stack] + [from_ahead(qkv_stack, "y", k) for k in range(1, n_y)]
 
-    gate_up_late = after(gate_up, qkv_stack)
-    gu_parts = gate_up_late.reshape(gate_up.shape[0], 2, n_shard, n_group, unit)
-    gu_own = lax.dynamic_index_in_dim(gu_parts, group_id, axis=3, keepdims=False)
-    gu_own = scaled(gu_own.reshape(-1, 2 * part), mlp_gain)
-    gate_own, up_own = gu_own[:, :part], gu_own[:, part:]
+    gate_up_late = after(gate_up, qkv_ring[1])
+    gate_own, up_own = select_units(
+        group_id.astype(jnp.int32).reshape(1),
+        mlp_gain.astype(F32)[:, None],
+        gate_up_late,
+        n_shard,
+        n_group,
+    )
     gate_wide = gather_z(gate_own)
 
-    qup_first = spread_begin(qup_wide)
     qkv_mat = jnp.zeros((width, qkv_stack.shape[2]), BF)
-    for dy, stack in enumerate(after(qkv_grid, qup_wide)):
+    for dy, stack in enumerate(qkv_grid):
         for dz in range(Z):
             at = position_of(dz, dy) * stack.shape[1]
             qkv_mat = lax.dynamic_update_slice(qkv_mat, stack[dz], (at, 0))
@@ -634,8 +675,6 @@
                     perm.append((j * CORES + c, target))
             block = lax.ppermute(block, ("x", "c"), perm)
         blocks.append(block)
-    qup_grid = spread_next(*qup_first)
-    blocks = after(blocks, qup_first)
     qkv_out = jnp.zeros((rows, qkv_own.shape[1]), F32)
     n_cols = qkv_own.shape[1] // n_group
     for (dc, dx), block in zip(offsets(), blocks):
@@ -655,46 +694,45 @@
     rms_query = inv_rms(qdown_out)
     normed_query = qdown_out * rms_query
     query_input = normed_query.astype(BF)
-    qup_slots = spread_end(qup_grid)
-    kv_stack = jnp.stack(after(kv_ring, qup_grid))
+    kv_stack = jnp.stack(kv_ring)
     kv_grid = [kv_stack] + [from_ahead(kv_stack, "y", k) for k in range(1, n_y)]
-    qup_mat = place_every(after(qup_slots, kv_stack), query_up.shape[0] // n_group)
-    kv_grid = after(kv_grid, qup_mat)
+    kv_grid = after(kv_grid, out_first)
     kv_whole = jnp.concatenate([stack[dz] for dz in range(Z) for stack in kv_grid])
-    query_late = after(query_input, out_first)
     out_grid = spread_next(*out_first)
-    query_rot, attn_low, logsum = attend(place, query_late, qup_mat, cosine, sine, kv_whole)
-    gate_blocks = swap_y(after(gate_wide, attn_low))
-    out_mat = place_every(after(spread_end(out_grid), attn_low), out_proj.shape[0] // n_group)
+    query_rot, attn_low, logsum = attend(place, query_input, qup_mat, cosine, sine, kv_whole)
+    gate_blocks = swap_y(gate_wide)
+    out_slots = spread_end(after(out_grid, attn_low))
+    out_mat = place_every(out_slots, out_proj.shape[0] // n_group)
     middle = x_rows + matmul(attn_low, out_mat)
     rms_second = inv_rms(middle)
     normed_second = middle * rms_second
     mlp_input = normed_second.astype(BF)
 
     mlp_all = jnp.concatenate(gather_group(mlp_input), axis=0)
-    up_blocks = swap_y(after(up_wide, mlp_input))
+    up_blocks = swap_y(up_wide)
     cot_rows = cotangent[0].astype(F32) * valid
     cot_late = after(cot_rows.astype(BF), mlp_input)
     cot_all = jnp.concatenate(gather_group(cot_late), axis=0)
     gate_mat = merge_y(after(gate_blocks, mlp_all), mlp_gain.shape[0])
     gate_part = matmul(mlp_all, gate_mat)
     up_mat = merge_y(after(up_blocks, (gate_part, down_mat)), mlp_gain.shape[0])
+    def pick_out(value, member):
+        parts = value.reshape(rows, n_shard, n_group, -1)
+        return lax.dynamic_index_in_dim(parts, member, axis=2, keepdims=False).reshape(rows, -1)
+
+    attn_late, query_late = after((attn_low, query_input), mlp_all)
+    attn_all = jnp.concatenate(exchange_group(attn_late, pick_out), axis=0)
+    query_all = jnp.concatenate(gather_group(query_late), axis=0)
+
+    up_mat, attn_all, query_all = lax.optimization_barrier((up_mat, attn_all, query_all))
     up_part = matmul(mlp_all, up_mat)
     sigmoid_gate = jax.nn.sigmoid(gate_part)
     activated = gate_part * sigmoid_gate
     hidden_low = (activated * up_part).astype(BF)
 
-    def pick_out(value, member):
-        parts = value.reshape(rows, n_shard, n_group, -1)
-        return lax.dynamic_index_in_dim(parts, member, axis=2, keepdims=False).reshape(rows, -1)
-
-    attn_late, query_late = after((attn_low, query_input), cot_all)
-    attn_all = jnp.concatenate(exchange_group(attn_late, pick_out), axis=0)
-    query_all = jnp.concatenate(gather_group(query_late), axis=0)
-
     down_term = contract_rows(hidden_low, cot_all).astype(BF)
     down_half = scatter_z(down_term)
-    down_mat = after(down_mat, (down_term, attn_all, query_all))
+    down_mat = after(down_mat, down_term)
     hidden_grad = contract_cols(cot_all, down_mat)
     gate_grad = hidden_grad * up_part * (sigmoid_gate * (1.0 + gate_part * (1.0 - sigmoid_gate)))
     gate_low = gate_grad.astype(BF)
@@ -704,7 +742,7 @@
     gate_term = contract_rows(mlp_all, gate_low).astype(BF)
     gate_ends = begin_reduce_y(gate_term)
     up_term = contract_rows(mlp_all, after(up_low, gate_term)).astype(BF)
-    up_ends = begin_reduce_y(up_term)
+    up_half = scatter_z(up_term)
     mlp_in_grad = after(reduce_group(split(partial_in)), up_term)
 
     middle_grad = cot_rows + rms_second * (
@@ -718,29 +756,33 @@
         place, query_rot, attn_val_grad, attn_low, logsum, cosine, sine, kv_whole
     )
     kv_slots = [kv_term[k * rows : (k + 1) * rows] for k in range(Z * n_y)]
-    kv_grad = scatter_small([kv_slots[k::n_y] for k in range(n_y)])
+    kv_near = small_over_y([kv_slots[k::n_y] for k in range(n_y)])
+    kv_blocks = small_over_z(kv_near)
     gate_pre = end_reduce_y(gate_ends[0], after(gate_ends[1], kv_term))
     gate_sum = scatter_z(gate_pre)
     out_term = contract_rows(attn_all, after(middle_all, gate_pre)).astype(BF)
     out_ends = begin_reduce_y(out_term)
+    kv_blocks, out_term = lax.optimization_barrier((kv_blocks, out_term))
+    kv_grad = added(kv_blocks)
     raw_all = jnp.concatenate(exchange_group(query_raw_grad, pick_cols), axis=0)
     query_in_grad = contract_cols(query_raw_grad, qup_mat)
     qup_term = contract_rows(query_all, raw_all).astype(BF)
-    qup_ends = begin_reduce_y(qup_term)
-    hidden_late = after(hidden_low, (qup_term, out_term))
-    layer_part = matmul(hidden_late, down_mat)
-    layer = (middle + reduce_group(split(layer_part))) * valid
     qdown_grad = rms_query * (
         query_in_grad
         - normed_query * jnp.mean(query_in_grad * normed_query, axis=-1, keepdims=True)
     )
-    kv_grad = after(kv_grad, down_half)
+    kv_grad, qup_term = lax.optimization_barrier((kv_grad, qup_term))
     key_raw_grad = rotate_back(kv_grad[:, :HD], cosine, sine)
     qkv_low = jnp.concatenate([qdown_grad, key_raw_grad, kv_grad[:, HD:]], axis=1).astype(BF)
-    qkv_all = jnp.concatenate(exchange_group(qkv_low, pick_cols), axis=0)
+    qkv_parts, out_ends = lax.optimization_barrier(
+        (exchange_group(qkv_low, pick_cols), out_ends)
+    )
+    out_pre = end_reduce_y(*out_ends)
+    out_sum = scatter_z(out_pre)
+    qkv_all = jnp.concatenate(after(qkv_parts, out_pre), axis=0)
     qkv_term = contract_rows(input_all, qkv_all).astype(BF)
     n_own = query_down.shape[0]
-    qkv_sum = scatter_small(
+    qkv_near = small_over_y(
         [
             [
                 lax.dynamic_slice_in_dim(qkv_term, position_of(dz, dy) * n_own, n_own)
@@ -748,35 +790,46 @@
             ]
             for dy in range(n_y)
         ]
-    ).astype(BF)
-    down_sum = reduce_own_y(down_half)
+    )
     first_part = contract_cols(after(qkv_all, qkv_term), qkv_mat)
-    up_pre = end_reduce_y(up_ends[0], after(up_ends[1], (qkv_low, layer_part)))
-    up_sum = scatter_z(up_pre)
-    out_pre = end_reduce_y(out_ends[0], after(out_ends[1], (up_pre, first_part)))
-    out_sum = scatter_z(out_pre)
-    qup_pre = end_reduce_y(qup_ends[0], after(qup_ends[1], out_pre))
+    first_in_grad = reduce_group(split(first_part))
+    qup_ends = begin_reduce_y(after(qup_term, out_ends))
+    layer_part = matmul(after(hidden_low, first_part), down_mat)
+    down_sum = reduce_own_y(after(down_half, layer_part))
+    up_sum = reduce_own_y(after(up_half, down_half))
+    qup_ends, first_in_grad, layer_part, up_sum = lax.optimization_barrier(
+        (qup_ends, first_in_grad, layer_part, up_sum)
+    )
+    qup_pre = end_reduce_y(*qup_ends)
     qup_sum = scatter_z(qup_pre)
-    first_in_grad = reduce_group(split(first_part))
+    layer_sum = reduce_group(split(layer_part))
+    up_slots = gather_group(up_sum)
+    gate_slots = gather_group(after(gate_sum, up_sum))
+    down_slots = gather_group(down_sum)
+    qkv_blocks = small_over_z(qkv_near)
+    qkv_blocks, up_slots, gate_slots = lax.optimization_barrier(
+        (qkv_blocks, up_slots, gate_slots)
+    )
     input_rows_grad = middle_grad + rms_first * (
         first_in_grad
         - normed_first * jnp.mean(first_in_grad * normed_first, axis=-1, keepdims=True)
     )
-
-    down_grad = place_group(gather_group(down_sum), 0, F32)
-    gate_sum = after(gate_sum, down_grad)
-    up_sum = after(up_sum, gate_sum)
-    gateup_slots = gather_group(jnp.concatenate([gate_sum, up_sum], axis=1))
-    out_sum = after(out_sum, up_sum)
-    out_grad = place_group(gather_group(out_sum), 0, F32)
-    qup_sum = after(qup_sum, out_sum)
     order = jnp.zeros((n_group,), jnp.int32)
     for k, (dc, dx) in enumerate(offsets()):
         order = order.at[member_of(dc, dx)].set(k)
     gateup_grad, second_gain_grad = interleave(
-        order, mlp_gain.astype(F32)[:, None], gate_up, gateup_slots, n_shard
-    )
-    qup_raw = place_group(gather_group(qup_sum), 1, F32)
+        order, mlp_gain.astype(F32)[:, None], gate_up, gate_slots, up_slots, n_shard
+    )
+    qkv_blocks, gateup_grad, layer_sum, down_slots = lax.optimization_barrier(
+        (qkv_blocks, gateup_grad, layer_sum, down_slots)
+    )
+    qkv_sum = added(qkv_blocks).astype(BF)
+    layer = (middle + layer_sum) * valid
+    out_slots = gather_group(after(out_sum, gate_slots))
+
+    down_grad = place_group(down_slots, 0, F32)
+    out_grad = place_group(out_slots, 0, F32)
+    qup_raw = place_group(gather_group(after(qup_sum, out_slots)), 1, F32)
     qkv_raw = place_group(gather_group(qkv_sum), 1, F32)
 
     def gain_grad(weight, grad):

time: 1120 us -> 907 us (0.81)
  waiting for transfers between devices: 479 us -> 317 us
  starting transfers between devices: 142 us -> 97.9 us
  local copies, waits for them, and re-layouts: 169 us -> 126 us
  other arithmetic: 89.7 us -> 106 us
    ppermute x55 -> x51, waiting for transfers between devices: 265 us -> 180 us  [from_ahead(): return lax.ppermute(value, axis, [((j + step) % n, j) for j in range(n)])]
    ppermute x22, waiting for transfers between devices: 171 us -> 104 us  [to_ahead(): return lax.ppermute(value, axis, [(j, (j + step) % n) for j in range(n)])]
    ppermute x22, starting transfers between devices: 67.9 us -> 36.1 us  [to_ahead(): return lax.ppermute(value, axis, [(j, (j + step) % n) for j in range(n)])]
    reshape x4 -> x0, local copies, waits for them, and re-layouts: 18.4 us -> none  [merge_y(): blocks = [block.reshape(Z, 1, n, m) for block in blocks]]
    ppermute x55 -> x51, starting transfers between devices: 62.3 us -> 47.3 us  [from_ahead(): return lax.ppermute(value, axis, [((j + step) % n, j) for j in range(n)])]
    pallas_call x0 -> x1, Pallas kernels: none -> 12.3 us  [select_units(): pl.pallas_call(lambda *refs: select_kernel(n_shard, n_group, *refs), out_...]
    dynamic_update_slice x16 -> x8, local copies, waits for them, and re-layouts: 25.8 us -> 13.7 us  [place_every(): lax.dynamic_update_slice(out, slot.reshape(Z, 1, 1, n, m), (0, at_y, memb...]
    unnamed x165 -> x178, local copies, waits for them, and re-layouts: 44.1 us -> 51.1 us
  transfers between devices with their start and end apart: 99 -> 95, of which waited for: 31 -> 30; matrix products, arithmetic and copies ran while one was open for 35% -> 38% of each run, Pallas kernels for 4% -> 8%
where the time goes in v2:
time: 907 us; the launch traced here: 896 us
  waiting for transfers between devices  317 us (35%)
  matrix products  161 us (18%)
  local copies, waits for them, and re-layouts  126 us (14%)
  other arithmetic  106 us (12%)
  starting transfers between devices  97.9 us (11%)
  Pallas kernels  71.8 us (8%)
  between operations  16 us (2%)
    ppermute x51, waiting for transfers between devices, from_ahead(): return lax.ppermute(value, axis, [((j + step) % n, j) for j in range(n)])  180 us
    ppermute x22, waiting for transfers between devices, to_ahead(): return lax.ppermute(value, axis, [(j, (j + step) % n) for j in range(n)])  104 us
    dot_general x6, matrix products, contract_cols(): lax.dot_general(left, right, (((1,), (1,)), ((), ())), preferred_element_...  68.2 us
    unnamed x178, local copies, waits for them, and re-layouts  51.1 us
    dot_general x5, matrix products, matmul(): return jnp.dot(left, right, preferred_element_type=F32)  48.6 us
    ppermute x51, starting transfers between devices, from_ahead(): return lax.ppermute(value, axis, [((j + step) % n, j) for j in range(n)])  47.3 us
    dot_general x6, matrix products, contract_rows(): lax.dot_general(left, right, (((0,), (0,)), ((), ())), preferred_element_...  44.2 us
    ppermute x22, starting transfers between devices, to_ahead(): return lax.ppermute(value, axis, [(j, (j + step) % n) for j in range(n)])  36.1 us
  transfers between devices with their start and end apart: 95, of which 30 were waited for; matrix products, arithmetic and copies ran while one was open for 38% of the time, Pallas kernels for 8%

profile of v2, /device:TPU:13, one launch (start us, length us, event | category | flops | bytes accessed | tf_op | source)
XLA Modules:
  0.0 896.1 jit_solution(6749098598217358775)
XLA Ops:
  27.8 13.1 %collective-permute-done.3 = bf16[256,384]{1,0:T(8,128)(2,1)S(1)} collective-permute-done((bf16[256,384]{1,0:T(8,128)(2,1)S(1)}, bf16[256,384]{1,0:T(8,128)(2,1)S(1)}, u32[]{:S(2)}, u32[]{:S(2)}) %collective-permute-start.3) | collective-permute-done | bytes 196640 | tf_op jit(solution)/shard_map/ppermute | solution.py:374
  40.9 7.3 collective-permute-done.4
  48.2 14.7 %collective-permute-done.5 = bf16[256,384]{1,0:T(8,128)(2,1)S(1)} collective-permute-done((bf16[256,384]{1,0:T(8,128)(2,1)S(1)}, bf16[256,384]{1,0:T(8,128)(2,1)S(1)}, u32[]{:S(2)}, u32[]{:S(2)}) %collective-permute-start.5) | collective-permute-done | bytes 196640 | tf_op jit(solution)/shard_map/ppermute | solution.py:374
  64.9 12.3 %shard_map.204 = (bf16[256,1408]{1,0:T(8,128)(2,1)}, bf16[256,1408]{1,0:T(8,128)(2,1)}) custom-call(s32[1]{0:T(128)} %bitcast.35.refs_0_, f32[256,1]{1,0:T(8,128)} %copy.32.refs_1_, bf16[256,11264]{1,0:T(8,128)(2,1)} %refs_2_.2), custom_call_target="tpu_custom_call" | custom-call | flops 1000 | bytes 1000 | tf_op jit(solution)/shard_map/pallas_call | solution.py:355
  88.0 6.5 fusion.33
  110.3 17.7 %collective-permute-done.9 = f32[256,384]{1,0:T(8,128)} collective-permute-done((f32[256,384]{1,0:T(8,128)}, f32[256,384]{1,0:T(8,128)}, u32[]{:S(2)}, u32[]{:S(2)}) %collective-permute-start.9) | collective-permute-done | bytes 393248 | tf_op jit(solution)/shard_map/ppermute | solution.py:676
  135.2 20.5 %collective-permute-done.10 = bf16[256,512]{1,0:T(8,128)(2,1)S(1)} collective-permute-done((bf16[256,512]{1,0:T(8,128)(2,1)S(1)}, bf16[256,512]{1,0:T(8,128)(2,1)S(1)}, u32[]{:S(2)}, u32[]{:S(2)}) %collective-permute-start.10) | collective-permute-done | bytes 262176 | tf_op jit(solution)/shard_map/ppermute | solution.py:374
  155.7 6.5 collective-permute-done.11
  162.2 14.2 %collective-permute-done.12 = bf16[256,512]{1,0:T(8,128)(2,1)S(1)} collective-permute-done((bf16[256,512]{1,0:T(8,128)(2,1)S(1)}, bf16[256,512]{1,0:T(8,128)(2,1)S(1)}, u32[]{:S(2)}, u32[]{:S(2)}) %collective-permute-start.12) | collective-permute-done | bytes 262176 | tf_op jit(solution)/shard_map/ppermute | solution.py:374
  182.4 19.7 %collective-permute-done.13 = bf16[4,256,512]{2,1,0:T(8,128)(2,1)} collective-permute-done((bf16[4,256,512]{2,1,0:T(8,128)(2,1)}, bf16[4,256,512]{2,1,0:T(8,128)(2,1)}, u32[]{:S(2)}, u32[]{:S(2)}) %collective-permute-start.13) | collective-permute-done | bytes 1048608 | tf_op jit(solution)/shard_map/ppermute | solution.py:374
  214.5 25.0 %shard_map.203 = (bf16[256,4096]{1,0:T(8,128)(2,1)S(1)}, bf16[256,4096]{1,0:T(8,128)(2,1)S(1)}, f32[16,1,256]{2,1,0:T(1,128)S(1)}) custom-call(s32[2]{0:T(128)S(1)} %copy-done.13, bf16[256,1024]{1,0:T(8,128)(2,1)S(1)} %fusion.32.input_ref, bf16[1024,4096]{1,0:T(8,128)(2,1)} %all-gather.6.cloned.1.call-done.up_ref, f32[256,128]{1,0:T(8,128)S(1)} %copy-done.11, ...), custom_call_target="tpu_custom_call" | custom-call | flops 1000 | bytes 1000 | tf_op jit(solution)/shard_map/pallas_call | solution.py:142
  246.4 15.4 %collective-permute-done.24 = bf16[176,2048]{1,0:T(8,128)(2,1)S(1)} collective-permute-done((bf16[176,2048]{1,0:T(8,128)(2,1)}, bf16[176,2048]{1,0:T(8,128)(2,1)S(1)}, u32[]{:S(2)}, u32[]{:S(2)}) %collective-permute-start.24) | collective-permute-done | bytes 720928 | tf_op jit(solution)/shard_map/ppermute | solution.py:374
  281.6 4.9 multiply_reduce_fusion.2
  294.9 18.2 %collective-permute-done.25 = bf16[256,2048]{1,0:T(8,128)(2,1)} collective-permute-done((bf16[256,2048]{1,0:T(8,128)(2,1)}, bf16[256,2048]{1,0:T(8,128)(2,1)}, u32[]{:S(2)}, u32[]{:S(2)}) %collective-permute-start.25) | collective-permute-done | bytes 1048608 | tf_op jit(solution)/shard_map/ppermute | solution.py:374
  319.7 15.9 %collective-permute-done.21 = bf16[256,2048]{1,0:T(8,128)(2,1)} collective-permute-done((bf16[256,2048]{1,0:T(8,128)(2,1)}, bf16[256,2048]{1,0:T(8,128)(2,1)}, u32[]{:S(2)}, u32[]{:S(2)}) %collective-permute-start.21) | collective-permute-done | bytes 1048608 | tf_op jit(solution)/shard_map/ppermute | solution.py:374
  348.3 9.2 %constant_dynamic-slice_fusion.11 = (bf16[256,8,1,128]{3,2,1,0:T(2,128)(2,1)S(1)}, bf16[256,8,1,128]{3,2,1,0:T(2,128)(2,1)}, bf16[256,8,1,128]{3,2,1,0:T(2,128)(2,1)}, bf16[256,8,1,128]{3,2,1,0:T(2,128)(2,1)S(1)}) fusion(bf16[256,8,4,128]{3,2,1,0:T(4,128)(2,1)} %reshape.310, s32[]{:T(128)S(6)} %select_n.232, s32[]{:T(128)S(6)} %select_n.233, ...), kind=kLoop, calls=%fused_computation.195 | loop fusion | bytes 4194320 | tf_op jit(solution)/shard_map/jit(dynamic_index_in_dim)/dynamic_slice | solution.py:721
  360.2 5.1 maximum_select_fusion
  365.3 13.2 %fusion.62 = f32[1024,1408]{1,0:T(8,128)} fusion(bf16[2048,1408]{1,0:T(8,128)(2,1)S(1)} %bitcast.211, bf16[256,2048]{1,0:T(8,128)(2,1)} %collective-permute-done.27, bf16[256,2048]{1,0:T(8,128)(2,1)} %collective-permute-done.26, bf16[256,2048]{1,0:T(8,128)(2,1)} %collective-permute-done.25, bf16[256,2048]{1,0:T(8,128)(2,1)} %multiply_convert_fusion.4), kind=kOutput, calls=%fused_computation.234 | convolution fusion | flops 5922357248 | bytes 15728640 | tf_op jit(solution)/shard_map/dot_general | solution.py:55
  384.0 13.6 %collective-permute-done.29 = bf16[1024,1408]{1,0:T(8,128)(2,1)} collective-permute-done((bf16[1024,1408]{1,0:T(8,128)(2,1)}, bf16[1024,1408]{1,0:T(8,128)(2,1)}, u32[]{:S(2)}, u32[]{:S(2)}) %collective-permute-start.29) | collective-permute-done | bytes 2883616 | tf_op jit(solution)/shard_map/ppermute | solution.py:374
  400.8 4.6 all-gather.10.cloned.1.call-done
  407.1 7.8 maximum_select_fusion.1
  426.0 12.5 %multiply_convert_fusion.2 = (bf16[1024,1408]{1,0:T(8,128)(2,1)S(1)}, f32[1024,1408]{1,0:T(8,128)}) fusion(f32[1024,1408]{1,0:T(8,128)} %fusion.62, bf16[2048,1408]{1,0:T(8,128)(2,1)S(1)} %bitcast.218, bf16[256,2048]{1,0:T(8,128)(2,1)} %collective-permute-done.27, bf16[256,2048]{1,0:T(8,128)(2,1)} %collective-permute-done.26, ...), kind=kOutput, calls=%fused_computation.9 | convolution fusion | flops 5931008000 | bytes 24379392 | tf_op jit(solution)/shard_map/dot_general | solution.py:55
  440.1 8.1 convolution_convert_fusion.2
  448.4 15.6 %multiply_convert_fusion = (bf16[1024,1408]{1,0:T(8,128)(2,1)S(1)}, bf16[1024,1408]{1,0:T(8,128)(2,1)}) fusion(f32[1024,1408]{1,0:T(8,128)} %fusion.62, f32[1024,1408]{1,0:T(8,128)} %get-tuple-element.304, bf16[1024,2048]{1,0:T(8,128)(2,1)} %constant_dynamic-update-slice_fusion.2, bf16[1408,2048]{1,0:T(8,128)(2,1)} %all-gather.10.cloned.1.call-done), kind=kOutput, calls=%fused_computation.7 | convolution fusion | flops 5924323328 | bytes 27262976 | tf_op jit(solution)/shard_map/dot_general | solution.py:63
  464.0 8.5 fusion.71
  472.5 12.5 %fusion.69 = (bf16[1024,2048]{1,0:T(8,128)(2,1)}, f32[1024,2048]{1,0:T(8,128)}) fusion(f32[1024,2048]{1,0:T(8,128)S(1)} %fusion.71, bf16[1024,1408]{1,0:T(8,128)(2,1)S(1)} %get-tuple-element.169, bf16[2048,1408]{1,0:T(8,128)(2,1)} %bitcast.215), kind=kOutput, calls=%fused_computation.240 | convolution fusion | flops 5909774336 | bytes 29622272 | tf_op jit(solution)/shard_map/dot_general | solution.py:63
  484.9 11.0 %convolution_convert_fusion.1 = bf16[2048,1408]{1,0:T(8,128)(2,1)} fusion(bf16[1024,1408]{1,0:T(8,128)(2,1)S(1)} %copy-done.71, bf16[256,2048]{1,0:T(8,128)(2,1)} %collective-permute-done.27, bf16[256,2048]{1,0:T(8,128)(2,1)} %collective-permute-done.26, bf16[256,2048]{1,0:T(8,128)(2,1)} %collective-permute-done.25, bf16[256,2048]{1,0:T(8,128)(2,1)} %multiply_convert_fusion.4), kind=kOutput, calls=%fused_computation.1 | convolution fusion | flops 5925240832 | bytes 12845056 | tf_op jit(solution)/shard_map/dot_general | solution.py:59
  496.0 10.8 %convolution_convert_fusion = bf16[2048,1408]{1,0:T(8,128)(2,1)} fusion(bf16[1024,1408]{1,0:T(8,128)(2,1)S(1)} %get-tuple-element.169, bf16[256,2048]{1,0:T(8,128)(2,1)} %collective-permute-done.27, bf16[256,2048]{1,0:T(8,128)(2,1)} %collective-permute-done.26, bf16[256,2048]{1,0:T(8,128)(2,1)} %collective-permute-done.25, ...), kind=kOutput, calls=%fused_computation | convolution fusion | flops 5925240832 | bytes 12845056 | tf_op jit(solution)/shard_map/dot_general | solution.py:59
  519.3 19.6 %collective-permute-done.38 = bf16[256,2048]{1,0:T(8,128)(2,1)S(1)} collective-permute-done((bf16[256,2048]{1,0:T(8,128)(2,1)}, bf16[256,2048]{1,0:T(8,128)(2,1)S(1)}, u32[]{:S(2)}, u32[]{:S(2)}) %collective-permute-start.38) | collective-permute-done | bytes 1048608 | tf_op jit(solution)/shard_map/ppermute | solution.py:379
  546.7 18.5 %convolution_convert_fusion.3.do_ref = bf16[256,4096]{1,0:T(8,128)(2,1)} fusion(bf16[256,2048]{1,0:T(8,128)(2,1)S(1)} %get-tuple-element.233, bf16[4096,2048]{1,0:T(8,128)(2,1)} %bitcast.204), kind=kOutput, calls=%fused_computation.12 | convolution fusion | flops 4296015872 | bytes 19922944 | tf_op jit(solution)/shard_map/dot_general | solution.py:63
  570.0 21.0 %shard_map.205 = (bf16[256,4096]{1,0:T(8,128)(2,1)S(1)}, bf16[2048,512]{1,0:T(8,128)(2,1)S(1)}) custom-call(s32[2]{0:T(128)S(1)} %copy-done.14, bf16[256,4096]{1,0:T(8,128)(2,1)S(1)} %copy-done.9, bf16[256,4096]{1,0:T(8,128)(2,1)S(1)} %copy-done.10, bf16[256,4096]{1,0:T(8,128)(2,1)S(1)} %copy-done.7, f32[16,1,256]{2,1,0:T(1,128)S(1)} %get-tuple-element.171.lse_ref, ...), custom_call_target="tpu_custom_call" | custom-call | flops 1000 | bytes 1000 | tf_op jit(solution)/shard_map/pallas_call | solution.py:239
  592.8 6.0 multiply_reduce_fusion.4
  606.7 10.6 %collective-permute-done.39 = bf16[4,256,512]{2,1,0:T(8,128)(2,1)S(1)} collective-permute-done((bf16[4,256,512]{2,1,0:T(8,128)(2,1)}, bf16[4,256,512]{2,1,0:T(8,128)(2,1)S(1)}, u32[]{:S(2)}, u32[]{:S(2)}) %collective-permute-start.39) | collective-permute-done | bytes 1048608 | tf_op jit(solution)/shard_map/ppermute | solution.py:379
  621.6 4.7 convolution_convert_fusion.4
  628.4 15.3 %collective-permute-start.40 = (bf16[256,512]{1,0:T(8,128)(2,1)S(1)}, bf16[256,512]{1,0:T(8,128)(2,1)S(1)}, u32[]{:S(2)}, u32[]{:S(2)}) collective-permute-start(bf16[256,512]{1,0:T(8,128)(2,1)S(1)} %get-tuple-element.289), channel_id=1, source_target_pairs={{0,2},{2,4},{4,6},{6,0},{1,3},{3,5},{5,7},{7,1},{8,10},{10,12},{12... | collective-permute-start | bytes 786440 | tf_op jit(solution)/shard_map/ppermute | solution.py:379
  648.2 5.0 fusion.25
  653.2 14.0 %collective-permute-done.40 = bf16[256,512]{1,0:T(8,128)(2,1)S(1)} collective-permute-done((bf16[256,512]{1,0:T(8,128)(2,1)S(1)}, bf16[256,512]{1,0:T(8,128)(2,1)S(1)}, u32[]{:S(2)}, u32[]{:S(2)}) %collective-permute-start.40) | collective-permute-done | bytes 262176 | tf_op jit(solution)/shard_map/ppermute | solution.py:379
  667.3 11.7 %collective-permute-done.41 = bf16[256,512]{1,0:T(8,128)(2,1)S(1)} collective-permute-done((bf16[256,512]{1,0:T(8,128)(2,1)S(1)}, bf16[256,512]{1,0:T(8,128)(2,1)S(1)}, u32[]{:S(2)}, u32[]{:S(2)}) %collective-permute-start.41) | collective-permute-done | bytes 262176 | tf_op jit(solution)/shard_map/ppermute | solution.py:379
  688.1 5.0 collective-permute-done.52
  697.1 4.6 convolution_convert_fusion.5
  701.6 7.2 fusion.70
  711.3 11.6 %fusion.72 = f32[1024,2048]{1,0:T(8,128)} fusion(bf16[1024,1408]{1,0:T(8,128)(2,1)} %copy-done.70, bf16[1408,2048]{1,0:T(8,128)(2,1)} %all-gather.10.cloned.1.call-done), kind=kOutput, calls=%fused_computation.243 | convolution fusion | flops 5905580032 | bytes 17039360 | tf_op jit(solution)/shard_map/dot_general | solution.py:55
  736.8 14.8 %collective-permute-done.61 = bf16[256,2048]{1,0:T(8,128)(2,1)} collective-permute-done((bf16[256,2048]{1,0:T(8,128)(2,1)}, bf16[256,2048]{1,0:T(8,128)(2,1)}, u32[]{:S(2)}, u32[]{:S(2)}) %collective-permute-start.61) | collective-permute-done | bytes 1048608 | tf_op jit(solution)/shard_map/ppermute | solution.py:379
  756.4 12.2 %collective-permute-done.62 = bf16[256,1408]{1,0:T(8,128)(2,1)S(1)} collective-permute-done((bf16[256,1408]{1,0:T(8,128)(2,1)S(1)}, bf16[256,1408]{1,0:T(8,128)(2,1)S(1)}, u32[]{:S(2)}, u32[]{:S(2)}) %collective-permute-start.62) | collective-permute-done | bytes 720928 | tf_op jit(solution)/shard_map/ppermute | solution.py:379
  770.8 6.1 convert.49
  791.1 17.2 %collective-permute-done.66.refs_4_ = bf16[256,1408]{1,0:T(8,128)(2,1)S(1)} collective-permute-done((bf16[256,1408]{1,0:T(8,128)(2,1)}, bf16[256,1408]{1,0:T(8,128)(2,1)S(1)}, u32[]{:S(2)}, u32[]{:S(2)}) %collective-permute-start.66) | collective-permute-done | bytes 720928 | tf_op jit(solution)/shard_map/ppermute | solution.py:374
  826.2 13.5 %shard_map.206 = (f32[256,11264]{1,0:T(8,128)}, f32[256,1]{1,0:T(8,128)}) custom-call(s32[4]{0:T(128)} %copy-done.58, f32[256,1]{1,0:T(8,128)} %copy.32.refs_1_, bf16[256,11264]{1,0:T(8,128)(2,1)} %refs_2_.2, bf16[256,1408]{1,0:T(8,128)(2,1)} %reduce-scatter.10.cloned.1.call-done.refs_3_, bf16[256,1408]{1,0:T(8,128)(2,1)} %copy-done.41, ...), custom_call_target="tpu_custom_call" | custom-call | flops 1000 | bytes 1000 | tf_op jit(solution)/shard_map/pallas_call | solution.py:310
  847.8 16.0 %collective-permute-done.71 = bf16[256,2048]{1,0:T(8,128)(2,1)S(1)} collective-permute-done((bf16[256,2048]{1,0:T(8,128)(2,1)}, bf16[256,2048]{1,0:T(8,128)(2,1)S(1)}, u32[]{:S(2)}, u32[]{:S(2)}) %collective-permute-start.71) | collective-permute-done | bytes 1048608 | tf_op jit(solution)/shard_map/ppermute | solution.py:379
  (493 shorter events, 301.1 us)
Async XLA Ops:
  7.2 98.5 %all-gather.8.cloned.1.call-start = ((), (), s32[]{:S(2)}) async-start(), calls=%async_computation.6 | async-start | bytes 2621440 | tf_op jit(solution)/shard_map/all_gather | solution.py:464
  9.3 202.0 %all-gather.6.cloned.1.call-start = ((), (), s32[]{:S(2)}) async-start(), calls=%async_computation.5 | async-start | bytes 8650752 | tf_op jit(solution)/shard_map/all_gather | solution.py:633
  14.1 251.1 %all-gather.12.cloned.1.call-start = ((), (), s32[]{:S(2)}) async-start(), calls=%async_computation.8 | async-start | bytes 3604480 | tf_op jit(solution)/shard_map/all_gather | solution.py:464
  18.7 62.0 %collective-permute-start = (bf16[256,2048]{1,0:T(8,128)(2,1)}, bf16[256,2048]{1,0:T(8,128)(2,1)}, u32[]{:S(2)}, u32[]{:S(2)}) collective-permute-start(bf16[256,2048]{1,0:T(8,128)(2,1)} %fusion.4), channel_id=1, source_target_pairs={{16,0},{0,16},{17,1},{1,17},{18,2},{2,18},{19,3},{3,19},{20,4},{4,... | collective-permute-start | bytes 3145736 | tf_op jit(solution)/shard_map/ppermute | solution.py:374
  25.7 37.2 %collective-permute-start.5 = (bf16[256,384]{1,0:T(8,128)(2,1)S(1)}, bf16[256,384]{1,0:T(8,128)(2,1)S(1)}, u32[]{:S(2)}, u32[]{:S(2)}) collective-permute-start(bf16[256,384]{1,0:T(8,128)(2,1)S(1)} %get-tuple-element.236), channel_id=1, source_target_pairs={{6,0},{0,2},{2,4},{4,6},{7,1},{1,3},{3,5},{5,7},{14,8},{8,10},{10,... | collective-permute-start | bytes 589832 | tf_op jit(solution)/shard_map/ppermute | solution.py:374
  77.2 242.5 %all-gather.14.cloned.1.call-start = ((), (), s32[]{:S(2)}) async-start(), calls=%async_computation.9 | async-start | bytes 3604480 | tf_op jit(solution)/shard_map/all_gather | solution.py:464
  105.7 73.9 %collective-permute-start.14 = (bf16[512,2048]{1,0:T(8,128)(2,1)}, bf16[512,2048]{1,0:T(8,128)(2,1)}, u32[]{:S(2)}, u32[]{:S(2)}) collective-permute-start(bf16[512,2048]{1,0:T(8,128)(2,1)} %all-gather.8.cloned.1.call-done), channel_id=1, source_target_pairs={{1,0},{0,1},{3,2},{2,3},{5,4},{4,5},{7,6},{6,7},{9,8},{8,9},{11,10... | collective-permute-start | bytes 6291464 | tf_op jit(solution)/shard_map/ppermute | solution.py:374
  108.1 94.1 %collective-permute-start.15 = (bf16[512,2048]{1,0:T(8,128)(2,1)}, bf16[512,2048]{1,0:T(8,128)(2,1)}, u32[]{:S(2)}, u32[]{:S(2)}) collective-permute-start(bf16[512,2048]{1,0:T(8,128)(2,1)} %all-gather.8.cloned.1.call-done), channel_id=1, source_target_pairs={{16,0},{0,16},{17,1},{1,17},{18,2},{2,18},{19,3},{3,19},{20,4},{4,... | collective-permute-start | bytes 6291464 | tf_op jit(solution)/shard_map/ppermute | solution.py:374
  132.8 29.4 %collective-permute-start.11 = (bf16[256,512]{1,0:T(8,128)(2,1)S(1)}, bf16[256,512]{1,0:T(8,128)(2,1)S(1)}, u32[]{:S(2)}, u32[]{:S(2)}) collective-permute-start(bf16[256,512]{1,0:T(8,128)(2,1)S(1)} %pad_maximum_fusion.12), channel_id=1, source_target_pairs={{4,0},{6,2},{0,4},{2,6},{5,1},{7,3},{1,5},{3,7},{12,8},{14,10},{8,... | collective-permute-start | bytes 786440 | tf_op jit(solution)/shard_map/ppermute | solution.py:374
  135.2 41.2 %collective-permute-start.12 = (bf16[256,512]{1,0:T(8,128)(2,1)S(1)}, bf16[256,512]{1,0:T(8,128)(2,1)S(1)}, u32[]{:S(2)}, u32[]{:S(2)}) collective-permute-start(bf16[256,512]{1,0:T(8,128)(2,1)S(1)} %pad_maximum_fusion.12), channel_id=1, source_target_pairs={{6,0},{0,2},{2,4},{4,6},{7,1},{1,3},{3,5},{5,7},{14,8},{8,10},{10,... | collective-permute-start | bytes 786440 | tf_op jit(solution)/shard_map/ppermute | solution.py:374
  177.5 227.8 %all-gather.10.cloned.1.call-start = ((), (), s32[]{:S(2)}) async-start(), calls=%async_computation.7 | async-start | bytes 7208960 | tf_op jit(solution)/shard_map/all_gather | solution.py:464
  179.6 62.6 %collective-permute-start.16 = (bf16[512,2048]{1,0:T(8,128)(2,1)}, bf16[512,2048]{1,0:T(8,128)(2,1)}, u32[]{:S(2)}, u32[]{:S(2)}) collective-permute-start(bf16[512,2048]{1,0:T(8,128)(2,1)} %collective-permute-done.14), channel_id=1, source_target_pairs={{16,0},{0,16},{17,1},{1,17},{18,2},{2,18},{19,3},{3,19},{20,4},{4,... | collective-permute-start | bytes 6291464 | tf_op jit(solution)/shard_map/ppermute | solution.py:374
  243.4 29.7 %collective-permute-start.18 = (bf16[512,2048]{1,0:T(8,128)(2,1)}, bf16[512,2048]{1,0:T(8,128)(2,1)}, u32[]{:S(2)}, u32[]{:S(2)}) collective-permute-start(bf16[512,2048]{1,0:T(8,128)(2,1)} %collective-permute-done.15), channel_id=1, source_target_pairs={{8,0},{0,8},{9,1},{1,9},{10,2},{2,10},{11,3},{3,11},{12,4},{4,12},... | collective-permute-start | bytes 6291464 | tf_op jit(solution)/shard_map/ppermute | solution.py:374
  244.3 34.5 %collective-permute-start.19 = (bf16[512,2048]{1,0:T(8,128)(2,1)}, bf16[512,2048]{1,0:T(8,128)(2,1)S(1)}, u32[]{:S(2)}, u32[]{:S(2)}) collective-permute-start(bf16[512,2048]{1,0:T(8,128)(2,1)} %collective-permute-done.14), channel_id=1, source_target_pairs={{8,0},{0,8},{9,1},{1,9},{10,2},{2,10},{11,3},{3,11},{12,4},{4,12},... | collective-permute-start | bytes 6291464 | tf_op jit(solution)/shard_map/ppermute | solution.py:374
  246.4 32.8 %collective-permute-start.20 = (bf16[512,2048]{1,0:T(8,128)(2,1)}, bf16[512,2048]{1,0:T(8,128)(2,1)}, u32[]{:S(2)}, u32[]{:S(2)}) collective-permute-start(bf16[512,2048]{1,0:T(8,128)(2,1)} %collective-permute-done.16), channel_id=1, source_target_pairs={{8,0},{0,8},{9,1},{1,9},{10,2},{2,10},{11,3},{3,11},{12,4},{4,12},... | collective-permute-start | bytes 6291464 | tf_op jit(solution)/shard_map/ppermute | solution.py:374
  264.9 468.9 %reduce-scatter.8.cloned.1.call-start = ((), (), s32[]{:S(2)}) async-start(), calls=%async_computation.11 | async-start | bytes 7208960 | tf_op jit(solution)/shard_map/reduce_scatter | solution.py:472
  265.2 94.6 %collective-permute-start.28 = (bf16[1024,1408]{1,0:T(8,128)(2,1)}, bf16[1024,1408]{1,0:T(8,128)(2,1)}, u32[]{:S(2)}, u32[]{:S(2)}) collective-permute-start(bf16[1024,1408]{1,0:T(8,128)(2,1)} %all-gather.12.cloned.1.call-done), channel_id=1, source_target_pairs={{1,0},{0,1},{3,2},{2,3},{5,4},{4,5},{7,6},{6,7},{9,8},{8,9},{11,10... | collective-permute-start | bytes 8650760 | tf_op jit(solution)/shard_map/ppermute | solution.py:374
  292.8 42.8 %collective-permute-start.21 = (bf16[256,2048]{1,0:T(8,128)(2,1)}, bf16[256,2048]{1,0:T(8,128)(2,1)}, u32[]{:S(2)}, u32[]{:S(2)}) collective-permute-start(bf16[256,2048]{1,0:T(8,128)(2,1)} %fusion.24), channel_id=1, source_target_pairs={{16,0},{0,16},{17,1},{1,17},{18,2},{2,18},{19,3},{3,19},{20,4},{4,... | collective-permute-start | bytes 3145736 | tf_op jit(solution)/shard_map/ppermute | solution.py:374
  292.9 46.0 %collective-permute-start.22 = (bf16[256,2048]{1,0:T(8,128)(2,1)}, bf16[256,2048]{1,0:T(8,128)(2,1)}, u32[]{:S(2)}, u32[]{:S(2)}) collective-permute-start(bf16[256,2048]{1,0:T(8,128)(2,1)} %fusion.24), channel_id=1, source_target_pairs={{8,0},{0,8},{9,1},{1,9},{10,2},{2,10},{11,3},{3,11},{12,4},{4,12},... | collective-permute-start | bytes 3145736 | tf_op jit(solution)/shard_map/ppermute | solution.py:374
  294.9 49.2 %collective-permute-start.26 = (bf16[256,2048]{1,0:T(8,128)(2,1)}, bf16[256,2048]{1,0:T(8,128)(2,1)}, u32[]{:S(2)}, u32[]{:S(2)}) collective-permute-start(bf16[256,2048]{1,0:T(8,128)(2,1)} %multiply_convert_fusion.4), channel_id=1, source_target_pairs={{8,0},{0,8},{9,1},{1,9},{10,2},{2,10},{11,3},{3,11},{12,4},{4,12},... | collective-permute-start | bytes 3145736 | tf_op jit(solution)/shard_map/ppermute | solution.py:374
  313.1 31.0 %collective-permute-start.27 = (bf16[256,2048]{1,0:T(8,128)(2,1)}, bf16[256,2048]{1,0:T(8,128)(2,1)}, u32[]{:S(2)}, u32[]{:S(2)}) collective-permute-start(bf16[256,2048]{1,0:T(8,128)(2,1)} %collective-permute-done.25), channel_id=1, source_target_pairs={{8,0},{0,8},{9,1},{1,9},{10,2},{2,10},{11,3},{3,11},{12,4},{4,12},... | collective-permute-start | bytes 3145736 | tf_op jit(solution)/shard_map/ppermute | solution.py:374
  335.6 62.0 %collective-permute-start.29 = (bf16[1024,1408]{1,0:T(8,128)(2,1)}, bf16[1024,1408]{1,0:T(8,128)(2,1)}, u32[]{:S(2)}, u32[]{:S(2)}) collective-permute-start(bf16[1024,1408]{1,0:T(8,128)(2,1)} %all-gather.14.cloned.1.call-done), channel_id=1, source_target_pairs={{1,0},{0,1},{3,2},{2,3},{5,4},{4,5},{7,6},{6,7},{9,8},{8,9},{11,10... | collective-permute-start | bytes 8650760 | tf_op jit(solution)/shard_map/ppermute | solution.py:374
  338.9 66.4 %collective-permute-start.23 = (bf16[256,2048]{1,0:T(8,128)(2,1)}, bf16[256,2048]{1,0:T(8,128)(2,1)}, u32[]{:S(2)}, u32[]{:S(2)}) collective-permute-start(bf16[256,2048]{1,0:T(8,128)(2,1)} %collective-permute-done.21), channel_id=1, source_target_pairs={{8,0},{0,8},{9,1},{1,9},{10,2},{2,10},{11,3},{3,11},{12,4},{4,12},... | collective-permute-start | bytes 3145736 | tf_op jit(solution)/shard_map/ppermute | solution.py:374
  344.1 63.0 %collective-permute-start.33 = (bf16[256,1024]{1,0:T(8,128)(2,1)S(1)}, bf16[256,1024]{1,0:T(8,128)(2,1)}, u32[]{:S(2)}, u32[]{:S(2)}) collective-permute-start(bf16[256,1024]{1,0:T(8,128)(2,1)S(1)} %fusion.32.input_ref), channel_id=1, source_target_pairs={{16,0},{0,16},{17,1},{1,17},{18,2},{2,18},{19,3},{3,19},{20,4},{4,... | collective-permute-start | bytes 1572872 | tf_op jit(solution)/shard_map/ppermute | solution.py:374
  345.3 77.8 %collective-permute-start.34 = (bf16[256,1024]{1,0:T(8,128)(2,1)S(1)}, bf16[256,1024]{1,0:T(8,128)(2,1)}, u32[]{:S(2)}, u32[]{:S(2)}) collective-permute-start(bf16[256,1024]{1,0:T(8,128)(2,1)S(1)} %fusion.32.input_ref), channel_id=1, source_target_pairs={{8,0},{0,8},{9,1},{1,9},{10,2},{2,10},{11,3},{3,11},{12,4},{4,12},... | collective-permute-start | bytes 1572872 | tf_op jit(solution)/shard_map/ppermute | solution.py:374
  359.8 58.6 %collective-permute-start.30 = (bf16[256,1024]{0,1:T(8,128)(2,1)S(1)}, bf16[256,1024]{0,1:T(8,128)(2,1)}, u32[]{:S(2)}, u32[]{:S(2)}) collective-permute-start(bf16[256,1024]{0,1:T(8,128)(2,1)S(1)} %bitcast.235), channel_id=1, source_target_pairs={{16,0},{24,8},{0,16},{8,24},{17,1},{25,9},{1,17},{9,25},{18,2},{26... | collective-permute-start | bytes 1572872 | tf_op jit(solution)/shard_map/ppermute | solution.py:412
  448.3 285.5 %reduce-scatter.6.cloned.1.call-start = ((), (), s32[]{:S(2)}) async-start(), calls=%async_computation.10 | async-start | bytes 7208960 | tf_op jit(solution)/shard_map/reduce_scatter | solution.py:472
  506.8 271.2 %reduce-scatter.10.cloned.1.call-start = ((), (), s32[]{:S(2)}) async-start(), calls=%async_computation.12 | async-start | bytes 3604480 | tf_op jit(solution)/shard_map/reduce_scatter | solution.py:472
  519.0 83.3 %collective-permute-start.46 = (bf16[4,256,1408]{2,1,0:T(8,128)(2,1)}, bf16[4,256,1408]{2,1,0:T(8,128)(2,1)}, u32[]{:S(2)}, u32[]{:S(2)}) collective-permute-start(bf16[4,256,1408]{2,1,0:T(8,128)(2,1)} %dynamic-slice_bitcast_fusion), channel_id=1, source_target_pairs={{0,1},{1,0},{2,3},{3,2},{4,5},{5,4},{6,7},{7,6},{8,9},{9,8},{10,11... | collective-permute-start | bytes 8650760 | tf_op jit(solution)/shard_map/ppermute | solution.py:379
  544.2 56.7 %collective-permute-start.43 = (bf16[256,2048]{1,0:T(8,128)(2,1)S(1)}, bf16[256,2048]{1,0:T(8,128)(2,1)}, u32[]{:S(2)}, u32[]{:S(2)}) collective-permute-start(bf16[256,2048]{1,0:T(8,128)(2,1)S(1)} %get-tuple-element.233), channel_id=1, source_target_pairs={{16,0},{0,16},{17,1},{1,17},{18,2},{2,18},{19,3},{3,19},{20,4},{4,... | collective-permute-start | bytes 3145736 | tf_op jit(solution)/shard_map/ppermute | solution.py:374
  545.3 73.8 %collective-permute-start.44 = (bf16[256,2048]{1,0:T(8,128)(2,1)S(1)}, bf16[256,2048]{1,0:T(8,128)(2,1)}, u32[]{:S(2)}, u32[]{:S(2)}) collective-permute-start(bf16[256,2048]{1,0:T(8,128)(2,1)S(1)} %get-tuple-element.233), channel_id=1, source_target_pairs={{8,0},{0,8},{9,1},{1,9},{10,2},{2,10},{11,3},{3,11},{12,4},{4,12},... | collective-permute-start | bytes 3145736 | tf_op jit(solution)/shard_map/ppermute | solution.py:374
  600.2 43.5 %collective-permute-start.47 = (bf16[256,1024]{1,0:T(8,128)(2,1)}, bf16[256,1024]{1,0:T(8,128)(2,1)}, u32[]{:S(2)}, u32[]{:S(2)}) collective-permute-start(bf16[256,1024]{1,0:T(8,128)(2,1)} %get-tuple-element.254), channel_id=1, source_target_pairs={{16,0},{24,8},{0,16},{8,24},{17,1},{25,9},{1,17},{9,25},{18,2},{26... | collective-permute-start | bytes 1572872 | tf_op jit(solution)/shard_map/ppermute | solution.py:412
  602.4 44.4 %collective-permute-start.48 = (bf16[256,1024]{1,0:T(8,128)(2,1)}, bf16[256,1024]{1,0:T(8,128)(2,1)}, u32[]{:S(2)}, u32[]{:S(2)}) collective-permute-start(bf16[256,1024]{1,0:T(8,128)(2,1)} %get-tuple-element.253), channel_id=1, source_target_pairs={{8,0},{0,8},{24,16},{16,24},{9,1},{1,9},{25,17},{17,25},{10,2},{2,... | collective-permute-start | bytes 1572872 | tf_op jit(solution)/shard_map/ppermute | solution.py:412
  606.6 209.0 %reduce-scatter.14.cloned.1.call-start = ((), (), s32[]{:S(2)}) async-start(), calls=%async_computation.14 | async-start | bytes 2621440 | tf_op jit(solution)/shard_map/reduce_scatter | solution.py:472
  617.2 31.0 %collective-permute-start.49 = (bf16[256,1024]{1,0:T(8,128)(2,1)}, bf16[256,1024]{1,0:T(8,128)(2,1)S(1)}, u32[]{:S(2)}, u32[]{:S(2)}) collective-permute-start(bf16[256,1024]{1,0:T(8,128)(2,1)} %get-tuple-element.252), channel_id=1, source_target_pairs={{24,0},{16,8},{8,16},{0,24},{25,1},{17,9},{9,17},{1,25},{26,2},{18... | collective-permute-start | bytes 1572872 | tf_op jit(solution)/shard_map/ppermute | solution.py:412
  628.1 65.1 %collective-permute-start.53 = (bf16[4,128,2048]{2,1,0:T(8,128)(2,1)}, bf16[4,128,2048]{2,1,0:T(8,128)(2,1)}, u32[]{:S(2)}, u32[]{:S(2)}) collective-permute-start(bf16[4,128,2048]{2,1,0:T(8,128)(2,1)} %get-tuple-element.243), channel_id=1, source_target_pairs={{0,1},{1,0},{2,3},{3,2},{4,5},{5,4},{6,7},{7,6},{8,9},{9,8},{10,11... | collective-permute-start | bytes 6291464 | tf_op jit(solution)/shard_map/ppermute | solution.py:379
  628.4 38.9 %collective-permute-start.40 = (bf16[256,512]{1,0:T(8,128)(2,1)S(1)}, bf16[256,512]{1,0:T(8,128)(2,1)S(1)}, u32[]{:S(2)}, u32[]{:S(2)}) collective-permute-start(bf16[256,512]{1,0:T(8,128)(2,1)S(1)} %get-tuple-element.289), channel_id=1, source_target_pairs={{0,2},{2,4},{4,6},{6,0},{1,3},{3,5},{5,7},{7,1},{8,10},{10,12},{12... | collective-permute-start | bytes 786440 | tf_op jit(solution)/shard_map/ppermute | solution.py:379
  643.6 35.3 %collective-permute-start.41 = (bf16[256,512]{1,0:T(8,128)(2,1)S(1)}, bf16[256,512]{1,0:T(8,128)(2,1)S(1)}, u32[]{:S(2)}, u32[]{:S(2)}) collective-permute-start(bf16[256,512]{1,0:T(8,128)(2,1)S(1)} %get-tuple-element.288), channel_id=1, source_target_pairs={{0,4},{2,6},{4,0},{6,2},{1,5},{3,7},{5,1},{7,3},{8,12},{10,14},{12... | collective-permute-start | bytes 786440 | tf_op jit(solution)/shard_map/ppermute | solution.py:379
  646.8 34.1 %collective-permute-start.42 = (bf16[256,512]{1,0:T(8,128)(2,1)S(1)}, bf16[256,512]{1,0:T(8,128)(2,1)S(1)}, u32[]{:S(2)}, u32[]{:S(2)}) collective-permute-start(bf16[256,512]{1,0:T(8,128)(2,1)S(1)} %get-tuple-element.287), channel_id=1, source_target_pairs={{0,6},{2,0},{4,2},{6,4},{1,7},{3,1},{5,3},{7,5},{8,14},{10,8},{12,... | collective-permute-start | bytes 786440 | tf_op jit(solution)/shard_map/ppermute | solution.py:379
  711.2 165.1 %reduce-scatter.12.cloned.1.call-start = ((), (), s32[]{:S(2)}) async-start(), calls=%async_computation.13 | async-start | bytes 1310720 | tf_op jit(solution)/shard_map/reduce_scatter | solution.py:472
  729.1 41.7 %collective-permute-start.58 = (bf16[4,128,1024]{2,1,0:T(8,128)(2,1)}, bf16[4,128,1024]{2,1,0:T(8,128)(2,1)}, u32[]{:S(2)}, u32[]{:S(2)}) collective-permute-start(bf16[4,128,1024]{2,1,0:T(8,128)(2,1)} %get-tuple-element.249), channel_id=1, source_target_pairs={{0,1},{1,0},{2,3},{3,2},{4,5},{5,4},{6,7},{7,6},{8,9},{9,8},{10,11... | collective-permute-start | bytes 3145736 | tf_op jit(solution)/shard_map/ppermute | solution.py:379
  732.4 54.6 %collective-permute-start.55 = (bf16[256,384]{1,0:T(8,128)(2,1)}, bf16[256,384]{1,0:T(8,128)(2,1)}, u32[]{:S(2)}, u32[]{:S(2)}) collective-permute-start(bf16[256,384]{1,0:T(8,128)(2,1)} %get-tuple-element.292), channel_id=1, source_target_pairs={{0,2},{2,4},{4,6},{6,0},{1,3},{3,5},{5,7},{7,1},{8,10},{10,12},{12... | collective-permute-start | bytes 589832 | tf_op jit(solution)/shard_map/ppermute | solution.py:379
  732.4 58.1 %collective-permute-start.56 = (bf16[256,384]{1,0:T(8,128)(2,1)}, bf16[256,384]{1,0:T(8,128)(2,1)}, u32[]{:S(2)}, u32[]{:S(2)}) collective-permute-start(bf16[256,384]{1,0:T(8,128)(2,1)} %get-tuple-element.291), channel_id=1, source_target_pairs={{0,4},{2,6},{4,0},{6,2},{1,5},{3,7},{5,1},{7,3},{8,12},{10,14},{12... | collective-permute-start | bytes 589832 | tf_op jit(solution)/shard_map/ppermute | solution.py:379
  735.1 55.6 %collective-permute-start.57 = (bf16[256,384]{1,0:T(8,128)(2,1)}, bf16[256,384]{1,0:T(8,128)(2,1)}, u32[]{:S(2)}, u32[]{:S(2)}) collective-permute-start(bf16[256,384]{1,0:T(8,128)(2,1)} %get-tuple-element.290), channel_id=1, source_target_pairs={{0,6},{2,0},{4,2},{6,4},{1,7},{3,1},{5,3},{7,5},{8,14},{10,8},{12,... | collective-permute-start | bytes 589832 | tf_op jit(solution)/shard_map/ppermute | solution.py:379
  776.9 34.2 %collective-permute-start.63 = (bf16[256,1408]{1,0:T(8,128)(2,1)}, bf16[256,1408]{1,0:T(8,128)(2,1)}, u32[]{:S(2)}, u32[]{:S(2)}) collective-permute-start(bf16[256,1408]{1,0:T(8,128)(2,1)} %fusion.29.refs_7_), channel_id=1, source_target_pairs={{16,0},{0,16},{17,1},{1,17},{18,2},{2,18},{19,3},{3,19},{20,4},{4,... | collective-permute-start | bytes 2162696 | tf_op jit(solution)/shard_map/ppermute | solution.py:374
  813.9 33.9 %collective-permute-start.69 = (bf16[256,2048]{1,0:T(8,128)(2,1)}, bf16[256,2048]{1,0:T(8,128)(2,1)S(1)}, u32[]{:S(2)}, u32[]{:S(2)}) collective-permute-start(bf16[256,2048]{1,0:T(8,128)(2,1)} %get-tuple-element.239), channel_id=1, source_target_pairs={{0,8},{8,0},{1,9},{9,1},{2,10},{10,2},{3,11},{11,3},{4,12},{12,4},... | collective-permute-start | bytes 3145736 | tf_op jit(solution)/shard_map/ppermute | solution.py:379
  819.2 44.6 %collective-permute-start.71 = (bf16[256,2048]{1,0:T(8,128)(2,1)}, bf16[256,2048]{1,0:T(8,128)(2,1)S(1)}, u32[]{:S(2)}, u32[]{:S(2)}) collective-permute-start(bf16[256,2048]{1,0:T(8,128)(2,1)} %add_convert_fusion.2), channel_id=1, source_target_pairs={{0,16},{16,0},{1,17},{17,1},{2,18},{18,2},{3,19},{19,3},{4,20},{20... | collective-permute-start | bytes 3145736 | tf_op jit(solution)/shard_map/ppermute | solution.py:379
  845.7 30.7 %collective-permute-start.81 = (bf16[128,2048]{1,0:T(8,128)(2,1)}, bf16[128,2048]{1,0:T(8,128)(2,1)}, u32[]{:S(2)}, u32[]{:S(2)}) collective-permute-start(bf16[128,2048]{1,0:T(8,128)(2,1)} %collective-permute-done.79), channel_id=1, source_target_pairs={{8,0},{0,8},{9,1},{1,9},{10,2},{2,10},{11,3},{3,11},{12,4},{4,12},... | collective-permute-start | bytes 1572872 | tf_op jit(solution)/shard_map/ppermute | solution.py:374
  (125 other events, 1814.2 us)
Sparse Core Ops, SparseCore 0:
  10.2 60.5 all-gather.7
  73.6 102.6 all-gather.5
  178.5 59.8 all-gather.11
  240.4 57.8 all-gather.13
  300.3 104.9 all-gather.9
  448.4 106.2 reduce-scatter.7
  557.0 120.0 reduce-scatter.5
  679.9 55.3 reduce-scatter.9
  737.7 49.7 reduce-scatter.13
  790.3 23.7 reduce-scatter.11

commit v3 on v2

--- a/solution.py
+++ b/solution.py
@@ -724,7 +724,6 @@
     attn_all = jnp.concatenate(exchange_group(attn_late, pick_out), axis=0)
     query_all = jnp.concatenate(gather_group(query_late), axis=0)
 
-    up_mat, attn_all, query_all = lax.optimization_barrier((up_mat, attn_all, query_all))
     up_part = matmul(mlp_all, up_mat)
     sigmoid_gate = jax.nn.sigmoid(gate_part)
     activated = gate_part * sigmoid_gate
@@ -732,7 +731,9 @@
 
     down_term = contract_rows(hidden_low, cot_all).astype(BF)
     down_half = scatter_z(down_term)
-    down_mat = after(down_mat, down_term)
+    down_mat, down_term, attn_all, query_all = lax.optimization_barrier(
+        (down_mat, down_term, attn_all, query_all)
+    )
     hidden_grad = contract_cols(cot_all, down_mat)
     gate_grad = hidden_grad * up_part * (sigmoid_gate * (1.0 + gate_part * (1.0 - sigmoid_gate)))
     gate_low = gate_grad.astype(BF)

time: 907 us -> 945 us (1.042)
  waiting for transfers between devices: 317 us -> 340 us
    ppermute x22, waiting for transfers between devices: 104 us -> 123 us  [to_ahead(): return lax.ppermute(value, axis, [(j, (j + step) % n) for j in range(n)])]
    unnamed x178 -> x182, local copies, waits for them, and re-layouts: 51.1 us -> 51.3 us
  transfers between devices with their start and end apart: 95 -> 95, of which waited for: 30 -> 29; matrix products, arithmetic and copies ran while one was open for 38% -> 41% of each run, Pallas kernels for 8% -> 8%
where the time goes in v3:
time: 945 us; the launch traced here: 931 us
  waiting for transfers between devices  340 us (36%)
  matrix products  169 us (18%)
  local copies, waits for them, and re-layouts  131 us (14%)
  other arithmetic  107 us (11%)
  starting transfers between devices  96.7 us (10%)
  Pallas kernels  71.8 us (8%)
  between operations  15.9 us (2%)
    ppermute x51, waiting for transfers between devices, from_ahead(): return lax.ppermute(value, axis, [((j + step) % n, j) for j in range(n)])  188 us
    ppermute x22, waiting for transfers between devices, to_ahead(): return lax.ppermute(value, axis, [(j, (j + step) % n) for j in range(n)])  123 us
    dot_general x6, matrix products, contract_cols(): lax.dot_general(left, right, (((1,), (1,)), ((), ())), preferred_element_...  71.3 us
    unnamed x182, local copies, waits for them, and re-layouts  51.3 us
    dot_general x6, matrix products, contract_rows(): lax.dot_general(left, right, (((0,), (0,)), ((), ())), preferred_element_...  49.2 us
    dot_general x5, matrix products, matmul(): return jnp.dot(left, right, preferred_element_type=F32)  48.4 us
    ppermute x51, starting transfers between devices, from_ahead(): return lax.ppermute(value, axis, [((j + step) % n, j) for j in range(n)])  43.7 us
    ppermute x22, starting transfers between devices, to_ahead(): return lax.ppermute(value, axis, [(j, (j + step) % n) for j in range(n)])  33.2 us
  transfers between devices with their start and end apart: 95, of which 29 were waited for; matrix products, arithmetic and copies ran while one was open for 41% of the time, Pallas kernels for 8%

profile of v3, /device:TPU:13, one launch (start us, length us, event | category | flops | bytes accessed | tf_op | source)
XLA Modules:
  0.0 931.1 jit_solution(12101085099466183714)
XLA Ops:
  27.8 13.1 %collective-permute-done.3 = bf16[256,384]{1,0:T(8,128)(2,1)S(1)} collective-permute-done((bf16[256,384]{1,0:T(8,128)(2,1)S(1)}, bf16[256,384]{1,0:T(8,128)(2,1)S(1)}, u32[]{:S(2)}, u32[]{:S(2)}) %collective-permute-start.3) | collective-permute-done | bytes 196640 | tf_op jit(solution)/shard_map/ppermute | solution.py:374
  40.9 7.3 collective-permute-done.4
  48.2 14.7 %collective-permute-done.5 = bf16[256,384]{1,0:T(8,128)(2,1)S(1)} collective-permute-done((bf16[256,384]{1,0:T(8,128)(2,1)S(1)}, bf16[256,384]{1,0:T(8,128)(2,1)S(1)}, u32[]{:S(2)}, u32[]{:S(2)}) %collective-permute-start.5) | collective-permute-done | bytes 196640 | tf_op jit(solution)/shard_map/ppermute | solution.py:374
  64.9 12.3 %shard_map.204 = (bf16[256,1408]{1,0:T(8,128)(2,1)}, bf16[256,1408]{1,0:T(8,128)(2,1)}) custom-call(s32[1]{0:T(128)} %bitcast.35.refs_0_, f32[256,1]{1,0:T(8,128)} %copy.32.refs_1_, bf16[256,11264]{1,0:T(8,128)(2,1)} %refs_2_.2), custom_call_target="tpu_custom_call" | custom-call | flops 1000 | bytes 1000 | tf_op jit(solution)/shard_map/pallas_call | solution.py:355
  88.1 6.5 fusion.33
  110.3 17.7 %collective-permute-done.9 = f32[256,384]{1,0:T(8,128)} collective-permute-done((f32[256,384]{1,0:T(8,128)}, f32[256,384]{1,0:T(8,128)}, u32[]{:S(2)}, u32[]{:S(2)}) %collective-permute-start.9) | collective-permute-done | bytes 393248 | tf_op jit(solution)/shard_map/ppermute | solution.py:676
  135.2 20.4 %collective-permute-done.10 = bf16[256,512]{1,0:T(8,128)(2,1)S(1)} collective-permute-done((bf16[256,512]{1,0:T(8,128)(2,1)S(1)}, bf16[256,512]{1,0:T(8,128)(2,1)S(1)}, u32[]{:S(2)}, u32[]{:S(2)}) %collective-permute-start.10) | collective-permute-done | bytes 262176 | tf_op jit(solution)/shard_map/ppermute | solution.py:374
  155.5 6.7 collective-permute-done.11
  162.2 14.2 %collective-permute-done.12 = bf16[256,512]{1,0:T(8,128)(2,1)S(1)} collective-permute-done((bf16[256,512]{1,0:T(8,128)(2,1)S(1)}, bf16[256,512]{1,0:T(8,128)(2,1)S(1)}, u32[]{:S(2)}, u32[]{:S(2)}) %collective-permute-start.12) | collective-permute-done | bytes 262176 | tf_op jit(solution)/shard_map/ppermute | solution.py:374
  182.5 19.7 %collective-permute-done.13 = bf16[4,256,512]{2,1,0:T(8,128)(2,1)} collective-permute-done((bf16[4,256,512]{2,1,0:T(8,128)(2,1)}, bf16[4,256,512]{2,1,0:T(8,128)(2,1)}, u32[]{:S(2)}, u32[]{:S(2)}) %collective-permute-start.13) | collective-permute-done | bytes 1048608 | tf_op jit(solution)/shard_map/ppermute | solution.py:374
  214.5 25.0 %shard_map.203 = (bf16[256,4096]{1,0:T(8,128)(2,1)S(1)}, bf16[256,4096]{1,0:T(8,128)(2,1)S(1)}, f32[16,1,256]{2,1,0:T(1,128)S(1)}) custom-call(s32[2]{0:T(128)S(1)} %copy-done.13, bf16[256,1024]{1,0:T(8,128)(2,1)S(1)} %fusion.32.input_ref, bf16[1024,4096]{1,0:T(8,128)(2,1)} %all-gather.6.cloned.1.call-done.up_ref, f32[256,128]{1,0:T(8,128)S(1)} %copy-done.11, ...), custom_call_target="tpu_custom_call" | custom-call | flops 1000 | bytes 1000 | tf_op jit(solution)/shard_map/pallas_call | solution.py:142
  246.4 15.4 %collective-permute-done.24 = bf16[176,2048]{1,0:T(8,128)(2,1)S(1)} collective-permute-done((bf16[176,2048]{1,0:T(8,128)(2,1)}, bf16[176,2048]{1,0:T(8,128)(2,1)S(1)}, u32[]{:S(2)}, u32[]{:S(2)}) %collective-permute-start.24) | collective-permute-done | bytes 720928 | tf_op jit(solution)/shard_map/ppermute | solution.py:374
  281.9 4.9 multiply_reduce_fusion.2
  295.1 18.2 %collective-permute-done.25 = bf16[256,2048]{1,0:T(8,128)(2,1)} collective-permute-done((bf16[256,2048]{1,0:T(8,128)(2,1)}, bf16[256,2048]{1,0:T(8,128)(2,1)}, u32[]{:S(2)}, u32[]{:S(2)}) %collective-permute-start.25) | collective-permute-done | bytes 1048608 | tf_op jit(solution)/shard_map/ppermute | solution.py:374
  319.9 15.9 %collective-permute-done.21 = bf16[256,2048]{1,0:T(8,128)(2,1)} collective-permute-done((bf16[256,2048]{1,0:T(8,128)(2,1)}, bf16[256,2048]{1,0:T(8,128)(2,1)}, u32[]{:S(2)}, u32[]{:S(2)}) %collective-permute-start.21) | collective-permute-done | bytes 1048608 | tf_op jit(solution)/shard_map/ppermute | solution.py:374
  348.5 9.2 constant_dynamic-slice_fusion.11
  363.9 5.1 maximum_select_fusion
  369.0 13.0 %fusion.62 = f32[1024,1408]{1,0:T(8,128)} fusion(bf16[2048,1408]{1,0:T(8,128)(2,1)S(1)} %bitcast.211, bf16[256,2048]{1,0:T(8,128)(2,1)} %collective-permute-done.27, bf16[256,2048]{1,0:T(8,128)(2,1)} %collective-permute-done.26, bf16[256,2048]{1,0:T(8,128)(2,1)} %collective-permute-done.25, bf16[256,2048]{1,0:T(8,128)(2,1)} %multiply_convert_fusion.4), kind=kOutput, calls=%fused_computation.234 | convolution fusion | flops 5922357248 | bytes 15728640 | tf_op jit(solution)/shard_map/dot_general | solution.py:55
  382.0 15.7 %collective-permute-done.29 = bf16[1024,1408]{1,0:T(8,128)(2,1)} collective-permute-done((bf16[1024,1408]{1,0:T(8,128)(2,1)}, bf16[1024,1408]{1,0:T(8,128)(2,1)}, u32[]{:S(2)}, u32[]{:S(2)}) %collective-permute-start.29) | collective-permute-done | bytes 2883616 | tf_op jit(solution)/shard_map/ppermute | solution.py:374
  405.3 5.2 maximum_select_fusion.1
  411.4 13.2 %multiply_convert_fusion.2 = (bf16[1024,1408]{1,0:T(8,128)(2,1)}, f32[1024,1408]{1,0:T(8,128)}) fusion(f32[1024,1408]{1,0:T(8,128)S(1)} %copy-done.72, bf16[2048,1408]{1,0:T(8,128)(2,1)S(1)} %bitcast.215, bf16[256,2048]{1,0:T(8,128)(2,1)} %collective-permute-done.27, bf16[256,2048]{1,0:T(8,128)(2,1)} %collective-permute-done.26, ...), kind=kOutput, calls=%fused_computation.9 | convolution fusion | flops 5931008000 | bytes 24379392 | tf_op jit(solution)/shard_map/dot_general | solution.py:55
  430.6 10.5 %convolution_convert_fusion.2 = bf16[1408,2048]{1,0:T(8,128)(2,1)} fusion(bf16[1024,1408]{1,0:T(8,128)(2,1)} %get-tuple-element.194, bf16[1024,2048]{1,0:T(8,128)(2,1)} %constant_dynamic-update-slice_fusion.2), kind=kOutput, calls=%fused_computation.2 | convolution fusion | flops 5908463616 | bytes 12845056 | tf_op jit(solution)/shard_map/dot_general | solution.py:59
  448.1 17.5 %multiply_convert_fusion = (bf16[1024,1408]{1,0:T(8,128)(2,1)S(1)}, bf16[1024,1408]{1,0:T(8,128)(2,1)}) fusion(f32[1024,1408]{1,0:T(8,128)} %fusion.62, f32[1024,1408]{1,0:T(8,128)} %get-tuple-element.302, bf16[1024,2048]{1,0:T(8,128)(2,1)} %constant_dynamic-update-slice_fusion.2, bf16[1408,2048]{1,0:T(8,128)(2,1)} %all-gather.10.cloned.1.call-done), kind=kOutput, calls=%fused_computation.7 | convolution fusion | flops 5924323328 | bytes 27262976 | tf_op jit(solution)/shard_map/dot_general | solution.py:63
  465.6 10.3 %fusion.71 = f32[1024,2048]{1,0:T(8,128)} fusion(bf16[1024,1408]{1,0:T(8,128)(2,1)} %get-tuple-element.166, bf16[2048,1408]{1,0:T(8,128)(2,1)S(1)} %bitcast.214), kind=kOutput, calls=%fused_computation.242 | convolution fusion | flops 5905580032 | bytes 17039360 | tf_op jit(solution)/shard_map/dot_general | solution.py:63
  475.9 11.9 %fusion.69 = (bf16[1024,2048]{1,0:T(8,128)(2,1)}, f32[1024,2048]{1,0:T(8,128)}) fusion(f32[1024,2048]{1,0:T(8,128)} %fusion.71, bf16[1024,1408]{1,0:T(8,128)(2,1)S(1)} %get-tuple-element.167, bf16[2048,1408]{1,0:T(8,128)(2,1)S(1)} %bitcast.218), kind=kOutput, calls=%fused_computation.240 | convolution fusion | flops 5909774336 | bytes 29622272 | tf_op jit(solution)/shard_map/dot_general | solution.py:63
  487.9 10.8 %convolution_convert_fusion.1 = bf16[2048,1408]{1,0:T(8,128)(2,1)} fusion(bf16[1024,1408]{1,0:T(8,128)(2,1)S(1)} %copy-done.73, bf16[256,2048]{1,0:T(8,128)(2,1)} %collective-permute-done.27, bf16[256,2048]{1,0:T(8,128)(2,1)} %collective-permute-done.26, bf16[256,2048]{1,0:T(8,128)(2,1)} %collective-permute-done.25, bf16[256,2048]{1,0:T(8,128)(2,1)} %multiply_convert_fusion.4), kind=kOutput, calls=%fused_computation.1 | convolution fusion | flops 5925240832 | bytes 12845056 | tf_op jit(solution)/shard_map/dot_general | solution.py:59
  498.7 11.1 %convolution_convert_fusion = bf16[2048,1408]{1,0:T(8,128)(2,1)} fusion(bf16[1024,1408]{1,0:T(8,128)(2,1)S(1)} %get-tuple-element.167, bf16[256,2048]{1,0:T(8,128)(2,1)} %collective-permute-done.27, bf16[256,2048]{1,0:T(8,128)(2,1)} %collective-permute-done.26, bf16[256,2048]{1,0:T(8,128)(2,1)} %collective-permute-done.25, ...), kind=kOutput, calls=%fused_computation | convolution fusion | flops 5925240832 | bytes 12845056 | tf_op jit(solution)/shard_map/dot_general | solution.py:59
  521.4 20.7 %collective-permute-done.38 = bf16[256,2048]{1,0:T(8,128)(2,1)S(1)} collective-permute-done((bf16[256,2048]{1,0:T(8,128)(2,1)}, bf16[256,2048]{1,0:T(8,128)(2,1)S(1)}, u32[]{:S(2)}, u32[]{:S(2)}) %collective-permute-start.38) | collective-permute-done | bytes 1048608 | tf_op jit(solution)/shard_map/ppermute | solution.py:379
  548.7 18.1 %convolution_convert_fusion.3.do_ref = bf16[256,4096]{1,0:T(8,128)(2,1)} fusion(bf16[256,2048]{1,0:T(8,128)(2,1)S(1)} %get-tuple-element.231, bf16[4096,2048]{1,0:T(8,128)(2,1)} %bitcast.204), kind=kOutput, calls=%fused_computation.12 | convolution fusion | flops 4296015872 | bytes 19922944 | tf_op jit(solution)/shard_map/dot_general | solution.py:63
  571.7 21.0 %shard_map.205 = (bf16[256,4096]{1,0:T(8,128)(2,1)S(1)}, bf16[2048,512]{1,0:T(8,128)(2,1)S(1)}) custom-call(s32[2]{0:T(128)S(1)} %copy-done.14, bf16[256,4096]{1,0:T(8,128)(2,1)S(1)} %copy-done.9, bf16[256,4096]{1,0:T(8,128)(2,1)S(1)} %copy-done.10, bf16[256,4096]{1,0:T(8,128)(2,1)S(1)} %copy-done.7, f32[16,1,256]{2,1,0:T(1,128)S(1)} %get-tuple-element.169.lse_ref, ...), custom_call_target="tpu_custom_call" | custom-call | flops 1000 | bytes 1000 | tf_op jit(solution)/shard_map/pallas_call | solution.py:239
  594.1 6.3 multiply_reduce_fusion.4
  608.7 8.8 collective-permute-done.39
  625.5 7.1 convolution_convert_fusion.4
  635.6 15.4 %collective-permute-start.40 = (bf16[256,512]{1,0:T(8,128)(2,1)}, bf16[256,512]{1,0:T(8,128)(2,1)S(1)}, u32[]{:S(2)}, u32[]{:S(2)}) collective-permute-start(bf16[256,512]{1,0:T(8,128)(2,1)} %get-tuple-element.287), channel_id=1, source_target_pairs={{0,2},{2,4},{4,6},{6,0},{1,3},{3,5},{5,7},{7,1},{8,10},{10,12},{12... | collective-permute-start | bytes 786440 | tf_op jit(solution)/shard_map/ppermute | solution.py:379
  656.2 5.1 fusion.25
  662.5 15.5 %collective-permute-done.40 = bf16[256,512]{1,0:T(8,128)(2,1)S(1)} collective-permute-done((bf16[256,512]{1,0:T(8,128)(2,1)}, bf16[256,512]{1,0:T(8,128)(2,1)S(1)}, u32[]{:S(2)}, u32[]{:S(2)}) %collective-permute-start.40) | collective-permute-done | bytes 262176 | tf_op jit(solution)/shard_map/ppermute | solution.py:379
  677.9 21.0 %collective-permute-done.41 = bf16[256,512]{1,0:T(8,128)(2,1)S(1)} collective-permute-done((bf16[256,512]{1,0:T(8,128)(2,1)}, bf16[256,512]{1,0:T(8,128)(2,1)S(1)}, u32[]{:S(2)}, u32[]{:S(2)}) %collective-permute-start.41) | collective-permute-done | bytes 262176 | tf_op jit(solution)/shard_map/ppermute | solution.py:379
  706.7 6.7 collective-permute-done.52
  721.9 7.2 fusion.70
  732.5 10.9 %fusion.72 = f32[1024,2048]{1,0:T(8,128)} fusion(bf16[1024,1408]{1,0:T(8,128)(2,1)S(1)} %copy-done.71, bf16[1408,2048]{1,0:T(8,128)(2,1)} %all-gather.10.cloned.1.call-done), kind=kOutput, calls=%fused_computation.243 | convolution fusion | flops 5905580032 | bytes 17039360 | tf_op jit(solution)/shard_map/dot_general | solution.py:55
  756.9 5.1 collective-permute-start.56
  762.0 12.7 %collective-permute-done.61 = bf16[256,2048]{1,0:T(8,128)(2,1)} collective-permute-done((bf16[256,2048]{1,0:T(8,128)(2,1)}, bf16[256,2048]{1,0:T(8,128)(2,1)}, u32[]{:S(2)}, u32[]{:S(2)}) %collective-permute-start.61) | collective-permute-done | bytes 1048608 | tf_op jit(solution)/shard_map/ppermute | solution.py:379
  777.7 11.3 %collective-permute-done.72 = bf16[176,2048]{1,0:T(8,128)(2,1)} collective-permute-done((bf16[176,2048]{1,0:T(8,128)(2,1)}, bf16[176,2048]{1,0:T(8,128)(2,1)}, u32[]{:S(2)}, u32[]{:S(2)}) %collective-permute-start.72) | collective-permute-done | bytes 720928 | tf_op jit(solution)/shard_map/ppermute | solution.py:379
  791.4 13.0 %collective-permute-done.62 = bf16[256,1408]{1,0:T(8,128)(2,1)S(1)} collective-permute-done((bf16[256,1408]{1,0:T(8,128)(2,1)S(1)}, bf16[256,1408]{1,0:T(8,128)(2,1)S(1)}, u32[]{:S(2)}, u32[]{:S(2)}) %collective-permute-start.62) | collective-permute-done | bytes 720928 | tf_op jit(solution)/shard_map/ppermute | solution.py:379
  805.5 6.5 convert.49
  822.2 21.9 %collective-permute-done.66.refs_4_ = bf16[256,1408]{1,0:T(8,128)(2,1)} collective-permute-done((bf16[256,1408]{1,0:T(8,128)(2,1)}, bf16[256,1408]{1,0:T(8,128)(2,1)}, u32[]{:S(2)}, u32[]{:S(2)}) %collective-permute-start.66) | collective-permute-done | bytes 720928 | tf_op jit(solution)/shard_map/ppermute | solution.py:374
  859.2 13.5 %shard_map.206 = (f32[256,11264]{1,0:T(8,128)}, f32[256,1]{1,0:T(8,128)}) custom-call(s32[4]{0:T(128)} %copy-done.59, f32[256,1]{1,0:T(8,128)} %copy.32.refs_1_, bf16[256,11264]{1,0:T(8,128)(2,1)} %refs_2_.2, bf16[256,1408]{1,0:T(8,128)(2,1)} %reduce-scatter.10.cloned.1.call-done.refs_3_, bf16[256,1408]{1,0:T(8,128)(2,1)} %collective-permute-done.66.refs_4_, ...), custom_call_target="tpu_custom_call" | custom-call | flops 1000 | bytes 1000 | tf_op jit(solution)/shard_map/pallas_call | solution.py:310
  883.2 15.8 %collective-permute-done.71 = bf16[256,2048]{1,0:T(8,128)(2,1)S(1)} collective-permute-done((bf16[256,2048]{1,0:T(8,128)(2,1)S(1)}, bf16[256,2048]{1,0:T(8,128)(2,1)S(1)}, u32[]{:S(2)}, u32[]{:S(2)}) %collective-permute-start.71) | collective-permute-done | bytes 1048608 | tf_op jit(solution)/shard_map/ppermute | solution.py:379
  (497 shorter events, 306.1 us)
Async XLA Ops:
  7.2 98.5 %all-gather.8.cloned.1.call-start = ((), (), s32[]{:S(2)}) async-start(), calls=%async_computation.6 | async-start | bytes 2621440 | tf_op jit(solution)/shard_map/all_gather | solution.py:464
  9.3 201.9 %all-gather.6.cloned.1.call-start = ((), (), s32[]{:S(2)}) async-start(), calls=%async_computation.5 | async-start | bytes 8650752 | tf_op jit(solution)/shard_map/all_gather | solution.py:633
  14.1 251.3 %all-gather.12.cloned.1.call-start = ((), (), s32[]{:S(2)}) async-start(), calls=%async_computation.8 | async-start | bytes 3604480 | tf_op jit(solution)/shard_map/all_gather | solution.py:464
  18.7 62.0 %collective-permute-start = (bf16[256,2048]{1,0:T(8,128)(2,1)}, bf16[256,2048]{1,0:T(8,128)(2,1)}, u32[]{:S(2)}, u32[]{:S(2)}) collective-permute-start(bf16[256,2048]{1,0:T(8,128)(2,1)} %fusion.4), channel_id=1, source_target_pairs={{16,0},{0,16},{17,1},{1,17},{18,2},{2,18},{19,3},{3,19},{20,4},{4,... | collective-permute-start | bytes 3145736 | tf_op jit(solution)/shard_map/ppermute | solution.py:374
  25.6 37.3 %collective-permute-start.5 = (bf16[256,384]{1,0:T(8,128)(2,1)S(1)}, bf16[256,384]{1,0:T(8,128)(2,1)S(1)}, u32[]{:S(2)}, u32[]{:S(2)}) collective-permute-start(bf16[256,384]{1,0:T(8,128)(2,1)S(1)} %get-tuple-element.234), channel_id=1, source_target_pairs={{6,0},{0,2},{2,4},{4,6},{7,1},{1,3},{3,5},{5,7},{14,8},{8,10},{10,... | collective-permute-start | bytes 589832 | tf_op jit(solution)/shard_map/ppermute | solution.py:374
  77.2 242.7 %all-gather.14.cloned.1.call-start = ((), (), s32[]{:S(2)}) async-start(), calls=%async_computation.9 | async-start | bytes 3604480 | tf_op jit(solution)/shard_map/all_gather | solution.py:464
  105.7 73.9 %collective-permute-start.14 = (bf16[512,2048]{1,0:T(8,128)(2,1)}, bf16[512,2048]{1,0:T(8,128)(2,1)}, u32[]{:S(2)}, u32[]{:S(2)}) collective-permute-start(bf16[512,2048]{1,0:T(8,128)(2,1)} %all-gather.8.cloned.1.call-done), channel_id=1, source_target_pairs={{1,0},{0,1},{3,2},{2,3},{5,4},{4,5},{7,6},{6,7},{9,8},{8,9},{11,10... | collective-permute-start | bytes 6291464 | tf_op jit(solution)/shard_map/ppermute | solution.py:374
  108.1 94.0 %collective-permute-start.15 = (bf16[512,2048]{1,0:T(8,128)(2,1)}, bf16[512,2048]{1,0:T(8,128)(2,1)}, u32[]{:S(2)}, u32[]{:S(2)}) collective-permute-start(bf16[512,2048]{1,0:T(8,128)(2,1)} %all-gather.8.cloned.1.call-done), channel_id=1, source_target_pairs={{16,0},{0,16},{17,1},{1,17},{18,2},{2,18},{19,3},{3,19},{20,4},{4,... | collective-permute-start | bytes 6291464 | tf_op jit(solution)/shard_map/ppermute | solution.py:374
  135.1 41.2 %collective-permute-start.12 = (bf16[256,512]{1,0:T(8,128)(2,1)S(1)}, bf16[256,512]{1,0:T(8,128)(2,1)S(1)}, u32[]{:S(2)}, u32[]{:S(2)}) collective-permute-start(bf16[256,512]{1,0:T(8,128)(2,1)S(1)} %pad_maximum_fusion.12), channel_id=1, source_target_pairs={{6,0},{0,2},{2,4},{4,6},{7,1},{1,3},{3,5},{5,7},{14,8},{8,10},{10,... | collective-permute-start | bytes 786440 | tf_op jit(solution)/shard_map/ppermute | solution.py:374
  177.5 227.8 %all-gather.10.cloned.1.call-start = ((), (), s32[]{:S(2)}) async-start(), calls=%async_computation.7 | async-start | bytes 7208960 | tf_op jit(solution)/shard_map/all_gather | solution.py:464
  179.6 62.5 %collective-permute-start.16 = (bf16[512,2048]{1,0:T(8,128)(2,1)}, bf16[512,2048]{1,0:T(8,128)(2,1)}, u32[]{:S(2)}, u32[]{:S(2)}) collective-permute-start(bf16[512,2048]{1,0:T(8,128)(2,1)} %collective-permute-done.14), channel_id=1, source_target_pairs={{16,0},{0,16},{17,1},{1,17},{18,2},{2,18},{19,3},{3,19},{20,4},{4,... | collective-permute-start | bytes 6291464 | tf_op jit(solution)/shard_map/ppermute | solution.py:374
  244.3 34.7 %collective-permute-start.19 = (bf16[512,2048]{1,0:T(8,128)(2,1)}, bf16[512,2048]{1,0:T(8,128)(2,1)S(1)}, u32[]{:S(2)}, u32[]{:S(2)}) collective-permute-start(bf16[512,2048]{1,0:T(8,128)(2,1)} %collective-permute-done.14), channel_id=1, source_target_pairs={{8,0},{0,8},{9,1},{1,9},{10,2},{2,10},{11,3},{3,11},{12,4},{4,12},... | collective-permute-start | bytes 6291464 | tf_op jit(solution)/shard_map/ppermute | solution.py:374
  246.4 33.0 %collective-permute-start.20 = (bf16[512,2048]{1,0:T(8,128)(2,1)}, bf16[512,2048]{1,0:T(8,128)(2,1)}, u32[]{:S(2)}, u32[]{:S(2)}) collective-permute-start(bf16[512,2048]{1,0:T(8,128)(2,1)} %collective-permute-done.16), channel_id=1, source_target_pairs={{8,0},{0,8},{9,1},{1,9},{10,2},{2,10},{11,3},{3,11},{12,4},{4,12},... | collective-permute-start | bytes 6291464 | tf_op jit(solution)/shard_map/ppermute | solution.py:374
  264.9 488.4 %reduce-scatter.8.cloned.1.call-start = ((), (), s32[]{:S(2)}) async-start(), calls=%async_computation.11 | async-start | bytes 7208960 | tf_op jit(solution)/shard_map/reduce_scatter | solution.py:472
  265.5 98.1 %collective-permute-start.28 = (bf16[1024,1408]{1,0:T(8,128)(2,1)}, bf16[1024,1408]{1,0:T(8,128)(2,1)}, u32[]{:S(2)}, u32[]{:S(2)}) collective-permute-start(bf16[1024,1408]{1,0:T(8,128)(2,1)} %all-gather.12.cloned.1.call-done), channel_id=1, source_target_pairs={{1,0},{0,1},{3,2},{2,3},{5,4},{4,5},{7,6},{6,7},{9,8},{8,9},{11,10... | collective-permute-start | bytes 8650760 | tf_op jit(solution)/shard_map/ppermute | solution.py:374
  293.0 42.8 %collective-permute-start.21 = (bf16[256,2048]{1,0:T(8,128)(2,1)}, bf16[256,2048]{1,0:T(8,128)(2,1)}, u32[]{:S(2)}, u32[]{:S(2)}) collective-permute-start(bf16[256,2048]{1,0:T(8,128)(2,1)} %fusion.24), channel_id=1, source_target_pairs={{16,0},{0,16},{17,1},{1,17},{18,2},{2,18},{19,3},{3,19},{20,4},{4,... | collective-permute-start | bytes 3145736 | tf_op jit(solution)/shard_map/ppermute | solution.py:374
  293.1 46.1 %collective-permute-start.22 = (bf16[256,2048]{1,0:T(8,128)(2,1)}, bf16[256,2048]{1,0:T(8,128)(2,1)}, u32[]{:S(2)}, u32[]{:S(2)}) collective-permute-start(bf16[256,2048]{1,0:T(8,128)(2,1)} %fusion.24), channel_id=1, source_target_pairs={{8,0},{0,8},{9,1},{1,9},{10,2},{2,10},{11,3},{3,11},{12,4},{4,12},... | collective-permute-start | bytes 3145736 | tf_op jit(solution)/shard_map/ppermute | solution.py:374
  295.1 49.3 %collective-permute-start.26 = (bf16[256,2048]{1,0:T(8,128)(2,1)}, bf16[256,2048]{1,0:T(8,128)(2,1)}, u32[]{:S(2)}, u32[]{:S(2)}) collective-permute-start(bf16[256,2048]{1,0:T(8,128)(2,1)} %multiply_convert_fusion.4), channel_id=1, source_target_pairs={{8,0},{0,8},{9,1},{1,9},{10,2},{2,10},{11,3},{3,11},{12,4},{4,12},... | collective-permute-start | bytes 3145736 | tf_op jit(solution)/shard_map/ppermute | solution.py:374
  335.8 61.9 %collective-permute-start.29 = (bf16[1024,1408]{1,0:T(8,128)(2,1)}, bf16[1024,1408]{1,0:T(8,128)(2,1)}, u32[]{:S(2)}, u32[]{:S(2)}) collective-permute-start(bf16[1024,1408]{1,0:T(8,128)(2,1)} %all-gather.14.cloned.1.call-done), channel_id=1, source_target_pairs={{1,0},{0,1},{3,2},{2,3},{5,4},{4,5},{7,6},{6,7},{9,8},{8,9},{11,10... | collective-permute-start | bytes 8650760 | tf_op jit(solution)/shard_map/ppermute | solution.py:374
  339.3 87.3 %collective-permute-start.23 = (bf16[256,2048]{1,0:T(8,128)(2,1)}, bf16[256,2048]{1,0:T(8,128)(2,1)}, u32[]{:S(2)}, u32[]{:S(2)}) collective-permute-start(bf16[256,2048]{1,0:T(8,128)(2,1)} %collective-permute-done.21), channel_id=1, source_target_pairs={{8,0},{0,8},{9,1},{1,9},{10,2},{2,10},{11,3},{3,11},{12,4},{4,12},... | collective-permute-start | bytes 3145736 | tf_op jit(solution)/shard_map/ppermute | solution.py:374
  344.4 86.2 %collective-permute-start.33 = (bf16[256,1024]{1,0:T(8,128)(2,1)S(1)}, bf16[256,1024]{1,0:T(8,128)(2,1)}, u32[]{:S(2)}, u32[]{:S(2)}) collective-permute-start(bf16[256,1024]{1,0:T(8,128)(2,1)S(1)} %fusion.32.input_ref), channel_id=1, source_target_pairs={{16,0},{0,16},{17,1},{1,17},{18,2},{2,18},{19,3},{3,19},{20,4},{4,... | collective-permute-start | bytes 1572872 | tf_op jit(solution)/shard_map/ppermute | solution.py:374
  345.6 99.6 %collective-permute-start.34 = (bf16[256,1024]{1,0:T(8,128)(2,1)S(1)}, bf16[256,1024]{1,0:T(8,128)(2,1)}, u32[]{:S(2)}, u32[]{:S(2)}) collective-permute-start(bf16[256,1024]{1,0:T(8,128)(2,1)S(1)} %fusion.32.input_ref), channel_id=1, source_target_pairs={{8,0},{0,8},{9,1},{1,9},{10,2},{2,10},{11,3},{3,11},{12,4},{4,12},... | collective-permute-start | bytes 1572872 | tf_op jit(solution)/shard_map/ppermute | solution.py:374
  363.5 78.6 %collective-permute-start.30 = (bf16[256,1024]{0,1:T(8,128)(2,1)}, bf16[256,1024]{0,1:T(8,128)(2,1)}, u32[]{:S(2)}, u32[]{:S(2)}) collective-permute-start(bf16[256,1024]{0,1:T(8,128)(2,1)} %bitcast.236), channel_id=1, source_target_pairs={{16,0},{24,8},{0,16},{8,24},{17,1},{25,9},{1,17},{9,25},{18,2},{26... | collective-permute-start | bytes 1572872 | tf_op jit(solution)/shard_map/ppermute | solution.py:412
  397.7 44.4 %collective-permute-start.31 = (bf16[256,1024]{0,1:T(8,128)(2,1)S(1)}, bf16[256,1024]{0,1:T(8,128)(2,1)}, u32[]{:S(2)}, u32[]{:S(2)}) collective-permute-start(bf16[256,1024]{0,1:T(8,128)(2,1)S(1)} %bitcast.235), channel_id=1, source_target_pairs={{8,0},{0,8},{24,16},{16,24},{9,1},{1,9},{25,17},{17,25},{10,2},{2,... | collective-permute-start | bytes 1572872 | tf_op jit(solution)/shard_map/ppermute | solution.py:412
  442.1 313.6 %reduce-scatter.6.cloned.1.call-start = ((), (), s32[]{:S(2)}) async-start(), calls=%async_computation.10 | async-start | bytes 7208960 | tf_op jit(solution)/shard_map/reduce_scatter | solution.py:472
  509.8 302.2 %reduce-scatter.10.cloned.1.call-start = ((), (), s32[]{:S(2)}) async-start(), calls=%async_computation.12 | async-start | bytes 3604480 | tf_op jit(solution)/shard_map/reduce_scatter | solution.py:472
  521.1 83.1 %collective-permute-start.46 = (bf16[4,256,1408]{2,1,0:T(8,128)(2,1)}, bf16[4,256,1408]{2,1,0:T(8,128)(2,1)}, u32[]{:S(2)}, u32[]{:S(2)}) collective-permute-start(bf16[4,256,1408]{2,1,0:T(8,128)(2,1)} %dynamic-slice_bitcast_fusion), channel_id=1, source_target_pairs={{0,1},{1,0},{2,3},{3,2},{4,5},{5,4},{6,7},{7,6},{8,9},{9,8},{10,11... | collective-permute-start | bytes 8650760 | tf_op jit(solution)/shard_map/ppermute | solution.py:379
  547.3 55.8 %collective-permute-start.43 = (bf16[256,2048]{1,0:T(8,128)(2,1)S(1)}, bf16[256,2048]{1,0:T(8,128)(2,1)}, u32[]{:S(2)}, u32[]{:S(2)}) collective-permute-start(bf16[256,2048]{1,0:T(8,128)(2,1)S(1)} %get-tuple-element.231), channel_id=1, source_target_pairs={{16,0},{0,16},{17,1},{1,17},{18,2},{2,18},{19,3},{3,19},{20,4},{4,... | collective-permute-start | bytes 3145736 | tf_op jit(solution)/shard_map/ppermute | solution.py:374
  547.4 74.6 %collective-permute-start.44 = (bf16[256,2048]{1,0:T(8,128)(2,1)S(1)}, bf16[256,2048]{1,0:T(8,128)(2,1)}, u32[]{:S(2)}, u32[]{:S(2)}) collective-permute-start(bf16[256,2048]{1,0:T(8,128)(2,1)S(1)} %get-tuple-element.231), channel_id=1, source_target_pairs={{8,0},{0,8},{9,1},{1,9},{10,2},{2,10},{11,3},{3,11},{12,4},{4,12},... | collective-permute-start | bytes 3145736 | tf_op jit(solution)/shard_map/ppermute | solution.py:374
  601.7 49.3 %collective-permute-start.47 = (bf16[256,1024]{1,0:T(8,128)(2,1)}, bf16[256,1024]{1,0:T(8,128)(2,1)}, u32[]{:S(2)}, u32[]{:S(2)}) collective-permute-start(bf16[256,1024]{1,0:T(8,128)(2,1)} %get-tuple-element.252), channel_id=1, source_target_pairs={{16,0},{24,8},{0,16},{8,24},{17,1},{25,9},{1,17},{9,25},{18,2},{26... | collective-permute-start | bytes 1572872 | tf_op jit(solution)/shard_map/ppermute | solution.py:412
  604.2 50.5 %collective-permute-start.48 = (bf16[256,1024]{1,0:T(8,128)(2,1)}, bf16[256,1024]{1,0:T(8,128)(2,1)}, u32[]{:S(2)}, u32[]{:S(2)}) collective-permute-start(bf16[256,1024]{1,0:T(8,128)(2,1)} %get-tuple-element.251), channel_id=1, source_target_pairs={{8,0},{0,8},{24,16},{16,24},{9,1},{1,9},{25,17},{17,25},{10,2},{2,... | collective-permute-start | bytes 1572872 | tf_op jit(solution)/shard_map/ppermute | solution.py:412
  617.5 38.6 %collective-permute-start.49 = (bf16[256,1024]{1,0:T(8,128)(2,1)}, bf16[256,1024]{1,0:T(8,128)(2,1)}, u32[]{:S(2)}, u32[]{:S(2)}) collective-permute-start(bf16[256,1024]{1,0:T(8,128)(2,1)} %get-tuple-element.250), channel_id=1, source_target_pairs={{24,0},{16,8},{8,16},{0,24},{25,1},{17,9},{9,17},{1,25},{26,2},{18... | collective-permute-start | bytes 1572872 | tf_op jit(solution)/shard_map/ppermute | solution.py:412
  634.4 79.0 %collective-permute-start.53 = (bf16[4,128,2048]{2,1,0:T(8,128)(2,1)}, bf16[4,128,2048]{2,1,0:T(8,128)(2,1)}, u32[]{:S(2)}, u32[]{:S(2)}) collective-permute-start(bf16[4,128,2048]{2,1,0:T(8,128)(2,1)} %get-tuple-element.241), channel_id=1, source_target_pairs={{0,1},{1,0},{2,3},{3,2},{4,5},{5,4},{6,7},{7,6},{8,9},{9,8},{10,11... | collective-permute-start | bytes 6291464 | tf_op jit(solution)/shard_map/ppermute | solution.py:379
  635.6 42.3 %collective-permute-start.40 = (bf16[256,512]{1,0:T(8,128)(2,1)}, bf16[256,512]{1,0:T(8,128)(2,1)S(1)}, u32[]{:S(2)}, u32[]{:S(2)}) collective-permute-start(bf16[256,512]{1,0:T(8,128)(2,1)} %get-tuple-element.287), channel_id=1, source_target_pairs={{0,2},{2,4},{4,6},{6,0},{1,3},{3,5},{5,7},{7,1},{8,10},{10,12},{12... | collective-permute-start | bytes 786440 | tf_op jit(solution)/shard_map/ppermute | solution.py:379
  651.0 47.9 %collective-permute-start.41 = (bf16[256,512]{1,0:T(8,128)(2,1)}, bf16[256,512]{1,0:T(8,128)(2,1)S(1)}, u32[]{:S(2)}, u32[]{:S(2)}) collective-permute-start(bf16[256,512]{1,0:T(8,128)(2,1)} %get-tuple-element.286), channel_id=1, source_target_pairs={{0,4},{2,6},{4,0},{6,2},{1,5},{3,7},{5,1},{7,3},{8,12},{10,14},{12... | collective-permute-start | bytes 786440 | tf_op jit(solution)/shard_map/ppermute | solution.py:379
  654.7 44.7 %collective-permute-start.42 = (bf16[256,512]{1,0:T(8,128)(2,1)}, bf16[256,512]{1,0:T(8,128)(2,1)S(1)}, u32[]{:S(2)}, u32[]{:S(2)}) collective-permute-start(bf16[256,512]{1,0:T(8,128)(2,1)} %get-tuple-element.285), channel_id=1, source_target_pairs={{0,6},{2,0},{4,2},{6,4},{1,7},{3,1},{5,3},{7,5},{8,14},{10,8},{12,... | collective-permute-start | bytes 786440 | tf_op jit(solution)/shard_map/ppermute | solution.py:379
  661.3 188.8 %reduce-scatter.14.cloned.1.call-start = ((), (), s32[]{:S(2)}) async-start(), calls=%async_computation.14 | async-start | bytes 2621440 | tf_op jit(solution)/shard_map/reduce_scatter | solution.py:472
  745.5 60.0 %collective-permute-start.58 = (bf16[4,128,1024]{2,1,0:T(8,128)(2,1)}, bf16[4,128,1024]{2,1,0:T(8,128)(2,1)S(1)}, u32[]{:S(2)}, u32[]{:S(2)}) collective-permute-start(bf16[4,128,1024]{2,1,0:T(8,128)(2,1)} %get-tuple-element.247), channel_id=1, source_target_pairs={{0,1},{1,0},{2,3},{3,2},{4,5},{5,4},{6,7},{7,6},{8,9},{9,8},{10,11... | collective-permute-start | bytes 3145736 | tf_op jit(solution)/shard_map/ppermute | solution.py:379
  746.6 165.1 %reduce-scatter.12.cloned.1.call-start = ((), (), s32[]{:S(2)}) async-start(), calls=%async_computation.13 | async-start | bytes 1310720 | tf_op jit(solution)/shard_map/reduce_scatter | solution.py:472
  753.3 66.1 %collective-permute-start.55 = (bf16[256,384]{1,0:T(8,128)(2,1)}, bf16[256,384]{1,0:T(8,128)(2,1)}, u32[]{:S(2)}, u32[]{:S(2)}) collective-permute-start(bf16[256,384]{1,0:T(8,128)(2,1)} %get-tuple-element.290), channel_id=1, source_target_pairs={{0,2},{2,4},{4,6},{6,0},{1,3},{3,5},{5,7},{7,1},{8,10},{10,12},{12... | collective-permute-start | bytes 589832 | tf_op jit(solution)/shard_map/ppermute | solution.py:379
  755.4 33.6 %collective-permute-start.72 = (bf16[176,2048]{1,0:T(8,128)(2,1)}, bf16[176,2048]{1,0:T(8,128)(2,1)}, u32[]{:S(2)}, u32[]{:S(2)}) collective-permute-start(bf16[176,2048]{1,0:T(8,128)(2,1)} %dynamic-slice_bitcast_fusion.5), channel_id=1, source_target_pairs={{0,1},{1,0},{2,3},{3,2},{4,5},{5,4},{6,7},{7,6},{8,9},{9,8},{10,11... | collective-permute-start | bytes 2162696 | tf_op jit(solution)/shard_map/ppermute | solution.py:379
  756.9 64.7 %collective-permute-start.56 = (bf16[256,384]{1,0:T(8,128)(2,1)}, bf16[256,384]{1,0:T(8,128)(2,1)}, u32[]{:S(2)}, u32[]{:S(2)}) collective-permute-start(bf16[256,384]{1,0:T(8,128)(2,1)} %get-tuple-element.289), channel_id=1, source_target_pairs={{0,4},{2,6},{4,0},{6,2},{1,5},{3,7},{5,1},{7,3},{8,12},{10,14},{12... | collective-permute-start | bytes 589832 | tf_op jit(solution)/shard_map/ppermute | solution.py:379
  789.0 33.2 %collective-permute-start.57 = (bf16[256,384]{1,0:T(8,128)(2,1)}, bf16[256,384]{1,0:T(8,128)(2,1)}, u32[]{:S(2)}, u32[]{:S(2)}) collective-permute-start(bf16[256,384]{1,0:T(8,128)(2,1)} %get-tuple-element.288), channel_id=1, source_target_pairs={{0,6},{2,0},{4,2},{6,4},{1,7},{3,1},{5,3},{7,5},{8,14},{10,8},{12,... | collective-permute-start | bytes 589832 | tf_op jit(solution)/shard_map/ppermute | solution.py:379
  812.0 34.3 %collective-permute-start.63 = (bf16[256,1408]{1,0:T(8,128)(2,1)}, bf16[256,1408]{1,0:T(8,128)(2,1)}, u32[]{:S(2)}, u32[]{:S(2)}) collective-permute-start(bf16[256,1408]{1,0:T(8,128)(2,1)} %fusion.29.refs_7_), channel_id=1, source_target_pairs={{16,0},{0,16},{17,1},{1,17},{18,2},{2,18},{19,3},{3,19},{20,4},{4,... | collective-permute-start | bytes 2162696 | tf_op jit(solution)/shard_map/ppermute | solution.py:374
  812.0 32.1 %collective-permute-start.66 = (bf16[256,1408]{1,0:T(8,128)(2,1)}, bf16[256,1408]{1,0:T(8,128)(2,1)}, u32[]{:S(2)}, u32[]{:S(2)}) collective-permute-start(bf16[256,1408]{1,0:T(8,128)(2,1)} %reduce-scatter.10.cloned.1.call-done.refs_3_), channel_id=1, source_target_pairs={{16,0},{0,16},{17,1},{1,17},{18,2},{2,18},{19,3},{3,19},{20,4},{4,... | collective-permute-start | bytes 2162696 | tf_op jit(solution)/shard_map/ppermute | solution.py:374
  819.3 31.7 %collective-permute-start.70 = (bf16[256,2048]{1,0:T(8,128)(2,1)}, bf16[256,2048]{1,0:T(8,128)(2,1)}, u32[]{:S(2)}, u32[]{:S(2)}) collective-permute-start(bf16[256,2048]{1,0:T(8,128)(2,1)} %get-tuple-element.238), channel_id=1, source_target_pairs={{0,8},{8,0},{1,9},{9,1},{2,10},{10,2},{3,11},{11,3},{4,12},{12,4},... | collective-permute-start | bytes 3145736 | tf_op jit(solution)/shard_map/ppermute | solution.py:379
  849.6 33.6 %collective-permute-start.69 = (bf16[256,2048]{1,0:T(8,128)(2,1)}, bf16[256,2048]{1,0:T(8,128)(2,1)S(1)}, u32[]{:S(2)}, u32[]{:S(2)}) collective-permute-start(bf16[256,2048]{1,0:T(8,128)(2,1)} %get-tuple-element.237), channel_id=1, source_target_pairs={{0,8},{8,0},{1,9},{9,1},{2,10},{10,2},{3,11},{11,3},{4,12},{12,4},... | collective-permute-start | bytes 3145736 | tf_op jit(solution)/shard_map/ppermute | solution.py:379
  853.3 45.7 %collective-permute-start.71 = (bf16[256,2048]{1,0:T(8,128)(2,1)S(1)}, bf16[256,2048]{1,0:T(8,128)(2,1)S(1)}, u32[]{:S(2)}, u32[]{:S(2)}) collective-permute-start(bf16[256,2048]{1,0:T(8,128)(2,1)S(1)} %add_convert_fusion.2), channel_id=1, source_target_pairs={{0,16},{16,0},{1,17},{17,1},{2,18},{18,2},{3,19},{19,3},{4,20},{20... | collective-permute-start | bytes 3145736 | tf_op jit(solution)/shard_map/ppermute | solution.py:379
  (127 other events, 2003.3 us)
Sparse Core Ops, SparseCore 0:
  10.2 60.5 all-gather.7
  73.6 102.6 all-gather.5
  178.5 59.8 all-gather.11
  240.4 57.8 all-gather.13
  300.3 104.9 all-gather.9
  442.2 106.3 reduce-scatter.7
  550.9 104.0 reduce-scatter.5
  661.4 64.7 reduce-scatter.9
  746.7 61.2 reduce-scatter.13
  819.4 28.1 reduce-scatter.11

commit v4 on v2

--- a/solution.py
+++ b/solution.py
@@ -63,7 +63,7 @@
     return lax.dot_general(left, right, (((1,), (1,)), ((), ())), preferred_element_type=F32)
 
 
-STEP_HEADS = 2
+STEP_HEADS = 4
 LIGHT = 1000
 NEG = -1e30
 

time: 907 us -> 901 us (level)
  transfers between devices with their start and end apart: 95 -> 95, of which waited for: 30 -> 30; matrix products, arithmetic and copies ran while one was open for 38% -> 39% of each run, Pallas kernels for 8% -> 7%
where the time goes in v4:
time: 901 us; the launch traced here: 893 us
  waiting for transfers between devices  323 us (36%)
  matrix products  161 us (18%)
  local copies, waits for them, and re-layouts  126 us (14%)
  other arithmetic  106 us (12%)
  starting transfers between devices  95.7 us (11%)
  Pallas kernels  64.6 us (7%)
  between operations  16 us (2%)
    ppermute x51, waiting for transfers between devices, from_ahead(): return lax.ppermute(value, axis, [((j + step) % n, j) for j in range(n)])  178 us
    ppermute x22, waiting for transfers between devices, to_ahead(): return lax.ppermute(value, axis, [(j, (j + step) % n) for j in range(n)])  107 us
    dot_general x6, matrix products, contract_cols(): lax.dot_general(left, right, (((1,), (1,)), ((), ())), preferred_element_...  68.5 us
    unnamed x178, local copies, waits for them, and re-layouts  51.2 us
    dot_general x5, matrix products, matmul(): return jnp.dot(left, right, preferred_element_type=F32)  48.7 us
    ppermute x51, starting transfers between devices, from_ahead(): return lax.ppermute(value, axis, [((j + step) % n, j) for j in range(n)])  48.2 us
    dot_general x6, matrix products, contract_rows(): lax.dot_general(left, right, (((0,), (0,)), ((), ())), preferred_element_...  44.2 us
    ppermute x22, starting transfers between devices, to_ahead(): return lax.ppermute(value, axis, [(j, (j + step) % n) for j in range(n)])  33.2 us
  transfers between devices with their start and end apart: 95, of which 30 were waited for; matrix products, arithmetic and copies ran while one was open for 39% of the time, Pallas kernels for 7%

profile of v4, /device:TPU:13, one launch (start us, length us, event | category | flops | bytes accessed | tf_op | source)
XLA Modules:
  0.0 892.8 jit_solution(9892843674562597646)
XLA Ops:
  27.8 13.1 %collective-permute-done.3 = bf16[256,384]{1,0:T(8,128)(2,1)S(1)} collective-permute-done((bf16[256,384]{1,0:T(8,128)(2,1)S(1)}, bf16[256,384]{1,0:T(8,128)(2,1)S(1)}, u32[]{:S(2)}, u32[]{:S(2)}) %collective-permute-start.3) | collective-permute-done | bytes 196640 | tf_op jit(solution)/shard_map/ppermute | solution.py:374
  40.9 7.3 collective-permute-done.4
  48.2 14.7 %collective-permute-done.5 = bf16[256,384]{1,0:T(8,128)(2,1)S(1)} collective-permute-done((bf16[256,384]{1,0:T(8,128)(2,1)S(1)}, bf16[256,384]{1,0:T(8,128)(2,1)S(1)}, u32[]{:S(2)}, u32[]{:S(2)}) %collective-permute-start.5) | collective-permute-done | bytes 196640 | tf_op jit(solution)/shard_map/ppermute | solution.py:374
  64.9 12.3 %shard_map.204 = (bf16[256,1408]{1,0:T(8,128)(2,1)}, bf16[256,1408]{1,0:T(8,128)(2,1)}) custom-call(s32[1]{0:T(128)} %bitcast.35.refs_0_, f32[256,1]{1,0:T(8,128)} %copy.32.refs_1_, bf16[256,11264]{1,0:T(8,128)(2,1)} %refs_2_.2), custom_call_target="tpu_custom_call" | custom-call | flops 1000 | bytes 1000 | tf_op jit(solution)/shard_map/pallas_call | solution.py:355
  88.0 6.5 fusion.33
  110.3 17.7 %collective-permute-done.9 = f32[256,384]{1,0:T(8,128)} collective-permute-done((f32[256,384]{1,0:T(8,128)}, f32[256,384]{1,0:T(8,128)}, u32[]{:S(2)}, u32[]{:S(2)}) %collective-permute-start.9) | collective-permute-done | bytes 393248 | tf_op jit(solution)/shard_map/ppermute | solution.py:676
  135.2 20.5 %collective-permute-done.10 = bf16[256,512]{1,0:T(8,128)(2,1)S(1)} collective-permute-done((bf16[256,512]{1,0:T(8,128)(2,1)S(1)}, bf16[256,512]{1,0:T(8,128)(2,1)S(1)}, u32[]{:S(2)}, u32[]{:S(2)}) %collective-permute-start.10) | collective-permute-done | bytes 262176 | tf_op jit(solution)/shard_map/ppermute | solution.py:374
  155.7 6.5 collective-permute-done.11
  162.2 14.2 %collective-permute-done.12 = bf16[256,512]{1,0:T(8,128)(2,1)S(1)} collective-permute-done((bf16[256,512]{1,0:T(8,128)(2,1)S(1)}, bf16[256,512]{1,0:T(8,128)(2,1)S(1)}, u32[]{:S(2)}, u32[]{:S(2)}) %collective-permute-start.12) | collective-permute-done | bytes 262176 | tf_op jit(solution)/shard_map/ppermute | solution.py:374
  182.6 19.5 %collective-permute-done.13 = bf16[4,256,512]{2,1,0:T(8,128)(2,1)} collective-permute-done((bf16[4,256,512]{2,1,0:T(8,128)(2,1)}, bf16[4,256,512]{2,1,0:T(8,128)(2,1)}, u32[]{:S(2)}, u32[]{:S(2)}) %collective-permute-start.13) | collective-permute-done | bytes 1048608 | tf_op jit(solution)/shard_map/ppermute | solution.py:374
  214.5 19.9 %shard_map.203 = (bf16[256,4096]{1,0:T(8,128)(2,1)S(1)}, bf16[256,4096]{1,0:T(8,128)(2,1)S(1)}, f32[16,1,256]{2,1,0:T(1,128)S(1)}) custom-call(s32[2]{0:T(128)S(1)} %copy-done.13, bf16[256,1024]{1,0:T(8,128)(2,1)S(1)} %fusion.32.input_ref, bf16[1024,4096]{1,0:T(8,128)(2,1)} %all-gather.6.cloned.1.call-done.up_ref, f32[256,128]{1,0:T(8,128)S(1)} %copy-done.11, ...), custom_call_target="tpu_custom_call" | custom-call | flops 1000 | bytes 1000 | tf_op jit(solution)/shard_map/pallas_call | solution.py:142
  241.2 15.3 %collective-permute-done.24 = bf16[176,2048]{1,0:T(8,128)(2,1)S(1)} collective-permute-done((bf16[176,2048]{1,0:T(8,128)(2,1)}, bf16[176,2048]{1,0:T(8,128)(2,1)S(1)}, u32[]{:S(2)}, u32[]{:S(2)}) %collective-permute-start.24) | collective-permute-done | bytes 720928 | tf_op jit(solution)/shard_map/ppermute | solution.py:374
  276.4 4.9 multiply_reduce_fusion.2
  289.9 17.7 %collective-permute-done.25 = bf16[256,2048]{1,0:T(8,128)(2,1)} collective-permute-done((bf16[256,2048]{1,0:T(8,128)(2,1)}, bf16[256,2048]{1,0:T(8,128)(2,1)}, u32[]{:S(2)}, u32[]{:S(2)}) %collective-permute-start.25) | collective-permute-done | bytes 1048608 | tf_op jit(solution)/shard_map/ppermute | solution.py:374
  307.5 4.8 collective-permute-start.27
  314.8 15.2 %collective-permute-done.21 = bf16[256,2048]{1,0:T(8,128)(2,1)} collective-permute-done((bf16[256,2048]{1,0:T(8,128)(2,1)}, bf16[256,2048]{1,0:T(8,128)(2,1)}, u32[]{:S(2)}, u32[]{:S(2)}) %collective-permute-start.21) | collective-permute-done | bytes 1048608 | tf_op jit(solution)/shard_map/ppermute | solution.py:374
  343.2 9.2 %constant_dynamic-slice_fusion.11 = (bf16[256,8,1,128]{3,2,1,0:T(2,128)(2,1)S(1)}, bf16[256,8,1,128]{3,2,1,0:T(2,128)(2,1)}, bf16[256,8,1,128]{3,2,1,0:T(2,128)(2,1)}, bf16[256,8,1,128]{3,2,1,0:T(2,128)(2,1)S(1)}) fusion(bf16[256,8,4,128]{3,2,1,0:T(4,128)(2,1)} %reshape.310, s32[]{:T(128)S(6)} %select_n.232, s32[]{:T(128)S(6)} %select_n.233, ...), kind=kLoop, calls=%fused_computation.195 | loop fusion | bytes 4194320 | tf_op jit(solution)/shard_map/jit(dynamic_index_in_dim)/dynamic_slice | solution.py:721
  355.1 5.2 maximum_select_fusion
  360.3 13.2 %fusion.62 = f32[1024,1408]{1,0:T(8,128)} fusion(bf16[2048,1408]{1,0:T(8,128)(2,1)S(1)} %bitcast.211, bf16[256,2048]{1,0:T(8,128)(2,1)} %collective-permute-done.27, bf16[256,2048]{1,0:T(8,128)(2,1)} %collective-permute-done.26, bf16[256,2048]{1,0:T(8,128)(2,1)} %collective-permute-done.25, bf16[256,2048]{1,0:T(8,128)(2,1)} %multiply_convert_fusion.4), kind=kOutput, calls=%fused_computation.234 | convolution fusion | flops 5922357248 | bytes 15728640 | tf_op jit(solution)/shard_map/dot_general | solution.py:55
  379.0 13.2 %collective-permute-done.29 = bf16[1024,1408]{1,0:T(8,128)(2,1)} collective-permute-done((bf16[1024,1408]{1,0:T(8,128)(2,1)}, bf16[1024,1408]{1,0:T(8,128)(2,1)}, u32[]{:S(2)}, u32[]{:S(2)}) %collective-permute-start.29) | collective-permute-done | bytes 2883616 | tf_op jit(solution)/shard_map/ppermute | solution.py:374
  395.5 9.9 %all-gather.10.cloned.1.call-done = bf16[1408,2048]{1,0:T(8,128)(2,1)} async-done(((bf16[352,2048]{1,0:T(8,128)(2,1)}), bf16[1408,2048]{1,0:T(8,128)(2,1)}) %all-gather.10.cloned.1.call-update) | async-done | bytes 5767184 | tf_op jit(solution)/shard_map/all_gather | solution.py:464
  407.1 7.8 maximum_select_fusion.1
  426.0 12.5 %multiply_convert_fusion.2 = (bf16[1024,1408]{1,0:T(8,128)(2,1)S(1)}, f32[1024,1408]{1,0:T(8,128)}) fusion(f32[1024,1408]{1,0:T(8,128)} %fusion.62, bf16[2048,1408]{1,0:T(8,128)(2,1)S(1)} %bitcast.218, bf16[256,2048]{1,0:T(8,128)(2,1)} %collective-permute-done.27, bf16[256,2048]{1,0:T(8,128)(2,1)} %collective-permute-done.26, ...), kind=kOutput, calls=%fused_computation.9 | convolution fusion | flops 5931008000 | bytes 24379392 | tf_op jit(solution)/shard_map/dot_general | solution.py:55
  440.1 8.1 convolution_convert_fusion.2
  448.3 15.6 %multiply_convert_fusion = (bf16[1024,1408]{1,0:T(8,128)(2,1)S(1)}, bf16[1024,1408]{1,0:T(8,128)(2,1)}) fusion(f32[1024,1408]{1,0:T(8,128)} %fusion.62, f32[1024,1408]{1,0:T(8,128)} %get-tuple-element.304, bf16[1024,2048]{1,0:T(8,128)(2,1)} %constant_dynamic-update-slice_fusion.2, bf16[1408,2048]{1,0:T(8,128)(2,1)} %all-gather.10.cloned.1.call-done), kind=kOutput, calls=%fused_computation.7 | convolution fusion | flops 5924323328 | bytes 27262976 | tf_op jit(solution)/shard_map/dot_general | solution.py:63
  463.9 8.5 fusion.71
  472.4 12.6 %fusion.69 = (bf16[1024,2048]{1,0:T(8,128)(2,1)}, f32[1024,2048]{1,0:T(8,128)}) fusion(f32[1024,2048]{1,0:T(8,128)S(1)} %fusion.71, bf16[1024,1408]{1,0:T(8,128)(2,1)S(1)} %get-tuple-element.169, bf16[2048,1408]{1,0:T(8,128)(2,1)} %bitcast.215), kind=kOutput, calls=%fused_computation.240 | convolution fusion | flops 5909774336 | bytes 29622272 | tf_op jit(solution)/shard_map/dot_general | solution.py:63
  485.0 11.0 %convolution_convert_fusion.1 = bf16[2048,1408]{1,0:T(8,128)(2,1)} fusion(bf16[1024,1408]{1,0:T(8,128)(2,1)S(1)} %copy-done.71, bf16[256,2048]{1,0:T(8,128)(2,1)} %collective-permute-done.27, bf16[256,2048]{1,0:T(8,128)(2,1)} %collective-permute-done.26, bf16[256,2048]{1,0:T(8,128)(2,1)} %collective-permute-done.25, bf16[256,2048]{1,0:T(8,128)(2,1)} %multiply_convert_fusion.4), kind=kOutput, calls=%fused_computation.1 | convolution fusion | flops 5925240832 | bytes 12845056 | tf_op jit(solution)/shard_map/dot_general | solution.py:59
  496.1 10.8 %convolution_convert_fusion = bf16[2048,1408]{1,0:T(8,128)(2,1)} fusion(bf16[1024,1408]{1,0:T(8,128)(2,1)S(1)} %get-tuple-element.169, bf16[256,2048]{1,0:T(8,128)(2,1)} %collective-permute-done.27, bf16[256,2048]{1,0:T(8,128)(2,1)} %collective-permute-done.26, bf16[256,2048]{1,0:T(8,128)(2,1)} %collective-permute-done.25, ...), kind=kOutput, calls=%fused_computation | convolution fusion | flops 5925240832 | bytes 12845056 | tf_op jit(solution)/shard_map/dot_general | solution.py:59
  519.3 19.6 %collective-permute-done.38 = bf16[256,2048]{1,0:T(8,128)(2,1)S(1)} collective-permute-done((bf16[256,2048]{1,0:T(8,128)(2,1)}, bf16[256,2048]{1,0:T(8,128)(2,1)S(1)}, u32[]{:S(2)}, u32[]{:S(2)}) %collective-permute-start.38) | collective-permute-done | bytes 1048608 | tf_op jit(solution)/shard_map/ppermute | solution.py:379
  546.7 18.6 %convolution_convert_fusion.3.do_ref = bf16[256,4096]{1,0:T(8,128)(2,1)} fusion(bf16[256,2048]{1,0:T(8,128)(2,1)S(1)} %get-tuple-element.233, bf16[4096,2048]{1,0:T(8,128)(2,1)} %bitcast.204), kind=kOutput, calls=%fused_computation.12 | convolution fusion | flops 4296015872 | bytes 19922944 | tf_op jit(solution)/shard_map/dot_general | solution.py:63
  570.1 18.9 %shard_map.205 = (bf16[256,4096]{1,0:T(8,128)(2,1)S(1)}, bf16[2048,512]{1,0:T(8,128)(2,1)S(1)}) custom-call(s32[2]{0:T(128)S(1)} %copy-done.14, bf16[256,4096]{1,0:T(8,128)(2,1)S(1)} %copy-done.9, bf16[256,4096]{1,0:T(8,128)(2,1)S(1)} %copy-done.10, bf16[256,4096]{1,0:T(8,128)(2,1)S(1)} %copy-done.7, f32[16,1,256]{2,1,0:T(1,128)S(1)} %get-tuple-element.171.lse_ref, ...), custom_call_target="tpu_custom_call" | custom-call | flops 1000 | bytes 1000 | tf_op jit(solution)/shard_map/pallas_call | solution.py:239
  590.9 6.0 multiply_reduce_fusion.4
  604.3 11.2 %collective-permute-done.39 = bf16[4,256,512]{2,1,0:T(8,128)(2,1)S(1)} collective-permute-done((bf16[4,256,512]{2,1,0:T(8,128)(2,1)}, bf16[4,256,512]{2,1,0:T(8,128)(2,1)S(1)}, u32[]{:S(2)}, u32[]{:S(2)}) %collective-permute-start.39) | collective-permute-done | bytes 1048608 | tf_op jit(solution)/shard_map/ppermute | solution.py:379
  625.8 9.6 %collective-permute-start.40 = (bf16[256,512]{1,0:T(8,128)(2,1)S(1)}, bf16[256,512]{1,0:T(8,128)(2,1)S(1)}, u32[]{:S(2)}, u32[]{:S(2)}) collective-permute-start(bf16[256,512]{1,0:T(8,128)(2,1)S(1)} %get-tuple-element.289), channel_id=1, source_target_pairs={{0,2},{2,4},{4,6},{6,0},{1,3},{3,5},{5,7},{7,1},{8,10},{10,12},{12... | collective-permute-start | bytes 786440 | tf_op jit(solution)/shard_map/ppermute | solution.py:379
  635.4 6.6 collective-permute-start.41
  643.4 5.0 fusion.25
  648.4 16.2 %collective-permute-done.40 = bf16[256,512]{1,0:T(8,128)(2,1)S(1)} collective-permute-done((bf16[256,512]{1,0:T(8,128)(2,1)S(1)}, bf16[256,512]{1,0:T(8,128)(2,1)S(1)}, u32[]{:S(2)}, u32[]{:S(2)}) %collective-permute-start.40) | collective-permute-done | bytes 262176 | tf_op jit(solution)/shard_map/ppermute | solution.py:379
  664.6 10.9 %collective-permute-done.41 = bf16[256,512]{1,0:T(8,128)(2,1)S(1)} collective-permute-done((bf16[256,512]{1,0:T(8,128)(2,1)S(1)}, bf16[256,512]{1,0:T(8,128)(2,1)S(1)}, u32[]{:S(2)}, u32[]{:S(2)}) %collective-permute-start.41) | collective-permute-done | bytes 262176 | tf_op jit(solution)/shard_map/ppermute | solution.py:379
  684.8 5.0 collective-permute-done.52
  698.3 7.2 fusion.70
  708.0 11.6 %fusion.72 = f32[1024,2048]{1,0:T(8,128)} fusion(bf16[1024,1408]{1,0:T(8,128)(2,1)} %copy-done.70, bf16[1408,2048]{1,0:T(8,128)(2,1)} %all-gather.10.cloned.1.call-done), kind=kOutput, calls=%fused_computation.243 | convolution fusion | flops 5905580032 | bytes 17039360 | tf_op jit(solution)/shard_map/dot_general | solution.py:55
  733.2 15.1 %collective-permute-done.61 = bf16[256,2048]{1,0:T(8,128)(2,1)} collective-permute-done((bf16[256,2048]{1,0:T(8,128)(2,1)}, bf16[256,2048]{1,0:T(8,128)(2,1)}, u32[]{:S(2)}, u32[]{:S(2)}) %collective-permute-start.61) | collective-permute-done | bytes 1048608 | tf_op jit(solution)/shard_map/ppermute | solution.py:379
  753.1 12.3 %collective-permute-done.62 = bf16[256,1408]{1,0:T(8,128)(2,1)S(1)} collective-permute-done((bf16[256,1408]{1,0:T(8,128)(2,1)S(1)}, bf16[256,1408]{1,0:T(8,128)(2,1)S(1)}, u32[]{:S(2)}, u32[]{:S(2)}) %collective-permute-start.62) | collective-permute-done | bytes 720928 | tf_op jit(solution)/shard_map/ppermute | solution.py:379
  767.6 6.1 convert.49
  787.9 17.3 %collective-permute-done.66.refs_4_ = bf16[256,1408]{1,0:T(8,128)(2,1)S(1)} collective-permute-done((bf16[256,1408]{1,0:T(8,128)(2,1)}, bf16[256,1408]{1,0:T(8,128)(2,1)S(1)}, u32[]{:S(2)}, u32[]{:S(2)}) %collective-permute-start.66) | collective-permute-done | bytes 720928 | tf_op jit(solution)/shard_map/ppermute | solution.py:374
  822.9 13.5 %shard_map.206 = (f32[256,11264]{1,0:T(8,128)}, f32[256,1]{1,0:T(8,128)}) custom-call(s32[4]{0:T(128)} %copy-done.58, f32[256,1]{1,0:T(8,128)} %copy.32.refs_1_, bf16[256,11264]{1,0:T(8,128)(2,1)} %refs_2_.2, bf16[256,1408]{1,0:T(8,128)(2,1)} %reduce-scatter.10.cloned.1.call-done.refs_3_, bf16[256,1408]{1,0:T(8,128)(2,1)} %copy-done.41, ...), custom_call_target="tpu_custom_call" | custom-call | flops 1000 | bytes 1000 | tf_op jit(solution)/shard_map/pallas_call | solution.py:310
  844.6 16.0 %collective-permute-done.71 = bf16[256,2048]{1,0:T(8,128)(2,1)S(1)} collective-permute-done((bf16[256,2048]{1,0:T(8,128)(2,1)}, bf16[256,2048]{1,0:T(8,128)(2,1)S(1)}, u32[]{:S(2)}, u32[]{:S(2)}) %collective-permute-start.71) | collective-permute-done | bytes 1048608 | tf_op jit(solution)/shard_map/ppermute | solution.py:379
  (493 shorter events, 302.4 us)
Async XLA Ops:
  7.2 98.5 %all-gather.8.cloned.1.call-start = ((), (), s32[]{:S(2)}) async-start(), calls=%async_computation.6 | async-start | bytes 2621440 | tf_op jit(solution)/shard_map/all_gather | solution.py:464
  9.3 202.0 %all-gather.6.cloned.1.call-start = ((), (), s32[]{:S(2)}) async-start(), calls=%async_computation.5 | async-start | bytes 8650752 | tf_op jit(solution)/shard_map/all_gather | solution.py:633
  14.1 245.9 %all-gather.12.cloned.1.call-start = ((), (), s32[]{:S(2)}) async-start(), calls=%async_computation.8 | async-start | bytes 3604480 | tf_op jit(solution)/shard_map/all_gather | solution.py:464
  18.7 62.0 %collective-permute-start = (bf16[256,2048]{1,0:T(8,128)(2,1)}, bf16[256,2048]{1,0:T(8,128)(2,1)}, u32[]{:S(2)}, u32[]{:S(2)}) collective-permute-start(bf16[256,2048]{1,0:T(8,128)(2,1)} %fusion.4), channel_id=1, source_target_pairs={{16,0},{0,16},{17,1},{1,17},{18,2},{2,18},{19,3},{3,19},{20,4},{4,... | collective-permute-start | bytes 3145736 | tf_op jit(solution)/shard_map/ppermute | solution.py:374
  25.7 37.2 %collective-permute-start.5 = (bf16[256,384]{1,0:T(8,128)(2,1)S(1)}, bf16[256,384]{1,0:T(8,128)(2,1)S(1)}, u32[]{:S(2)}, u32[]{:S(2)}) collective-permute-start(bf16[256,384]{1,0:T(8,128)(2,1)S(1)} %get-tuple-element.236), channel_id=1, source_target_pairs={{6,0},{0,2},{2,4},{4,6},{7,1},{1,3},{3,5},{5,7},{14,8},{8,10},{10,... | collective-permute-start | bytes 589832 | tf_op jit(solution)/shard_map/ppermute | solution.py:374
  77.2 237.6 %all-gather.14.cloned.1.call-start = ((), (), s32[]{:S(2)}) async-start(), calls=%async_computation.9 | async-start | bytes 3604480 | tf_op jit(solution)/shard_map/all_gather | solution.py:464
  105.7 74.1 %collective-permute-start.14 = (bf16[512,2048]{1,0:T(8,128)(2,1)}, bf16[512,2048]{1,0:T(8,128)(2,1)}, u32[]{:S(2)}, u32[]{:S(2)}) collective-permute-start(bf16[512,2048]{1,0:T(8,128)(2,1)} %all-gather.8.cloned.1.call-done), channel_id=1, source_target_pairs={{1,0},{0,1},{3,2},{2,3},{5,4},{4,5},{7,6},{6,7},{9,8},{8,9},{11,10... | collective-permute-start | bytes 6291464 | tf_op jit(solution)/shard_map/ppermute | solution.py:374
  108.1 94.1 %collective-permute-start.15 = (bf16[512,2048]{1,0:T(8,128)(2,1)}, bf16[512,2048]{1,0:T(8,128)(2,1)}, u32[]{:S(2)}, u32[]{:S(2)}) collective-permute-start(bf16[512,2048]{1,0:T(8,128)(2,1)} %all-gather.8.cloned.1.call-done), channel_id=1, source_target_pairs={{16,0},{0,16},{17,1},{1,17},{18,2},{2,18},{19,3},{3,19},{20,4},{4,... | collective-permute-start | bytes 6291464 | tf_op jit(solution)/shard_map/ppermute | solution.py:374
  132.8 29.4 %collective-permute-start.11 = (bf16[256,512]{1,0:T(8,128)(2,1)S(1)}, bf16[256,512]{1,0:T(8,128)(2,1)S(1)}, u32[]{:S(2)}, u32[]{:S(2)}) collective-permute-start(bf16[256,512]{1,0:T(8,128)(2,1)S(1)} %pad_maximum_fusion.12), channel_id=1, source_target_pairs={{4,0},{6,2},{0,4},{2,6},{5,1},{7,3},{1,5},{3,7},{12,8},{14,10},{8,... | collective-permute-start | bytes 786440 | tf_op jit(solution)/shard_map/ppermute | solution.py:374
  135.2 41.2 %collective-permute-start.12 = (bf16[256,512]{1,0:T(8,128)(2,1)S(1)}, bf16[256,512]{1,0:T(8,128)(2,1)S(1)}, u32[]{:S(2)}, u32[]{:S(2)}) collective-permute-start(bf16[256,512]{1,0:T(8,128)(2,1)S(1)} %pad_maximum_fusion.12), channel_id=1, source_target_pairs={{6,0},{0,2},{2,4},{4,6},{7,1},{1,3},{3,5},{5,7},{14,8},{8,10},{10,... | collective-permute-start | bytes 786440 | tf_op jit(solution)/shard_map/ppermute | solution.py:374
  177.5 227.8 %all-gather.10.cloned.1.call-start = ((), (), s32[]{:S(2)}) async-start(), calls=%async_computation.7 | async-start | bytes 7208960 | tf_op jit(solution)/shard_map/all_gather | solution.py:464
  179.8 57.2 %collective-permute-start.16 = (bf16[512,2048]{1,0:T(8,128)(2,1)}, bf16[512,2048]{1,0:T(8,128)(2,1)}, u32[]{:S(2)}, u32[]{:S(2)}) collective-permute-start(bf16[512,2048]{1,0:T(8,128)(2,1)} %collective-permute-done.14), channel_id=1, source_target_pairs={{16,0},{0,16},{17,1},{1,17},{18,2},{2,18},{19,3},{3,19},{20,4},{4,... | collective-permute-start | bytes 6291464 | tf_op jit(solution)/shard_map/ppermute | solution.py:374
  238.2 29.6 %collective-permute-start.18 = (bf16[512,2048]{1,0:T(8,128)(2,1)}, bf16[512,2048]{1,0:T(8,128)(2,1)}, u32[]{:S(2)}, u32[]{:S(2)}) collective-permute-start(bf16[512,2048]{1,0:T(8,128)(2,1)} %collective-permute-done.15), channel_id=1, source_target_pairs={{8,0},{0,8},{9,1},{1,9},{10,2},{2,10},{11,3},{3,11},{12,4},{4,12},... | collective-permute-start | bytes 6291464 | tf_op jit(solution)/shard_map/ppermute | solution.py:374
  239.2 34.3 %collective-permute-start.19 = (bf16[512,2048]{1,0:T(8,128)(2,1)}, bf16[512,2048]{1,0:T(8,128)(2,1)S(1)}, u32[]{:S(2)}, u32[]{:S(2)}) collective-permute-start(bf16[512,2048]{1,0:T(8,128)(2,1)} %collective-permute-done.14), channel_id=1, source_target_pairs={{8,0},{0,8},{9,1},{1,9},{10,2},{2,10},{11,3},{3,11},{12,4},{4,12},... | collective-permute-start | bytes 6291464 | tf_op jit(solution)/shard_map/ppermute | solution.py:374
  241.2 32.6 %collective-permute-start.20 = (bf16[512,2048]{1,0:T(8,128)(2,1)}, bf16[512,2048]{1,0:T(8,128)(2,1)}, u32[]{:S(2)}, u32[]{:S(2)}) collective-permute-start(bf16[512,2048]{1,0:T(8,128)(2,1)} %collective-permute-done.16), channel_id=1, source_target_pairs={{8,0},{0,8},{9,1},{1,9},{10,2},{2,10},{11,3},{3,11},{12,4},{4,12},... | collective-permute-start | bytes 6291464 | tf_op jit(solution)/shard_map/ppermute | solution.py:374
  259.7 470.5 %reduce-scatter.8.cloned.1.call-start = ((), (), s32[]{:S(2)}) async-start(), calls=%async_computation.11 | async-start | bytes 7208960 | tf_op jit(solution)/shard_map/reduce_scatter | solution.py:472
  260.0 94.8 %collective-permute-start.28 = (bf16[1024,1408]{1,0:T(8,128)(2,1)}, bf16[1024,1408]{1,0:T(8,128)(2,1)}, u32[]{:S(2)}, u32[]{:S(2)}) collective-permute-start(bf16[1024,1408]{1,0:T(8,128)(2,1)} %all-gather.12.cloned.1.call-done), channel_id=1, source_target_pairs={{1,0},{0,1},{3,2},{2,3},{5,4},{4,5},{7,6},{6,7},{9,8},{8,9},{11,10... | collective-permute-start | bytes 8650760 | tf_op jit(solution)/shard_map/ppermute | solution.py:374
  287.5 42.5 %collective-permute-start.21 = (bf16[256,2048]{1,0:T(8,128)(2,1)}, bf16[256,2048]{1,0:T(8,128)(2,1)}, u32[]{:S(2)}, u32[]{:S(2)}) collective-permute-start(bf16[256,2048]{1,0:T(8,128)(2,1)} %fusion.24), channel_id=1, source_target_pairs={{16,0},{0,16},{17,1},{1,17},{18,2},{2,18},{19,3},{3,19},{20,4},{4,... | collective-permute-start | bytes 3145736 | tf_op jit(solution)/shard_map/ppermute | solution.py:374
  287.6 46.4 %collective-permute-start.22 = (bf16[256,2048]{1,0:T(8,128)(2,1)}, bf16[256,2048]{1,0:T(8,128)(2,1)}, u32[]{:S(2)}, u32[]{:S(2)}) collective-permute-start(bf16[256,2048]{1,0:T(8,128)(2,1)} %fusion.24), channel_id=1, source_target_pairs={{8,0},{0,8},{9,1},{1,9},{10,2},{2,10},{11,3},{3,11},{12,4},{4,12},... | collective-permute-start | bytes 3145736 | tf_op jit(solution)/shard_map/ppermute | solution.py:374
  289.9 49.2 %collective-permute-start.26 = (bf16[256,2048]{1,0:T(8,128)(2,1)}, bf16[256,2048]{1,0:T(8,128)(2,1)}, u32[]{:S(2)}, u32[]{:S(2)}) collective-permute-start(bf16[256,2048]{1,0:T(8,128)(2,1)} %multiply_convert_fusion.4), channel_id=1, source_target_pairs={{8,0},{0,8},{9,1},{1,9},{10,2},{2,10},{11,3},{3,11},{12,4},{4,12},... | collective-permute-start | bytes 3145736 | tf_op jit(solution)/shard_map/ppermute | solution.py:374
  307.5 31.5 %collective-permute-start.27 = (bf16[256,2048]{1,0:T(8,128)(2,1)}, bf16[256,2048]{1,0:T(8,128)(2,1)}, u32[]{:S(2)}, u32[]{:S(2)}) collective-permute-start(bf16[256,2048]{1,0:T(8,128)(2,1)} %collective-permute-done.25), channel_id=1, source_target_pairs={{8,0},{0,8},{9,1},{1,9},{10,2},{2,10},{11,3},{3,11},{12,4},{4,12},... | collective-permute-start | bytes 3145736 | tf_op jit(solution)/shard_map/ppermute | solution.py:374
  330.0 62.2 %collective-permute-start.29 = (bf16[1024,1408]{1,0:T(8,128)(2,1)}, bf16[1024,1408]{1,0:T(8,128)(2,1)}, u32[]{:S(2)}, u32[]{:S(2)}) collective-permute-start(bf16[1024,1408]{1,0:T(8,128)(2,1)} %all-gather.14.cloned.1.call-done), channel_id=1, source_target_pairs={{1,0},{0,1},{3,2},{2,3},{5,4},{4,5},{7,6},{6,7},{9,8},{8,9},{11,10... | collective-permute-start | bytes 8650760 | tf_op jit(solution)/shard_map/ppermute | solution.py:374
  334.0 71.3 %collective-permute-start.23 = (bf16[256,2048]{1,0:T(8,128)(2,1)}, bf16[256,2048]{1,0:T(8,128)(2,1)}, u32[]{:S(2)}, u32[]{:S(2)}) collective-permute-start(bf16[256,2048]{1,0:T(8,128)(2,1)} %collective-permute-done.21), channel_id=1, source_target_pairs={{8,0},{0,8},{9,1},{1,9},{10,2},{2,10},{11,3},{3,11},{12,4},{4,12},... | collective-permute-start | bytes 3145736 | tf_op jit(solution)/shard_map/ppermute | solution.py:374
  339.1 68.0 %collective-permute-start.33 = (bf16[256,1024]{1,0:T(8,128)(2,1)S(1)}, bf16[256,1024]{1,0:T(8,128)(2,1)}, u32[]{:S(2)}, u32[]{:S(2)}) collective-permute-start(bf16[256,1024]{1,0:T(8,128)(2,1)S(1)} %fusion.32.input_ref), channel_id=1, source_target_pairs={{16,0},{0,16},{17,1},{1,17},{18,2},{2,18},{19,3},{3,19},{20,4},{4,... | collective-permute-start | bytes 1572872 | tf_op jit(solution)/shard_map/ppermute | solution.py:374
  340.3 82.9 %collective-permute-start.34 = (bf16[256,1024]{1,0:T(8,128)(2,1)S(1)}, bf16[256,1024]{1,0:T(8,128)(2,1)}, u32[]{:S(2)}, u32[]{:S(2)}) collective-permute-start(bf16[256,1024]{1,0:T(8,128)(2,1)S(1)} %fusion.32.input_ref), channel_id=1, source_target_pairs={{8,0},{0,8},{9,1},{1,9},{10,2},{2,10},{11,3},{3,11},{12,4},{4,12},... | collective-permute-start | bytes 1572872 | tf_op jit(solution)/shard_map/ppermute | solution.py:374
  354.8 63.6 %collective-permute-start.30 = (bf16[256,1024]{0,1:T(8,128)(2,1)S(1)}, bf16[256,1024]{0,1:T(8,128)(2,1)}, u32[]{:S(2)}, u32[]{:S(2)}) collective-permute-start(bf16[256,1024]{0,1:T(8,128)(2,1)S(1)} %bitcast.235), channel_id=1, source_target_pairs={{16,0},{24,8},{0,16},{8,24},{17,1},{25,9},{1,17},{9,25},{18,2},{26... | collective-permute-start | bytes 1572872 | tf_op jit(solution)/shard_map/ppermute | solution.py:412
  448.3 282.0 %reduce-scatter.6.cloned.1.call-start = ((), (), s32[]{:S(2)}) async-start(), calls=%async_computation.10 | async-start | bytes 7208960 | tf_op jit(solution)/shard_map/reduce_scatter | solution.py:472
  506.9 267.8 %reduce-scatter.10.cloned.1.call-start = ((), (), s32[]{:S(2)}) async-start(), calls=%async_computation.12 | async-start | bytes 3604480 | tf_op jit(solution)/shard_map/reduce_scatter | solution.py:472
  519.1 80.6 %collective-permute-start.46 = (bf16[4,256,1408]{2,1,0:T(8,128)(2,1)}, bf16[4,256,1408]{2,1,0:T(8,128)(2,1)}, u32[]{:S(2)}, u32[]{:S(2)}) collective-permute-start(bf16[4,256,1408]{2,1,0:T(8,128)(2,1)} %dynamic-slice_bitcast_fusion), channel_id=1, source_target_pairs={{0,1},{1,0},{2,3},{3,2},{4,5},{5,4},{6,7},{7,6},{8,9},{9,8},{10,11... | collective-permute-start | bytes 8650760 | tf_op jit(solution)/shard_map/ppermute | solution.py:379
  544.2 54.4 %collective-permute-start.43 = (bf16[256,2048]{1,0:T(8,128)(2,1)S(1)}, bf16[256,2048]{1,0:T(8,128)(2,1)}, u32[]{:S(2)}, u32[]{:S(2)}) collective-permute-start(bf16[256,2048]{1,0:T(8,128)(2,1)S(1)} %get-tuple-element.233), channel_id=1, source_target_pairs={{16,0},{0,16},{17,1},{1,17},{18,2},{2,18},{19,3},{3,19},{20,4},{4,... | collective-permute-start | bytes 3145736 | tf_op jit(solution)/shard_map/ppermute | solution.py:374
  545.4 71.4 %collective-permute-start.44 = (bf16[256,2048]{1,0:T(8,128)(2,1)S(1)}, bf16[256,2048]{1,0:T(8,128)(2,1)}, u32[]{:S(2)}, u32[]{:S(2)}) collective-permute-start(bf16[256,2048]{1,0:T(8,128)(2,1)S(1)} %get-tuple-element.233), channel_id=1, source_target_pairs={{8,0},{0,8},{9,1},{1,9},{10,2},{2,10},{11,3},{3,11},{12,4},{4,12},... | collective-permute-start | bytes 3145736 | tf_op jit(solution)/shard_map/ppermute | solution.py:374
  598.2 37.2 %collective-permute-start.47 = (bf16[256,1024]{1,0:T(8,128)(2,1)}, bf16[256,1024]{1,0:T(8,128)(2,1)}, u32[]{:S(2)}, u32[]{:S(2)}) collective-permute-start(bf16[256,1024]{1,0:T(8,128)(2,1)} %get-tuple-element.254), channel_id=1, source_target_pairs={{16,0},{24,8},{0,16},{8,24},{17,1},{25,9},{1,17},{9,25},{18,2},{26... | collective-permute-start | bytes 1572872 | tf_op jit(solution)/shard_map/ppermute | solution.py:412
  599.7 42.3 %collective-permute-start.48 = (bf16[256,1024]{1,0:T(8,128)(2,1)}, bf16[256,1024]{1,0:T(8,128)(2,1)}, u32[]{:S(2)}, u32[]{:S(2)}) collective-permute-start(bf16[256,1024]{1,0:T(8,128)(2,1)} %get-tuple-element.253), channel_id=1, source_target_pairs={{8,0},{0,8},{24,16},{16,24},{9,1},{1,9},{25,17},{17,25},{10,2},{2,... | collective-permute-start | bytes 1572872 | tf_op jit(solution)/shard_map/ppermute | solution.py:412
  604.2 208.1 %reduce-scatter.14.cloned.1.call-start = ((), (), s32[]{:S(2)}) async-start(), calls=%async_computation.14 | async-start | bytes 2621440 | tf_op jit(solution)/shard_map/reduce_scatter | solution.py:472
  625.8 64.1 %collective-permute-start.53 = (bf16[4,128,2048]{2,1,0:T(8,128)(2,1)}, bf16[4,128,2048]{2,1,0:T(8,128)(2,1)}, u32[]{:S(2)}, u32[]{:S(2)}) collective-permute-start(bf16[4,128,2048]{2,1,0:T(8,128)(2,1)} %get-tuple-element.243), channel_id=1, source_target_pairs={{0,1},{1,0},{2,3},{3,2},{4,5},{5,4},{6,7},{7,6},{8,9},{9,8},{10,11... | collective-permute-start | bytes 6291464 | tf_op jit(solution)/shard_map/ppermute | solution.py:379
  625.8 38.8 %collective-permute-start.40 = (bf16[256,512]{1,0:T(8,128)(2,1)S(1)}, bf16[256,512]{1,0:T(8,128)(2,1)S(1)}, u32[]{:S(2)}, u32[]{:S(2)}) collective-permute-start(bf16[256,512]{1,0:T(8,128)(2,1)S(1)} %get-tuple-element.289), channel_id=1, source_target_pairs={{0,2},{2,4},{4,6},{6,0},{1,3},{3,5},{5,7},{7,1},{8,10},{10,12},{12... | collective-permute-start | bytes 786440 | tf_op jit(solution)/shard_map/ppermute | solution.py:379
  635.4 40.1 %collective-permute-start.41 = (bf16[256,512]{1,0:T(8,128)(2,1)S(1)}, bf16[256,512]{1,0:T(8,128)(2,1)S(1)}, u32[]{:S(2)}, u32[]{:S(2)}) collective-permute-start(bf16[256,512]{1,0:T(8,128)(2,1)S(1)} %get-tuple-element.288), channel_id=1, source_target_pairs={{0,4},{2,6},{4,0},{6,2},{1,5},{3,7},{5,1},{7,3},{8,12},{10,14},{12... | collective-permute-start | bytes 786440 | tf_op jit(solution)/shard_map/ppermute | solution.py:379
  642.0 35.6 %collective-permute-start.42 = (bf16[256,512]{1,0:T(8,128)(2,1)S(1)}, bf16[256,512]{1,0:T(8,128)(2,1)S(1)}, u32[]{:S(2)}, u32[]{:S(2)}) collective-permute-start(bf16[256,512]{1,0:T(8,128)(2,1)S(1)} %get-tuple-element.287), channel_id=1, source_target_pairs={{0,6},{2,0},{4,2},{6,4},{1,7},{3,1},{5,3},{7,5},{8,14},{10,8},{12,... | collective-permute-start | bytes 786440 | tf_op jit(solution)/shard_map/ppermute | solution.py:379
  708.0 165.1 %reduce-scatter.12.cloned.1.call-start = ((), (), s32[]{:S(2)}) async-start(), calls=%async_computation.13 | async-start | bytes 1310720 | tf_op jit(solution)/shard_map/reduce_scatter | solution.py:472
  725.8 41.7 %collective-permute-start.58 = (bf16[4,128,1024]{2,1,0:T(8,128)(2,1)}, bf16[4,128,1024]{2,1,0:T(8,128)(2,1)}, u32[]{:S(2)}, u32[]{:S(2)}) collective-permute-start(bf16[4,128,1024]{2,1,0:T(8,128)(2,1)} %get-tuple-element.249), channel_id=1, source_target_pairs={{0,1},{1,0},{2,3},{3,2},{4,5},{5,4},{6,7},{7,6},{8,9},{9,8},{10,11... | collective-permute-start | bytes 3145736 | tf_op jit(solution)/shard_map/ppermute | solution.py:379
  729.1 54.6 %collective-permute-start.55 = (bf16[256,384]{1,0:T(8,128)(2,1)}, bf16[256,384]{1,0:T(8,128)(2,1)}, u32[]{:S(2)}, u32[]{:S(2)}) collective-permute-start(bf16[256,384]{1,0:T(8,128)(2,1)} %get-tuple-element.292), channel_id=1, source_target_pairs={{0,2},{2,4},{4,6},{6,0},{1,3},{3,5},{5,7},{7,1},{8,10},{10,12},{12... | collective-permute-start | bytes 589832 | tf_op jit(solution)/shard_map/ppermute | solution.py:379
  729.1 58.1 %collective-permute-start.56 = (bf16[256,384]{1,0:T(8,128)(2,1)}, bf16[256,384]{1,0:T(8,128)(2,1)}, u32[]{:S(2)}, u32[]{:S(2)}) collective-permute-start(bf16[256,384]{1,0:T(8,128)(2,1)} %get-tuple-element.291), channel_id=1, source_target_pairs={{0,4},{2,6},{4,0},{6,2},{1,5},{3,7},{5,1},{7,3},{8,12},{10,14},{12... | collective-permute-start | bytes 589832 | tf_op jit(solution)/shard_map/ppermute | solution.py:379
  731.5 55.9 %collective-permute-start.57 = (bf16[256,384]{1,0:T(8,128)(2,1)}, bf16[256,384]{1,0:T(8,128)(2,1)}, u32[]{:S(2)}, u32[]{:S(2)}) collective-permute-start(bf16[256,384]{1,0:T(8,128)(2,1)} %get-tuple-element.290), channel_id=1, source_target_pairs={{0,6},{2,0},{4,2},{6,4},{1,7},{3,1},{5,3},{7,5},{8,14},{10,8},{12,... | collective-permute-start | bytes 589832 | tf_op jit(solution)/shard_map/ppermute | solution.py:379
  773.7 34.2 %collective-permute-start.63 = (bf16[256,1408]{1,0:T(8,128)(2,1)}, bf16[256,1408]{1,0:T(8,128)(2,1)}, u32[]{:S(2)}, u32[]{:S(2)}) collective-permute-start(bf16[256,1408]{1,0:T(8,128)(2,1)} %fusion.29.refs_7_), channel_id=1, source_target_pairs={{16,0},{0,16},{17,1},{1,17},{18,2},{2,18},{19,3},{3,19},{20,4},{4,... | collective-permute-start | bytes 2162696 | tf_op jit(solution)/shard_map/ppermute | solution.py:374
  783.7 29.0 %collective-permute-start.70 = (bf16[256,2048]{1,0:T(8,128)(2,1)}, bf16[256,2048]{1,0:T(8,128)(2,1)}, u32[]{:S(2)}, u32[]{:S(2)}) collective-permute-start(bf16[256,2048]{1,0:T(8,128)(2,1)} %get-tuple-element.240), channel_id=1, source_target_pairs={{0,8},{8,0},{1,9},{9,1},{2,10},{10,2},{3,11},{11,3},{4,12},{12,4},... | collective-permute-start | bytes 3145736 | tf_op jit(solution)/shard_map/ppermute | solution.py:379
  810.6 34.0 %collective-permute-start.69 = (bf16[256,2048]{1,0:T(8,128)(2,1)}, bf16[256,2048]{1,0:T(8,128)(2,1)S(1)}, u32[]{:S(2)}, u32[]{:S(2)}) collective-permute-start(bf16[256,2048]{1,0:T(8,128)(2,1)} %get-tuple-element.239), channel_id=1, source_target_pairs={{0,8},{8,0},{1,9},{9,1},{2,10},{10,2},{3,11},{11,3},{4,12},{12,4},... | collective-permute-start | bytes 3145736 | tf_op jit(solution)/shard_map/ppermute | solution.py:379
  816.0 44.6 %collective-permute-start.71 = (bf16[256,2048]{1,0:T(8,128)(2,1)}, bf16[256,2048]{1,0:T(8,128)(2,1)S(1)}, u32[]{:S(2)}, u32[]{:S(2)}) collective-permute-start(bf16[256,2048]{1,0:T(8,128)(2,1)} %add_convert_fusion.2), channel_id=1, source_target_pairs={{0,16},{16,0},{1,17},{17,1},{2,18},{18,2},{3,19},{19,3},{4,20},{20... | collective-permute-start | bytes 3145736 | tf_op jit(solution)/shard_map/ppermute | solution.py:379
  842.5 30.7 %collective-permute-start.81 = (bf16[128,2048]{1,0:T(8,128)(2,1)}, bf16[128,2048]{1,0:T(8,128)(2,1)}, u32[]{:S(2)}, u32[]{:S(2)}) collective-permute-start(bf16[128,2048]{1,0:T(8,128)(2,1)} %collective-permute-done.79), channel_id=1, source_target_pairs={{8,0},{0,8},{9,1},{1,9},{10,2},{2,10},{11,3},{3,11},{12,4},{4,12},... | collective-permute-start | bytes 1572872 | tf_op jit(solution)/shard_map/ppermute | solution.py:374
  (125 other events, 1814.8 us)
Sparse Core Ops, SparseCore 0:
  10.2 60.5 all-gather.7
  73.6 102.6 all-gather.5
  178.5 59.8 all-gather.11
  240.4 57.8 all-gather.13
  300.3 104.9 all-gather.9
  448.4 102.9 reduce-scatter.7
  553.7 119.8 reduce-scatter.5
  676.5 55.6 reduce-scatter.9
  734.5 49.7 reduce-scatter.13
  787.1 23.7 reduce-scatter.11

commit v5 on v4

--- a/solution.py
+++ b/solution.py
@@ -201,6 +201,7 @@
         at = pl.ds(pl.multiple_of(c * chunk_rows, chunk_rows), chunk_rows)
         keys = kv_ref[at, :HD]
         values = kv_ref[at, HD:]
+        weights = []
         for j in range(STEP_HEADS):
             query = q_ref[:, j * HD : (j + 1) * HD]
             out_grad = do_ref[:, j * HD : (j + 1) * HD]
@@ -208,9 +209,15 @@
             if masked:
                 probs = jnp.where(seen(probs.shape, rows, place_ref[1]), probs, 0.0)
             score_grad = (probs * (dot_last(values, out_grad) - deltas[j])).astype(BF)
-            acc_ref[at, HD:] += matmul(probs.astype(BF), out_grad)
-            acc_ref[at, :HD] += matmul(score_grad, query)
             dqs_ref[j] += contract_rows(score_grad, keys)
+            weights.append((probs.astype(BF), score_grad, out_grad, query))
+        prob_rows, grad_rows, out_grads, queries = zip(*weights)
+        acc_ref[at, HD:] += matmul(
+            jnp.concatenate(prob_rows, axis=1), jnp.concatenate(out_grads, axis=0)
+        )
+        acc_ref[at, :HD] += matmul(
+            jnp.concatenate(grad_rows, axis=1), jnp.concatenate(queries, axis=0)
+        )
 
     @pl.loop(Z - place_ref[0], Z)
     def _(c):

time: 901 us -> 907 us (level)
  waiting for transfers between devices: 323 us -> 308 us
  starting transfers between devices: 95.7 us -> 106 us
    ppermute x22, waiting for transfers between devices: 107 us -> 92.4 us  [to_ahead(): return lax.ppermute(value, axis, [(j, (j + step) % n) for j in range(n)])]
    ppermute x22, starting transfers between devices: 33.2 us -> 43.4 us  [to_ahead(): return lax.ppermute(value, axis, [(j, (j + step) % n) for j in range(n)])]
  transfers between devices with their start and end apart: 95 -> 95, of which waited for: 30 -> 30; matrix products, arithmetic and copies ran while one was open for 39% -> 39% of each run, Pallas kernels for 7% -> 8%
where the time goes in v5:
time: 907 us; the launch traced here: 893 us
  waiting for transfers between devices  308 us (34%)
  matrix products  161 us (18%)
  local copies, waits for them, and re-layouts  127 us (14%)
  starting transfers between devices  106 us (12%)
  other arithmetic  106 us (12%)
  Pallas kernels  68.7 us (8%)
  between operations  16 us (2%)
    ppermute x51, waiting for transfers between devices, from_ahead(): return lax.ppermute(value, axis, [((j + step) % n, j) for j in range(n)])  178 us
    ppermute x22, waiting for transfers between devices, to_ahead(): return lax.ppermute(value, axis, [(j, (j + step) % n) for j in range(n)])  92.4 us
    dot_general x6, matrix products, contract_cols(): lax.dot_general(left, right, (((1,), (1,)), ((), ())), preferred_element_...  68.5 us
    unnamed x178, local copies, waits for them, and re-layouts  51.3 us
    dot_general x5, matrix products, matmul(): return jnp.dot(left, right, preferred_element_type=F32)  48.7 us
    ppermute x51, starting transfers between devices, from_ahead(): return lax.ppermute(value, axis, [((j + step) % n, j) for j in range(n)])  48.2 us
    dot_general x6, matrix products, contract_rows(): lax.dot_general(left, right, (((0,), (0,)), ((), ())), preferred_element_...  44.2 us
    ppermute x22, starting transfers between devices, to_ahead(): return lax.ppermute(value, axis, [(j, (j + step) % n) for j in range(n)])  43.4 us
  transfers between devices with their start and end apart: 95, of which 30 were waited for; matrix products, arithmetic and copies ran while one was open for 39% of the time, Pallas kernels for 8%

profile of v5, /device:TPU:13, one launch (start us, length us, event | category | flops | bytes accessed | tf_op | source)
XLA Modules:
  0.0 893.0 jit_solution(4761724564717721598)
XLA Ops:
  27.8 13.1 %collective-permute-done.3 = bf16[256,384]{1,0:T(8,128)(2,1)S(1)} collective-permute-done((bf16[256,384]{1,0:T(8,128)(2,1)S(1)}, bf16[256,384]{1,0:T(8,128)(2,1)S(1)}, u32[]{:S(2)}, u32[]{:S(2)}) %collective-permute-start.3) | collective-permute-done | bytes 196640 | tf_op jit(solution)/shard_map/ppermute | solution.py:381
  40.9 7.3 collective-permute-done.4
  48.2 14.7 %collective-permute-done.5 = bf16[256,384]{1,0:T(8,128)(2,1)S(1)} collective-permute-done((bf16[256,384]{1,0:T(8,128)(2,1)S(1)}, bf16[256,384]{1,0:T(8,128)(2,1)S(1)}, u32[]{:S(2)}, u32[]{:S(2)}) %collective-permute-start.5) | collective-permute-done | bytes 196640 | tf_op jit(solution)/shard_map/ppermute | solution.py:381
  64.9 12.3 %shard_map.204 = (bf16[256,1408]{1,0:T(8,128)(2,1)}, bf16[256,1408]{1,0:T(8,128)(2,1)}) custom-call(s32[1]{0:T(128)} %bitcast.35.refs_0_, f32[256,1]{1,0:T(8,128)} %copy.32.refs_1_, bf16[256,11264]{1,0:T(8,128)(2,1)} %refs_2_.2), custom_call_target="tpu_custom_call" | custom-call | flops 1000 | bytes 1000 | tf_op jit(solution)/shard_map/pallas_call | solution.py:362
  88.0 6.5 fusion.33
  110.3 17.7 %collective-permute-done.9 = f32[256,384]{1,0:T(8,128)} collective-permute-done((f32[256,384]{1,0:T(8,128)}, f32[256,384]{1,0:T(8,128)}, u32[]{:S(2)}, u32[]{:S(2)}) %collective-permute-start.9) | collective-permute-done | bytes 393248 | tf_op jit(solution)/shard_map/ppermute | solution.py:683
  135.2 20.5 %collective-permute-done.10 = bf16[256,512]{1,0:T(8,128)(2,1)S(1)} collective-permute-done((bf16[256,512]{1,0:T(8,128)(2,1)S(1)}, bf16[256,512]{1,0:T(8,128)(2,1)S(1)}, u32[]{:S(2)}, u32[]{:S(2)}) %collective-permute-start.10) | collective-permute-done | bytes 262176 | tf_op jit(solution)/shard_map/ppermute | solution.py:381
  155.7 6.5 collective-permute-done.11
  162.2 14.2 %collective-permute-done.12 = bf16[256,512]{1,0:T(8,128)(2,1)S(1)} collective-permute-done((bf16[256,512]{1,0:T(8,128)(2,1)S(1)}, bf16[256,512]{1,0:T(8,128)(2,1)S(1)}, u32[]{:S(2)}, u32[]{:S(2)}) %collective-permute-start.12) | collective-permute-done | bytes 262176 | tf_op jit(solution)/shard_map/ppermute | solution.py:381
  182.6 19.5 %collective-permute-done.13 = bf16[4,256,512]{2,1,0:T(8,128)(2,1)} collective-permute-done((bf16[4,256,512]{2,1,0:T(8,128)(2,1)}, bf16[4,256,512]{2,1,0:T(8,128)(2,1)}, u32[]{:S(2)}, u32[]{:S(2)}) %collective-permute-start.13) | collective-permute-done | bytes 1048608 | tf_op jit(solution)/shard_map/ppermute | solution.py:381
  214.5 19.9 %shard_map.203 = (bf16[256,4096]{1,0:T(8,128)(2,1)S(1)}, bf16[256,4096]{1,0:T(8,128)(2,1)S(1)}, f32[16,1,256]{2,1,0:T(1,128)S(1)}) custom-call(s32[2]{0:T(128)S(1)} %copy-done.13, bf16[256,1024]{1,0:T(8,128)(2,1)S(1)} %fusion.32.input_ref, bf16[1024,4096]{1,0:T(8,128)(2,1)} %all-gather.6.cloned.1.call-done.up_ref, f32[256,128]{1,0:T(8,128)S(1)} %copy-done.11, ...), custom_call_target="tpu_custom_call" | custom-call | flops 1000 | bytes 1000 | tf_op jit(solution)/shard_map/pallas_call | solution.py:142
  241.2 15.3 %collective-permute-done.24 = bf16[176,2048]{1,0:T(8,128)(2,1)S(1)} collective-permute-done((bf16[176,2048]{1,0:T(8,128)(2,1)}, bf16[176,2048]{1,0:T(8,128)(2,1)S(1)}, u32[]{:S(2)}, u32[]{:S(2)}) %collective-permute-start.24) | collective-permute-done | bytes 720928 | tf_op jit(solution)/shard_map/ppermute | solution.py:381
  276.4 4.9 multiply_reduce_fusion.2
  289.9 17.7 %collective-permute-done.25 = bf16[256,2048]{1,0:T(8,128)(2,1)} collective-permute-done((bf16[256,2048]{1,0:T(8,128)(2,1)}, bf16[256,2048]{1,0:T(8,128)(2,1)}, u32[]{:S(2)}, u32[]{:S(2)}) %collective-permute-start.25) | collective-permute-done | bytes 1048608 | tf_op jit(solution)/shard_map/ppermute | solution.py:381
  307.5 4.8 collective-permute-start.27
  314.8 15.2 %collective-permute-done.21 = bf16[256,2048]{1,0:T(8,128)(2,1)} collective-permute-done((bf16[256,2048]{1,0:T(8,128)(2,1)}, bf16[256,2048]{1,0:T(8,128)(2,1)}, u32[]{:S(2)}, u32[]{:S(2)}) %collective-permute-start.21) | collective-permute-done | bytes 1048608 | tf_op jit(solution)/shard_map/ppermute | solution.py:381
  343.2 9.2 %constant_dynamic-slice_fusion.11 = (bf16[256,8,1,128]{3,2,1,0:T(2,128)(2,1)S(1)}, bf16[256,8,1,128]{3,2,1,0:T(2,128)(2,1)}, bf16[256,8,1,128]{3,2,1,0:T(2,128)(2,1)}, bf16[256,8,1,128]{3,2,1,0:T(2,128)(2,1)S(1)}) fusion(bf16[256,8,4,128]{3,2,1,0:T(4,128)(2,1)} %reshape.310, s32[]{:T(128)S(6)} %select_n.232, s32[]{:T(128)S(6)} %select_n.233, ...), kind=kLoop, calls=%fused_computation.195 | loop fusion | bytes 4194320 | tf_op jit(solution)/shard_map/jit(dynamic_index_in_dim)/dynamic_slice | solution.py:728
  355.1 5.2 maximum_select_fusion
  360.3 13.2 %fusion.62 = f32[1024,1408]{1,0:T(8,128)} fusion(bf16[2048,1408]{1,0:T(8,128)(2,1)S(1)} %bitcast.211, bf16[256,2048]{1,0:T(8,128)(2,1)} %collective-permute-done.27, bf16[256,2048]{1,0:T(8,128)(2,1)} %collective-permute-done.26, bf16[256,2048]{1,0:T(8,128)(2,1)} %collective-permute-done.25, bf16[256,2048]{1,0:T(8,128)(2,1)} %multiply_convert_fusion.4), kind=kOutput, calls=%fused_computation.234 | convolution fusion | flops 5922357248 | bytes 15728640 | tf_op jit(solution)/shard_map/dot_general | solution.py:55
  379.0 13.2 %collective-permute-done.29 = bf16[1024,1408]{1,0:T(8,128)(2,1)} collective-permute-done((bf16[1024,1408]{1,0:T(8,128)(2,1)}, bf16[1024,1408]{1,0:T(8,128)(2,1)}, u32[]{:S(2)}, u32[]{:S(2)}) %collective-permute-start.29) | collective-permute-done | bytes 2883616 | tf_op jit(solution)/shard_map/ppermute | solution.py:381
  395.5 9.9 %all-gather.10.cloned.1.call-done = bf16[1408,2048]{1,0:T(8,128)(2,1)} async-done(((bf16[352,2048]{1,0:T(8,128)(2,1)}), bf16[1408,2048]{1,0:T(8,128)(2,1)}) %all-gather.10.cloned.1.call-update) | async-done | bytes 5767184 | tf_op jit(solution)/shard_map/all_gather | solution.py:471
  407.1 7.8 maximum_select_fusion.1
  426.0 12.5 %multiply_convert_fusion.2 = (bf16[1024,1408]{1,0:T(8,128)(2,1)S(1)}, f32[1024,1408]{1,0:T(8,128)}) fusion(f32[1024,1408]{1,0:T(8,128)} %fusion.62, bf16[2048,1408]{1,0:T(8,128)(2,1)S(1)} %bitcast.218, bf16[256,2048]{1,0:T(8,128)(2,1)} %collective-permute-done.27, bf16[256,2048]{1,0:T(8,128)(2,1)} %collective-permute-done.26, ...), kind=kOutput, calls=%fused_computation.9 | convolution fusion | flops 5931008000 | bytes 24379392 | tf_op jit(solution)/shard_map/dot_general | solution.py:55
  440.1 8.1 convolution_convert_fusion.2
  448.3 15.6 %multiply_convert_fusion = (bf16[1024,1408]{1,0:T(8,128)(2,1)S(1)}, bf16[1024,1408]{1,0:T(8,128)(2,1)}) fusion(f32[1024,1408]{1,0:T(8,128)} %fusion.62, f32[1024,1408]{1,0:T(8,128)} %get-tuple-element.304, bf16[1024,2048]{1,0:T(8,128)(2,1)} %constant_dynamic-update-slice_fusion.2, bf16[1408,2048]{1,0:T(8,128)(2,1)} %all-gather.10.cloned.1.call-done), kind=kOutput, calls=%fused_computation.7 | convolution fusion | flops 5924323328 | bytes 27262976 | tf_op jit(solution)/shard_map/dot_general | solution.py:63
  463.9 8.5 fusion.71
  472.4 12.6 %fusion.69 = (bf16[1024,2048]{1,0:T(8,128)(2,1)}, f32[1024,2048]{1,0:T(8,128)}) fusion(f32[1024,2048]{1,0:T(8,128)S(1)} %fusion.71, bf16[1024,1408]{1,0:T(8,128)(2,1)S(1)} %get-tuple-element.169, bf16[2048,1408]{1,0:T(8,128)(2,1)} %bitcast.215), kind=kOutput, calls=%fused_computation.240 | convolution fusion | flops 5909774336 | bytes 29622272 | tf_op jit(solution)/shard_map/dot_general | solution.py:63
  485.0 11.0 %convolution_convert_fusion.1 = bf16[2048,1408]{1,0:T(8,128)(2,1)} fusion(bf16[1024,1408]{1,0:T(8,128)(2,1)S(1)} %copy-done.71, bf16[256,2048]{1,0:T(8,128)(2,1)} %collective-permute-done.27, bf16[256,2048]{1,0:T(8,128)(2,1)} %collective-permute-done.26, bf16[256,2048]{1,0:T(8,128)(2,1)} %collective-permute-done.25, bf16[256,2048]{1,0:T(8,128)(2,1)} %multiply_convert_fusion.4), kind=kOutput, calls=%fused_computation.1 | convolution fusion | flops 5925240832 | bytes 12845056 | tf_op jit(solution)/shard_map/dot_general | solution.py:59
  496.1 10.8 %convolution_convert_fusion = bf16[2048,1408]{1,0:T(8,128)(2,1)} fusion(bf16[1024,1408]{1,0:T(8,128)(2,1)S(1)} %get-tuple-element.169, bf16[256,2048]{1,0:T(8,128)(2,1)} %collective-permute-done.27, bf16[256,2048]{1,0:T(8,128)(2,1)} %collective-permute-done.26, bf16[256,2048]{1,0:T(8,128)(2,1)} %collective-permute-done.25, ...), kind=kOutput, calls=%fused_computation | convolution fusion | flops 5925240832 | bytes 12845056 | tf_op jit(solution)/shard_map/dot_general | solution.py:59
  519.3 19.6 %collective-permute-done.38 = bf16[256,2048]{1,0:T(8,128)(2,1)S(1)} collective-permute-done((bf16[256,2048]{1,0:T(8,128)(2,1)}, bf16[256,2048]{1,0:T(8,128)(2,1)S(1)}, u32[]{:S(2)}, u32[]{:S(2)}) %collective-permute-start.38) | collective-permute-done | bytes 1048608 | tf_op jit(solution)/shard_map/ppermute | solution.py:386
  546.7 18.6 %convolution_convert_fusion.3.do_ref = bf16[256,4096]{1,0:T(8,128)(2,1)} fusion(bf16[256,2048]{1,0:T(8,128)(2,1)S(1)} %get-tuple-element.233, bf16[4096,2048]{1,0:T(8,128)(2,1)} %bitcast.204), kind=kOutput, calls=%fused_computation.12 | convolution fusion | flops 4296015872 | bytes 19922944 | tf_op jit(solution)/shard_map/dot_general | solution.py:63
  570.1 23.0 %shard_map.205 = (bf16[256,4096]{1,0:T(8,128)(2,1)S(1)}, bf16[2048,512]{1,0:T(8,128)(2,1)S(1)}) custom-call(s32[2]{0:T(128)S(1)} %copy-done.14, bf16[256,4096]{1,0:T(8,128)(2,1)S(1)} %copy-done.9, bf16[256,4096]{1,0:T(8,128)(2,1)S(1)} %copy-done.10, bf16[256,4096]{1,0:T(8,128)(2,1)S(1)} %copy-done.7, f32[16,1,256]{2,1,0:T(1,128)S(1)} %get-tuple-element.171.lse_ref, ...), custom_call_target="tpu_custom_call" | custom-call | flops 1000 | bytes 1000 | tf_op jit(solution)/shard_map/pallas_call | solution.py:246
  595.0 6.0 multiply_reduce_fusion.4
  608.4 11.2 %collective-permute-done.39 = bf16[4,256,512]{2,1,0:T(8,128)(2,1)S(1)} collective-permute-done((bf16[4,256,512]{2,1,0:T(8,128)(2,1)}, bf16[4,256,512]{2,1,0:T(8,128)(2,1)S(1)}, u32[]{:S(2)}, u32[]{:S(2)}) %collective-permute-start.39) | collective-permute-done | bytes 1048608 | tf_op jit(solution)/shard_map/ppermute | solution.py:386
  630.0 11.3 %collective-permute-start.40 = (bf16[256,512]{1,0:T(8,128)(2,1)S(1)}, bf16[256,512]{1,0:T(8,128)(2,1)S(1)}, u32[]{:S(2)}, u32[]{:S(2)}) collective-permute-start(bf16[256,512]{1,0:T(8,128)(2,1)S(1)} %get-tuple-element.289), channel_id=1, source_target_pairs={{0,2},{2,4},{4,6},{6,0},{1,3},{3,5},{5,7},{7,1},{8,10},{10,12},{12... | collective-permute-start | bytes 786440 | tf_op jit(solution)/shard_map/ppermute | solution.py:386
  641.3 8.3 collective-permute-start.41
  651.0 5.0 fusion.25
  657.7 18.0 %collective-permute-done.41 = bf16[256,512]{1,0:T(8,128)(2,1)S(1)} collective-permute-done((bf16[256,512]{1,0:T(8,128)(2,1)S(1)}, bf16[256,512]{1,0:T(8,128)(2,1)S(1)}, u32[]{:S(2)}, u32[]{:S(2)}) %collective-permute-start.41) | collective-permute-done | bytes 262176 | tf_op jit(solution)/shard_map/ppermute | solution.py:386
  685.1 4.9 collective-permute-done.52
  698.5 7.2 fusion.70
  708.1 11.6 %fusion.72 = f32[1024,2048]{1,0:T(8,128)} fusion(bf16[1024,1408]{1,0:T(8,128)(2,1)} %copy-done.70, bf16[1408,2048]{1,0:T(8,128)(2,1)} %all-gather.10.cloned.1.call-done), kind=kOutput, calls=%fused_computation.243 | convolution fusion | flops 5905580032 | bytes 17039360 | tf_op jit(solution)/shard_map/dot_general | solution.py:55
  729.3 8.0 collective-permute-start.56
  740.3 8.1 collective-permute-done.61
  753.2 12.4 %collective-permute-done.62 = bf16[256,1408]{1,0:T(8,128)(2,1)S(1)} collective-permute-done((bf16[256,1408]{1,0:T(8,128)(2,1)S(1)}, bf16[256,1408]{1,0:T(8,128)(2,1)S(1)}, u32[]{:S(2)}, u32[]{:S(2)}) %collective-permute-start.62) | collective-permute-done | bytes 720928 | tf_op jit(solution)/shard_map/ppermute | solution.py:386
  767.7 6.1 convert.49
  788.1 17.2 %collective-permute-done.66.refs_4_ = bf16[256,1408]{1,0:T(8,128)(2,1)S(1)} collective-permute-done((bf16[256,1408]{1,0:T(8,128)(2,1)}, bf16[256,1408]{1,0:T(8,128)(2,1)S(1)}, u32[]{:S(2)}, u32[]{:S(2)}) %collective-permute-start.66) | collective-permute-done | bytes 720928 | tf_op jit(solution)/shard_map/ppermute | solution.py:381
  823.1 13.5 %shard_map.206 = (f32[256,11264]{1,0:T(8,128)}, f32[256,1]{1,0:T(8,128)}) custom-call(s32[4]{0:T(128)} %copy-done.58, f32[256,1]{1,0:T(8,128)} %copy.32.refs_1_, bf16[256,11264]{1,0:T(8,128)(2,1)} %refs_2_.2, bf16[256,1408]{1,0:T(8,128)(2,1)} %reduce-scatter.10.cloned.1.call-done.refs_3_, bf16[256,1408]{1,0:T(8,128)(2,1)} %copy-done.41, ...), custom_call_target="tpu_custom_call" | custom-call | flops 1000 | bytes 1000 | tf_op jit(solution)/shard_map/pallas_call | solution.py:317
  844.7 16.0 %collective-permute-done.71 = bf16[256,2048]{1,0:T(8,128)(2,1)S(1)} collective-permute-done((bf16[256,2048]{1,0:T(8,128)(2,1)}, bf16[256,2048]{1,0:T(8,128)(2,1)S(1)}, u32[]{:S(2)}, u32[]{:S(2)}) %collective-permute-start.71) | collective-permute-done | bytes 1048608 | tf_op jit(solution)/shard_map/ppermute | solution.py:386
  (493 shorter events, 303.2 us)
Async XLA Ops:
  7.2 98.5 %all-gather.8.cloned.1.call-start = ((), (), s32[]{:S(2)}) async-start(), calls=%async_computation.6 | async-start | bytes 2621440 | tf_op jit(solution)/shard_map/all_gather | solution.py:471
  9.3 202.0 %all-gather.6.cloned.1.call-start = ((), (), s32[]{:S(2)}) async-start(), calls=%async_computation.5 | async-start | bytes 8650752 | tf_op jit(solution)/shard_map/all_gather | solution.py:640
  14.1 245.9 %all-gather.12.cloned.1.call-start = ((), (), s32[]{:S(2)}) async-start(), calls=%async_computation.8 | async-start | bytes 3604480 | tf_op jit(solution)/shard_map/all_gather | solution.py:471
  18.7 62.0 %collective-permute-start = (bf16[256,2048]{1,0:T(8,128)(2,1)}, bf16[256,2048]{1,0:T(8,128)(2,1)}, u32[]{:S(2)}, u32[]{:S(2)}) collective-permute-start(bf16[256,2048]{1,0:T(8,128)(2,1)} %fusion.4), channel_id=1, source_target_pairs={{16,0},{0,16},{17,1},{1,17},{18,2},{2,18},{19,3},{3,19},{20,4},{4,... | collective-permute-start | bytes 3145736 | tf_op jit(solution)/shard_map/ppermute | solution.py:381
  25.7 37.2 %collective-permute-start.5 = (bf16[256,384]{1,0:T(8,128)(2,1)S(1)}, bf16[256,384]{1,0:T(8,128)(2,1)S(1)}, u32[]{:S(2)}, u32[]{:S(2)}) collective-permute-start(bf16[256,384]{1,0:T(8,128)(2,1)S(1)} %get-tuple-element.236), channel_id=1, source_target_pairs={{6,0},{0,2},{2,4},{4,6},{7,1},{1,3},{3,5},{5,7},{14,8},{8,10},{10,... | collective-permute-start | bytes 589832 | tf_op jit(solution)/shard_map/ppermute | solution.py:381
  77.2 237.6 %all-gather.14.cloned.1.call-start = ((), (), s32[]{:S(2)}) async-start(), calls=%async_computation.9 | async-start | bytes 3604480 | tf_op jit(solution)/shard_map/all_gather | solution.py:471
  105.7 74.1 %collective-permute-start.14 = (bf16[512,2048]{1,0:T(8,128)(2,1)}, bf16[512,2048]{1,0:T(8,128)(2,1)}, u32[]{:S(2)}, u32[]{:S(2)}) collective-permute-start(bf16[512,2048]{1,0:T(8,128)(2,1)} %all-gather.8.cloned.1.call-done), channel_id=1, source_target_pairs={{1,0},{0,1},{3,2},{2,3},{5,4},{4,5},{7,6},{6,7},{9,8},{8,9},{11,10... | collective-permute-start | bytes 6291464 | tf_op jit(solution)/shard_map/ppermute | solution.py:381
  108.1 94.1 %collective-permute-start.15 = (bf16[512,2048]{1,0:T(8,128)(2,1)}, bf16[512,2048]{1,0:T(8,128)(2,1)}, u32[]{:S(2)}, u32[]{:S(2)}) collective-permute-start(bf16[512,2048]{1,0:T(8,128)(2,1)} %all-gather.8.cloned.1.call-done), channel_id=1, source_target_pairs={{16,0},{0,16},{17,1},{1,17},{18,2},{2,18},{19,3},{3,19},{20,4},{4,... | collective-permute-start | bytes 6291464 | tf_op jit(solution)/shard_map/ppermute | solution.py:381
  132.8 29.4 %collective-permute-start.11 = (bf16[256,512]{1,0:T(8,128)(2,1)S(1)}, bf16[256,512]{1,0:T(8,128)(2,1)S(1)}, u32[]{:S(2)}, u32[]{:S(2)}) collective-permute-start(bf16[256,512]{1,0:T(8,128)(2,1)S(1)} %pad_maximum_fusion.12), channel_id=1, source_target_pairs={{4,0},{6,2},{0,4},{2,6},{5,1},{7,3},{1,5},{3,7},{12,8},{14,10},{8,... | collective-permute-start | bytes 786440 | tf_op jit(solution)/shard_map/ppermute | solution.py:381
  135.2 41.2 %collective-permute-start.12 = (bf16[256,512]{1,0:T(8,128)(2,1)S(1)}, bf16[256,512]{1,0:T(8,128)(2,1)S(1)}, u32[]{:S(2)}, u32[]{:S(2)}) collective-permute-start(bf16[256,512]{1,0:T(8,128)(2,1)S(1)} %pad_maximum_fusion.12), channel_id=1, source_target_pairs={{6,0},{0,2},{2,4},{4,6},{7,1},{1,3},{3,5},{5,7},{14,8},{8,10},{10,... | collective-permute-start | bytes 786440 | tf_op jit(solution)/shard_map/ppermute | solution.py:381
  177.5 227.8 %all-gather.10.cloned.1.call-start = ((), (), s32[]{:S(2)}) async-start(), calls=%async_computation.7 | async-start | bytes 7208960 | tf_op jit(solution)/shard_map/all_gather | solution.py:471
  179.8 57.2 %collective-permute-start.16 = (bf16[512,2048]{1,0:T(8,128)(2,1)}, bf16[512,2048]{1,0:T(8,128)(2,1)}, u32[]{:S(2)}, u32[]{:S(2)}) collective-permute-start(bf16[512,2048]{1,0:T(8,128)(2,1)} %collective-permute-done.14), channel_id=1, source_target_pairs={{16,0},{0,16},{17,1},{1,17},{18,2},{2,18},{19,3},{3,19},{20,4},{4,... | collective-permute-start | bytes 6291464 | tf_op jit(solution)/shard_map/ppermute | solution.py:381
  237.0 28.9 %collective-permute-start.17 = (bf16[512,2048]{1,0:T(8,128)(2,1)}, bf16[512,2048]{1,0:T(8,128)(2,1)}, u32[]{:S(2)}, u32[]{:S(2)}) collective-permute-start(bf16[512,2048]{1,0:T(8,128)(2,1)} %all-gather.8.cloned.1.call-done), channel_id=1, source_target_pairs={{8,0},{0,8},{9,1},{1,9},{10,2},{2,10},{11,3},{3,11},{12,4},{4,12},... | collective-permute-start | bytes 6291464 | tf_op jit(solution)/shard_map/ppermute | solution.py:381
  238.2 29.6 %collective-permute-start.18 = (bf16[512,2048]{1,0:T(8,128)(2,1)}, bf16[512,2048]{1,0:T(8,128)(2,1)}, u32[]{:S(2)}, u32[]{:S(2)}) collective-permute-start(bf16[512,2048]{1,0:T(8,128)(2,1)} %collective-permute-done.15), channel_id=1, source_target_pairs={{8,0},{0,8},{9,1},{1,9},{10,2},{2,10},{11,3},{3,11},{12,4},{4,12},... | collective-permute-start | bytes 6291464 | tf_op jit(solution)/shard_map/ppermute | solution.py:381
  239.2 34.3 %collective-permute-start.19 = (bf16[512,2048]{1,0:T(8,128)(2,1)}, bf16[512,2048]{1,0:T(8,128)(2,1)S(1)}, u32[]{:S(2)}, u32[]{:S(2)}) collective-permute-start(bf16[512,2048]{1,0:T(8,128)(2,1)} %collective-permute-done.14), channel_id=1, source_target_pairs={{8,0},{0,8},{9,1},{1,9},{10,2},{2,10},{11,3},{3,11},{12,4},{4,12},... | collective-permute-start | bytes 6291464 | tf_op jit(solution)/shard_map/ppermute | solution.py:381
  241.2 32.6 %collective-permute-start.20 = (bf16[512,2048]{1,0:T(8,128)(2,1)}, bf16[512,2048]{1,0:T(8,128)(2,1)}, u32[]{:S(2)}, u32[]{:S(2)}) collective-permute-start(bf16[512,2048]{1,0:T(8,128)(2,1)} %collective-permute-done.16), channel_id=1, source_target_pairs={{8,0},{0,8},{9,1},{1,9},{10,2},{2,10},{11,3},{3,11},{12,4},{4,12},... | collective-permute-start | bytes 6291464 | tf_op jit(solution)/shard_map/ppermute | solution.py:381
  259.7 477.6 %reduce-scatter.8.cloned.1.call-start = ((), (), s32[]{:S(2)}) async-start(), calls=%async_computation.11 | async-start | bytes 7208960 | tf_op jit(solution)/shard_map/reduce_scatter | solution.py:479
  260.0 94.8 %collective-permute-start.28 = (bf16[1024,1408]{1,0:T(8,128)(2,1)}, bf16[1024,1408]{1,0:T(8,128)(2,1)}, u32[]{:S(2)}, u32[]{:S(2)}) collective-permute-start(bf16[1024,1408]{1,0:T(8,128)(2,1)} %all-gather.12.cloned.1.call-done), channel_id=1, source_target_pairs={{1,0},{0,1},{3,2},{2,3},{5,4},{4,5},{7,6},{6,7},{9,8},{8,9},{11,10... | collective-permute-start | bytes 8650760 | tf_op jit(solution)/shard_map/ppermute | solution.py:381
  287.5 42.5 %collective-permute-start.21 = (bf16[256,2048]{1,0:T(8,128)(2,1)}, bf16[256,2048]{1,0:T(8,128)(2,1)}, u32[]{:S(2)}, u32[]{:S(2)}) collective-permute-start(bf16[256,2048]{1,0:T(8,128)(2,1)} %fusion.24), channel_id=1, source_target_pairs={{16,0},{0,16},{17,1},{1,17},{18,2},{2,18},{19,3},{3,19},{20,4},{4,... | collective-permute-start | bytes 3145736 | tf_op jit(solution)/shard_map/ppermute | solution.py:381
  287.6 46.4 %collective-permute-start.22 = (bf16[256,2048]{1,0:T(8,128)(2,1)}, bf16[256,2048]{1,0:T(8,128)(2,1)}, u32[]{:S(2)}, u32[]{:S(2)}) collective-permute-start(bf16[256,2048]{1,0:T(8,128)(2,1)} %fusion.24), channel_id=1, source_target_pairs={{8,0},{0,8},{9,1},{1,9},{10,2},{2,10},{11,3},{3,11},{12,4},{4,12},... | collective-permute-start | bytes 3145736 | tf_op jit(solution)/shard_map/ppermute | solution.py:381
  289.9 49.2 %collective-permute-start.26 = (bf16[256,2048]{1,0:T(8,128)(2,1)}, bf16[256,2048]{1,0:T(8,128)(2,1)}, u32[]{:S(2)}, u32[]{:S(2)}) collective-permute-start(bf16[256,2048]{1,0:T(8,128)(2,1)} %multiply_convert_fusion.4), channel_id=1, source_target_pairs={{8,0},{0,8},{9,1},{1,9},{10,2},{2,10},{11,3},{3,11},{12,4},{4,12},... | collective-permute-start | bytes 3145736 | tf_op jit(solution)/shard_map/ppermute | solution.py:381
  307.5 31.5 %collective-permute-start.27 = (bf16[256,2048]{1,0:T(8,128)(2,1)}, bf16[256,2048]{1,0:T(8,128)(2,1)}, u32[]{:S(2)}, u32[]{:S(2)}) collective-permute-start(bf16[256,2048]{1,0:T(8,128)(2,1)} %collective-permute-done.25), channel_id=1, source_target_pairs={{8,0},{0,8},{9,1},{1,9},{10,2},{2,10},{11,3},{3,11},{12,4},{4,12},... | collective-permute-start | bytes 3145736 | tf_op jit(solution)/shard_map/ppermute | solution.py:381
  330.0 62.2 %collective-permute-start.29 = (bf16[1024,1408]{1,0:T(8,128)(2,1)}, bf16[1024,1408]{1,0:T(8,128)(2,1)}, u32[]{:S(2)}, u32[]{:S(2)}) collective-permute-start(bf16[1024,1408]{1,0:T(8,128)(2,1)} %all-gather.14.cloned.1.call-done), channel_id=1, source_target_pairs={{1,0},{0,1},{3,2},{2,3},{5,4},{4,5},{7,6},{6,7},{9,8},{8,9},{11,10... | collective-permute-start | bytes 8650760 | tf_op jit(solution)/shard_map/ppermute | solution.py:381
  334.0 71.3 %collective-permute-start.23 = (bf16[256,2048]{1,0:T(8,128)(2,1)}, bf16[256,2048]{1,0:T(8,128)(2,1)}, u32[]{:S(2)}, u32[]{:S(2)}) collective-permute-start(bf16[256,2048]{1,0:T(8,128)(2,1)} %collective-permute-done.21), channel_id=1, source_target_pairs={{8,0},{0,8},{9,1},{1,9},{10,2},{2,10},{11,3},{3,11},{12,4},{4,12},... | collective-permute-start | bytes 3145736 | tf_op jit(solution)/shard_map/ppermute | solution.py:381
  339.1 68.0 %collective-permute-start.33 = (bf16[256,1024]{1,0:T(8,128)(2,1)S(1)}, bf16[256,1024]{1,0:T(8,128)(2,1)}, u32[]{:S(2)}, u32[]{:S(2)}) collective-permute-start(bf16[256,1024]{1,0:T(8,128)(2,1)S(1)} %fusion.32.input_ref), channel_id=1, source_target_pairs={{16,0},{0,16},{17,1},{1,17},{18,2},{2,18},{19,3},{3,19},{20,4},{4,... | collective-permute-start | bytes 1572872 | tf_op jit(solution)/shard_map/ppermute | solution.py:381
  340.3 82.9 %collective-permute-start.34 = (bf16[256,1024]{1,0:T(8,128)(2,1)S(1)}, bf16[256,1024]{1,0:T(8,128)(2,1)}, u32[]{:S(2)}, u32[]{:S(2)}) collective-permute-start(bf16[256,1024]{1,0:T(8,128)(2,1)S(1)} %fusion.32.input_ref), channel_id=1, source_target_pairs={{8,0},{0,8},{9,1},{1,9},{10,2},{2,10},{11,3},{3,11},{12,4},{4,12},... | collective-permute-start | bytes 1572872 | tf_op jit(solution)/shard_map/ppermute | solution.py:381
  354.8 63.6 %collective-permute-start.30 = (bf16[256,1024]{0,1:T(8,128)(2,1)S(1)}, bf16[256,1024]{0,1:T(8,128)(2,1)}, u32[]{:S(2)}, u32[]{:S(2)}) collective-permute-start(bf16[256,1024]{0,1:T(8,128)(2,1)S(1)} %bitcast.235), channel_id=1, source_target_pairs={{16,0},{24,8},{0,16},{8,24},{17,1},{25,9},{1,17},{9,25},{18,2},{26... | collective-permute-start | bytes 1572872 | tf_op jit(solution)/shard_map/ppermute | solution.py:419
  448.3 289.0 %reduce-scatter.6.cloned.1.call-start = ((), (), s32[]{:S(2)}) async-start(), calls=%async_computation.10 | async-start | bytes 7208960 | tf_op jit(solution)/shard_map/reduce_scatter | solution.py:479
  506.9 267.9 %reduce-scatter.10.cloned.1.call-start = ((), (), s32[]{:S(2)}) async-start(), calls=%async_computation.12 | async-start | bytes 3604480 | tf_op jit(solution)/shard_map/reduce_scatter | solution.py:479
  519.1 84.7 %collective-permute-start.46 = (bf16[4,256,1408]{2,1,0:T(8,128)(2,1)}, bf16[4,256,1408]{2,1,0:T(8,128)(2,1)}, u32[]{:S(2)}, u32[]{:S(2)}) collective-permute-start(bf16[4,256,1408]{2,1,0:T(8,128)(2,1)} %dynamic-slice_bitcast_fusion), channel_id=1, source_target_pairs={{0,1},{1,0},{2,3},{3,2},{4,5},{5,4},{6,7},{7,6},{8,9},{9,8},{10,11... | collective-permute-start | bytes 8650760 | tf_op jit(solution)/shard_map/ppermute | solution.py:386
  544.2 58.5 %collective-permute-start.43 = (bf16[256,2048]{1,0:T(8,128)(2,1)S(1)}, bf16[256,2048]{1,0:T(8,128)(2,1)}, u32[]{:S(2)}, u32[]{:S(2)}) collective-permute-start(bf16[256,2048]{1,0:T(8,128)(2,1)S(1)} %get-tuple-element.233), channel_id=1, source_target_pairs={{16,0},{0,16},{17,1},{1,17},{18,2},{2,18},{19,3},{3,19},{20,4},{4,... | collective-permute-start | bytes 3145736 | tf_op jit(solution)/shard_map/ppermute | solution.py:381
  545.4 75.5 %collective-permute-start.44 = (bf16[256,2048]{1,0:T(8,128)(2,1)S(1)}, bf16[256,2048]{1,0:T(8,128)(2,1)}, u32[]{:S(2)}, u32[]{:S(2)}) collective-permute-start(bf16[256,2048]{1,0:T(8,128)(2,1)S(1)} %get-tuple-element.233), channel_id=1, source_target_pairs={{8,0},{0,8},{9,1},{1,9},{10,2},{2,10},{11,3},{3,11},{12,4},{4,12},... | collective-permute-start | bytes 3145736 | tf_op jit(solution)/shard_map/ppermute | solution.py:381
  602.3 38.9 %collective-permute-start.47 = (bf16[256,1024]{1,0:T(8,128)(2,1)}, bf16[256,1024]{1,0:T(8,128)(2,1)}, u32[]{:S(2)}, u32[]{:S(2)}) collective-permute-start(bf16[256,1024]{1,0:T(8,128)(2,1)} %get-tuple-element.254), channel_id=1, source_target_pairs={{16,0},{24,8},{0,16},{8,24},{17,1},{25,9},{1,17},{9,25},{18,2},{26... | collective-permute-start | bytes 1572872 | tf_op jit(solution)/shard_map/ppermute | solution.py:419
  603.8 45.8 %collective-permute-start.48 = (bf16[256,1024]{1,0:T(8,128)(2,1)}, bf16[256,1024]{1,0:T(8,128)(2,1)}, u32[]{:S(2)}, u32[]{:S(2)}) collective-permute-start(bf16[256,1024]{1,0:T(8,128)(2,1)} %get-tuple-element.253), channel_id=1, source_target_pairs={{8,0},{0,8},{24,16},{16,24},{9,1},{1,9},{25,17},{17,25},{10,2},{2,... | collective-permute-start | bytes 1572872 | tf_op jit(solution)/shard_map/ppermute | solution.py:419
  608.3 204.2 %reduce-scatter.14.cloned.1.call-start = ((), (), s32[]{:S(2)}) async-start(), calls=%async_computation.14 | async-start | bytes 2621440 | tf_op jit(solution)/shard_map/reduce_scatter | solution.py:479
  619.6 31.5 %collective-permute-start.49 = (bf16[256,1024]{1,0:T(8,128)(2,1)}, bf16[256,1024]{1,0:T(8,128)(2,1)S(1)}, u32[]{:S(2)}, u32[]{:S(2)}) collective-permute-start(bf16[256,1024]{1,0:T(8,128)(2,1)} %get-tuple-element.252), channel_id=1, source_target_pairs={{24,0},{16,8},{8,16},{0,24},{25,1},{17,9},{9,17},{1,25},{26,2},{18... | collective-permute-start | bytes 1572872 | tf_op jit(solution)/shard_map/ppermute | solution.py:419
  629.9 60.1 %collective-permute-start.53 = (bf16[4,128,2048]{2,1,0:T(8,128)(2,1)}, bf16[4,128,2048]{2,1,0:T(8,128)(2,1)}, u32[]{:S(2)}, u32[]{:S(2)}) collective-permute-start(bf16[4,128,2048]{2,1,0:T(8,128)(2,1)} %get-tuple-element.243), channel_id=1, source_target_pairs={{0,1},{1,0},{2,3},{3,2},{4,5},{5,4},{6,7},{7,6},{8,9},{9,8},{10,11... | collective-permute-start | bytes 6291464 | tf_op jit(solution)/shard_map/ppermute | solution.py:386
  641.3 34.4 %collective-permute-start.41 = (bf16[256,512]{1,0:T(8,128)(2,1)S(1)}, bf16[256,512]{1,0:T(8,128)(2,1)S(1)}, u32[]{:S(2)}, u32[]{:S(2)}) collective-permute-start(bf16[256,512]{1,0:T(8,128)(2,1)S(1)} %get-tuple-element.288), channel_id=1, source_target_pairs={{0,4},{2,6},{4,0},{6,2},{1,5},{3,7},{5,1},{7,3},{8,12},{10,14},{12... | collective-permute-start | bytes 786440 | tf_op jit(solution)/shard_map/ppermute | solution.py:386
  708.0 165.2 %reduce-scatter.12.cloned.1.call-start = ((), (), s32[]{:S(2)}) async-start(), calls=%async_computation.13 | async-start | bytes 1310720 | tf_op jit(solution)/shard_map/reduce_scatter | solution.py:479
  726.0 41.7 %collective-permute-start.58 = (bf16[4,128,1024]{2,1,0:T(8,128)(2,1)}, bf16[4,128,1024]{2,1,0:T(8,128)(2,1)}, u32[]{:S(2)}, u32[]{:S(2)}) collective-permute-start(bf16[4,128,1024]{2,1,0:T(8,128)(2,1)} %get-tuple-element.249), channel_id=1, source_target_pairs={{0,1},{1,0},{2,3},{3,2},{4,5},{5,4},{6,7},{7,6},{8,9},{9,8},{10,11... | collective-permute-start | bytes 3145736 | tf_op jit(solution)/shard_map/ppermute | solution.py:386
  729.3 54.7 %collective-permute-start.55 = (bf16[256,384]{1,0:T(8,128)(2,1)}, bf16[256,384]{1,0:T(8,128)(2,1)}, u32[]{:S(2)}, u32[]{:S(2)}) collective-permute-start(bf16[256,384]{1,0:T(8,128)(2,1)} %get-tuple-element.292), channel_id=1, source_target_pairs={{0,2},{2,4},{4,6},{6,0},{1,3},{3,5},{5,7},{7,1},{8,10},{10,12},{12... | collective-permute-start | bytes 589832 | tf_op jit(solution)/shard_map/ppermute | solution.py:386
  729.3 58.2 %collective-permute-start.56 = (bf16[256,384]{1,0:T(8,128)(2,1)}, bf16[256,384]{1,0:T(8,128)(2,1)}, u32[]{:S(2)}, u32[]{:S(2)}) collective-permute-start(bf16[256,384]{1,0:T(8,128)(2,1)} %get-tuple-element.291), channel_id=1, source_target_pairs={{0,4},{2,6},{4,0},{6,2},{1,5},{3,7},{5,1},{7,3},{8,12},{10,14},{12... | collective-permute-start | bytes 589832 | tf_op jit(solution)/shard_map/ppermute | solution.py:386
  738.7 48.9 %collective-permute-start.57 = (bf16[256,384]{1,0:T(8,128)(2,1)}, bf16[256,384]{1,0:T(8,128)(2,1)}, u32[]{:S(2)}, u32[]{:S(2)}) collective-permute-start(bf16[256,384]{1,0:T(8,128)(2,1)} %get-tuple-element.290), channel_id=1, source_target_pairs={{0,6},{2,0},{4,2},{6,4},{1,7},{3,1},{5,3},{7,5},{8,14},{10,8},{12,... | collective-permute-start | bytes 589832 | tf_op jit(solution)/shard_map/ppermute | solution.py:386
  773.8 34.2 %collective-permute-start.63 = (bf16[256,1408]{1,0:T(8,128)(2,1)}, bf16[256,1408]{1,0:T(8,128)(2,1)}, u32[]{:S(2)}, u32[]{:S(2)}) collective-permute-start(bf16[256,1408]{1,0:T(8,128)(2,1)} %fusion.29.refs_7_), channel_id=1, source_target_pairs={{16,0},{0,16},{17,1},{1,17},{18,2},{2,18},{19,3},{3,19},{20,4},{4,... | collective-permute-start | bytes 2162696 | tf_op jit(solution)/shard_map/ppermute | solution.py:381
  784.0 29.0 %collective-permute-start.70 = (bf16[256,2048]{1,0:T(8,128)(2,1)}, bf16[256,2048]{1,0:T(8,128)(2,1)}, u32[]{:S(2)}, u32[]{:S(2)}) collective-permute-start(bf16[256,2048]{1,0:T(8,128)(2,1)} %get-tuple-element.240), channel_id=1, source_target_pairs={{0,8},{8,0},{1,9},{9,1},{2,10},{10,2},{3,11},{11,3},{4,12},{12,4},... | collective-permute-start | bytes 3145736 | tf_op jit(solution)/shard_map/ppermute | solution.py:386
  810.8 34.0 %collective-permute-start.69 = (bf16[256,2048]{1,0:T(8,128)(2,1)}, bf16[256,2048]{1,0:T(8,128)(2,1)S(1)}, u32[]{:S(2)}, u32[]{:S(2)}) collective-permute-start(bf16[256,2048]{1,0:T(8,128)(2,1)} %get-tuple-element.239), channel_id=1, source_target_pairs={{0,8},{8,0},{1,9},{9,1},{2,10},{10,2},{3,11},{11,3},{4,12},{12,4},... | collective-permute-start | bytes 3145736 | tf_op jit(solution)/shard_map/ppermute | solution.py:386
  816.1 44.6 %collective-permute-start.71 = (bf16[256,2048]{1,0:T(8,128)(2,1)}, bf16[256,2048]{1,0:T(8,128)(2,1)S(1)}, u32[]{:S(2)}, u32[]{:S(2)}) collective-permute-start(bf16[256,2048]{1,0:T(8,128)(2,1)} %add_convert_fusion.2), channel_id=1, source_target_pairs={{0,16},{16,0},{1,17},{17,1},{2,18},{18,2},{3,19},{19,3},{4,20},{20... | collective-permute-start | bytes 3145736 | tf_op jit(solution)/shard_map/ppermute | solution.py:386
  842.6 30.7 %collective-permute-start.81 = (bf16[128,2048]{1,0:T(8,128)(2,1)}, bf16[128,2048]{1,0:T(8,128)(2,1)}, u32[]{:S(2)}, u32[]{:S(2)}) collective-permute-start(bf16[128,2048]{1,0:T(8,128)(2,1)} %collective-permute-done.79), channel_id=1, source_target_pairs={{8,0},{0,8},{9,1},{1,9},{10,2},{2,10},{11,3},{3,11},{12,4},{4,12},... | collective-permute-start | bytes 1572872 | tf_op jit(solution)/shard_map/ppermute | solution.py:381
  (125 other events, 1777.2 us)
Sparse Core Ops, SparseCore 0:
  10.2 60.5 all-gather.7
  73.6 102.6 all-gather.5
  178.5 59.8 all-gather.11
  240.4 57.8 all-gather.13
  300.3 104.9 all-gather.9
  448.4 102.9 reduce-scatter.7
  553.7 115.9 reduce-scatter.5
  672.6 56.0 reduce-scatter.9
  731.0 59.3 reduce-scatter.13
  793.2 23.9 reduce-scatter.11
